TPU v7x, 32 devices: a whole 2x2x4 slice. The times are simulated.
32 devices in a mesh: dp: 8 (over z, x), mem: 4 (over y, core).
Axes of the slice: x: 2, y: 2, z: 4, core: 2. Of those that a mesh axis runs over, the one named last changes fastest.
Arguments:
- target_in: bfloat16 [16384, 512], P(('dp', 'mem')), may hold values from -6 to 6
- memory: bfloat16 [16384, 512], P(('dp', 'mem')), may hold values from -6 to 6
- out_grad: bfloat16 [16384, 512], P(('dp', 'mem')), may hold values from -6 to 6
- self_query: bfloat16 [512, 512], P(('dp', 'mem')), may hold values from -0.25 to 0.25
- self_key: bfloat16 [512, 512], P(('dp', 'mem')), may hold values from -0.25 to 0.25
- self_value: bfloat16 [512, 512], P(('dp', 'mem')), may hold values from -0.25 to 0.25
- self_out: bfloat16 [512, 512], P(('dp', 'mem')), may hold values from -0.75 to 0.75
- cross_query: bfloat16 [512, 512], P(('dp', 'mem')), may hold values from -0.25 to 0.25
- cross_key: bfloat16 [512, 512], P(('dp', 'mem')), may hold values from -0.25 to 0.25
- cross_value: bfloat16 [512, 512], P(('dp', 'mem')), may hold values from -0.25 to 0.25
- cross_out: bfloat16 [512, 512], P(('dp', 'mem')), may hold values from -0.75 to 0.75
- ffn_in: bfloat16 [512, 2048], P(('dp', 'mem')), may hold values from -0.25 to 0.25
- ffn_out: bfloat16 [2048, 512], P(('dp', 'mem')), may hold values from -0.125 to 0.125
- attn_gain: bfloat16 [512], P(('dp', 'mem')), may hold values from 0.5 to 1.5
- attn_shift: bfloat16 [512], P(('dp', 'mem')), may hold values from -3 to 3
- cross_gain: bfloat16 [512], P(('dp', 'mem')), may hold values from 0.5 to 1.5
- cross_shift: bfloat16 [512], P(('dp', 'mem')), may hold values from -3 to 3
- ffn_gain: bfloat16 [512], P(('dp', 'mem')), may hold values from 0.5 to 1.5
- ffn_shift: bfloat16 [512], P(('dp', 'mem')), may hold values from -3 to 3
- tgt_lens: int32 [8, 64], P('dp'), may hold values from 1 to 256, as said below
- src_lens: int32 [8, 64], P('dp'), may hold values from 1 to 112, as said below
- src_offsets: int32 [8, 64], P('dp'), may hold values from 0 to 1936, as said below
Outputs:
- layer_out: bfloat16 [16384, 512], P(('dp', 'mem'))
- target_grad: float32 [16384, 512], P(('dp', 'mem'))
- memory_grad: float32 [16384, 512], P(('dp', 'mem'))
- self_query_grad: float32 [512, 512], P(('dp', 'mem'))
- self_key_grad: float32 [512, 512], P(('dp', 'mem'))
- self_value_grad: float32 [512, 512], P(('dp', 'mem'))
- self_out_grad: float32 [512, 512], P(('dp', 'mem'))
- cross_query_grad: float32 [512, 512], P(('dp', 'mem'))
- cross_key_grad: float32 [512, 512], P(('dp', 'mem'))
- cross_value_grad: float32 [512, 512], P(('dp', 'mem'))
- cross_out_grad: float32 [512, 512], P(('dp', 'mem'))
- ffn_in_grad: float32 [512, 2048], P(('dp', 'mem'))
- ffn_out_grad: float32 [2048, 512], P(('dp', 'mem'))
- attn_gain_grad: float32 [512], P(('dp', 'mem'))
- attn_shift_grad: float32 [512], P(('dp', 'mem'))
- cross_gain_grad: float32 [512], P(('dp', 'mem'))
- cross_shift_grad: float32 [512], P(('dp', 'mem'))
- ffn_gain_grad: float32 [512], P(('dp', 'mem'))
- ffn_shift_grad: float32 [512], P(('dp', 'mem'))
Inputs may be any that keep to these rules, and one draw needn't show every extreme that they name: `tgt_lens`: the 16 entries of one device fill its 512 target rows exactly; every device has a sentence of 256 rows. `src_lens`: the source lengths of a group sum to at most 2048. The source rows [src_offsets, src_offsets + src_lens) of a group's sentences are disjoint and lie within the group's 2048 source rows, in no particular order.
All inputs are finite; a program needn't handle non-finite values.
Results may differ from a plain program's by a relative error of at most 0.03.
Values may be sent and summed in bfloat16 or wider, within the bound.
A program may use at most 128 MiB of HBM per device.

v0:
```python
import jax
import jax.numpy as jnp
from jax import lax
from jax.sharding import PartitionSpec as P

HEADS = 8
HEAD = 64


eps_norm = 1e-05
score_scale = 0.125


def layer_norm(values, gain, shift):
    centre = values - jnp.mean(values, axis=-1, keepdims=True)
    spread = jnp.mean(centre * centre, axis=-1, keepdims=True)
    return centre * lax.rsqrt(spread + eps_norm) * gain + shift


def head_split(values):
    return values.reshape(values.shape[0], HEADS, HEAD)


def matmul(left, right):
    return jnp.dot(left, right, preferred_element_type=jnp.float32)


def left_grad(inputs, grads):
    return jnp.einsum("ra,rb->ab", inputs, grads, preferred_element_type=jnp.float32)


def back_through(grads, weight):
    return jnp.einsum("rb,ab->ra", grads, weight, preferred_element_type=jnp.float32)


def row_pick(table, member):
    return lax.dynamic_index_in_dim(table, member, 0, keepdims=False)


def exp_scores(q_block, keys, low_block, high_block, key_base):
    raw_scores = (
        jnp.einsum(
            "qhd,khd->hqk",
            head_split(q_block),
            head_split(keys),
            preferred_element_type=jnp.float32,
        )
        * score_scale
    )
    position = key_base + lax.broadcasted_iota(jnp.int32, (q_block.shape[0], keys.shape[0]), 1)
    allowed = (position >= low_block[:, None]) & (position < high_block[:, None])
    return jnp.where(allowed[None], jnp.exp(raw_scores), 0.0)


def attend(queries, keys, values, low_edge, high_edge, key_base):
    row_count = queries.shape[0]
    block_rows = min(512, row_count)
    blocks = row_count // block_rows
    value_heads = head_split(values)

    def one_block(pieces):
        q_block, low_block, high_block = pieces
        expo_val = exp_scores(q_block, keys, low_block, high_block, key_base)
        numerator = jnp.einsum(
            "hqk,khd->qhd",
            expo_val.astype(jnp.bfloat16),
            value_heads,
            preferred_element_type=jnp.float32,
        )
        return (numerator.reshape(block_rows, -1), jnp.sum(expo_val, axis=2).T)

    numerator, totals = lax.map(
        one_block,
        (
            queries.reshape(blocks, block_rows, -1),
            low_edge.reshape(blocks, block_rows),
            high_edge.reshape(blocks, block_rows),
        ),
    )
    return (numerator.reshape(row_count, -1), totals.reshape(row_count, -1))


def divide_heads(numerator, totals):
    return (head_split(numerator) / totals[:, :, None]).reshape(numerator.shape[0], -1)


def flow_terms(upstream, output, totals):
    upstream_f = head_split(upstream.astype(jnp.float32))
    numer_grad = (
        (upstream_f / totals[:, :, None]).astype(jnp.bfloat16).reshape(upstream.shape[0], -1)
    )
    correction = -jnp.sum(upstream_f * head_split(output), axis=2) / totals
    return (numer_grad, correction)


def attend_back(queries, keys, values, low_edge, high_edge, key_base, numer_grad, correction):
    row_count = queries.shape[0]
    block_rows = min(512, row_count)
    blocks = row_count // block_rows
    key_heads = head_split(keys)
    value_heads = head_split(values)

    def one_block(carry, pieces):
        key_grad, value_grad = carry
        q_block, low_block, high_block, grad_block, corr_block = pieces
        expo_val = exp_scores(q_block, keys, low_block, high_block, key_base)
        flow_grad = (
            jnp.einsum("qhd,khd->hqk", grad_block, value_heads, preferred_element_type=jnp.float32)
            + corr_block.T[:, :, None]
        )
        score_grad = (expo_val * flow_grad).astype(jnp.bfloat16)
        query_grad = (
            jnp.einsum("hqk,khd->qhd", score_grad, key_heads, preferred_element_type=jnp.float32)
            * score_scale
        )
        key_grad = (
            key_grad
            + jnp.einsum(
                "hqk,qhd->khd", score_grad, head_split(q_block), preferred_element_type=jnp.float32
            )
            * score_scale
        )
        value_grad = value_grad + jnp.einsum(
            "hqk,qhd->khd",
            expo_val.astype(jnp.bfloat16),
            grad_block,
            preferred_element_type=jnp.float32,
        )
        return ((key_grad, value_grad), query_grad.reshape(block_rows, -1))

    empty = jnp.zeros((keys.shape[0], HEADS, HEAD), jnp.float32)
    carried, query_grad = lax.scan(
        one_block,
        (empty, empty),
        (
            queries.reshape(blocks, block_rows, -1),
            low_edge.reshape(blocks, block_rows),
            high_edge.reshape(blocks, block_rows),
            numer_grad.reshape(blocks, block_rows, HEADS, HEAD),
            correction.reshape(blocks, block_rows, HEADS),
        ),
    )
    return (
        query_grad.reshape(row_count, -1),
        carried[0].reshape(keys.shape[0], -1),
        carried[1].reshape(keys.shape[0], -1),
    )


def local(
    target_in,
    memory,
    out_grad,
    self_query,
    self_key,
    self_value,
    self_out,
    cross_query,
    cross_key,
    cross_value,
    cross_out,
    ffn_in,
    ffn_out,
    attn_gain,
    attn_shift,
    cross_gain,
    cross_shift,
    ffn_gain,
    ffn_shift,
    tgt_lens,
    src_lens,
    src_offsets,
):
    gathered = (
        lax.all_gather(self_query, ("dp", "mem"), axis=0, tiled=True),
        lax.all_gather(self_key, ("dp", "mem"), axis=0, tiled=True),
        lax.all_gather(self_value, ("dp", "mem"), axis=0, tiled=True),
        lax.all_gather(self_out, ("dp", "mem"), axis=0, tiled=True),
        lax.all_gather(cross_query, ("dp", "mem"), axis=0, tiled=True),
        lax.all_gather(cross_key, ("dp", "mem"), axis=0, tiled=True),
        lax.all_gather(cross_value, ("dp", "mem"), axis=0, tiled=True),
        lax.all_gather(cross_out, ("dp", "mem"), axis=0, tiled=True),
        lax.all_gather(ffn_in, ("dp", "mem"), axis=0, tiled=True),
        lax.all_gather(ffn_out, ("dp", "mem"), axis=0, tiled=True),
        lax.all_gather(attn_gain, ("dp", "mem"), axis=0, tiled=True),
        lax.all_gather(attn_shift, ("dp", "mem"), axis=0, tiled=True),
        lax.all_gather(cross_gain, ("dp", "mem"), axis=0, tiled=True),
        lax.all_gather(cross_shift, ("dp", "mem"), axis=0, tiled=True),
        lax.all_gather(ffn_gain, ("dp", "mem"), axis=0, tiled=True),
        lax.all_gather(ffn_shift, ("dp", "mem"), axis=0, tiled=True),
    )
    (
        query_self,
        key_self,
        value_self,
        out_self,
        query_cross,
        key_cross,
        value_cross,
        out_cross,
        ffn_first,
        ffn_second,
    ) = gathered[:10]
    gain_attn, shift_attn, gain_cross, shift_cross, gain_ffn, shift_ffn = [
        param.astype(jnp.float32) for param in gathered[10:]
    ]
    member = lax.axis_index("mem")
    groups = lax.axis_size("mem")
    row_count = target_in.shape[0]
    src_rows = memory.shape[0]
    per_device = tgt_lens.shape[1] // groups
    lengths = tgt_lens[0].reshape(groups, per_device)
    starts = jnp.cumsum(lengths, axis=1) - lengths
    position = lax.broadcasted_iota(jnp.int32, (groups, row_count, per_device), 1)
    sentence_of = jnp.sum((position >= starts[:, None, :]).astype(jnp.int32), axis=2) - 1
    picker = sentence_of[:, :, None] == lax.broadcasted_iota(
        jnp.int32, (groups, row_count, per_device), 2
    )
    self_low_all = jnp.sum(jnp.where(picker, starts[:, None, :], 0), axis=2)
    cross_low_all = jnp.sum(
        jnp.where(picker, src_offsets[0].reshape(groups, per_device)[:, None, :], 0), axis=2
    )
    cross_high_all = cross_low_all + jnp.sum(
        jnp.where(picker, src_lens[0].reshape(groups, per_device)[:, None, :], 0), axis=2
    )
    self_low = row_pick(self_low_all, member)
    self_high = lax.iota(jnp.int32, row_count) + 1
    group_low = cross_low_all.reshape(-1)
    group_high = cross_high_all.reshape(-1)
    queries_self = matmul(target_in, query_self).astype(jnp.bfloat16)
    keys_self = matmul(target_in, key_self).astype(jnp.bfloat16)
    values_self = matmul(target_in, value_self).astype(jnp.bfloat16)
    numer_self, totals_self = attend(queries_self, keys_self, values_self, self_low, self_high, 0)
    out_self_f = divide_heads(numer_self, totals_self)
    o_self = out_self_f.astype(jnp.bfloat16)
    after_self, pull_self = jax.vjp(
        layer_norm, target_in.astype(jnp.float32) + matmul(o_self, out_self), gain_attn, shift_attn
    )
    after_self_b = after_self.astype(jnp.bfloat16)
    queries_cross = matmul(after_self_b, query_cross).astype(jnp.bfloat16)
    keys_cross = matmul(memory, key_cross).astype(jnp.bfloat16)
    values_cross = matmul(memory, value_cross).astype(jnp.bfloat16)
    group_queries = lax.all_gather(queries_cross, "mem", axis=0, tiled=True)
    numer_part, totals_part = attend(
        group_queries, keys_cross, values_cross, group_low, group_high, member * src_rows
    )
    numer_cross, totals_cross = lax.psum((numer_part, totals_part), "mem")
    group_out = divide_heads(numer_cross, totals_cross)
    out_cross_f = lax.dynamic_slice_in_dim(group_out, member * row_count, row_count, 0)
    o_cross = out_cross_f.astype(jnp.bfloat16)
    after_cross, pull_cross = jax.vjp(
        layer_norm, after_self + matmul(o_cross, out_cross), gain_cross, shift_cross
    )
    after_cross_b = after_cross.astype(jnp.bfloat16)
    hidden = matmul(after_cross_b, ffn_first)
    activated, pull_silu = jax.vjp(jax.nn.silu, hidden)
    act_b = activated.astype(jnp.bfloat16)
    layer_final, pull_ffn = jax.vjp(
        layer_norm, after_cross + matmul(act_b, ffn_second), gain_ffn, shift_ffn
    )
    layer_out = layer_final.astype(jnp.bfloat16)
    d_pre_out, g_gain_ffn, g_shift_ffn = pull_ffn(out_grad.astype(jnp.float32))
    d_branch = d_pre_out.astype(jnp.bfloat16)
    g_ffn_second = left_grad(act_b, d_branch)
    d_hidden = pull_silu(back_through(d_branch, ffn_second))[0].astype(jnp.bfloat16)
    g_ffn_first = left_grad(after_cross_b, d_hidden)
    d_after_cross = d_pre_out + back_through(d_hidden, ffn_first)
    d_pre_cross, g_gain_cross, g_shift_cross = pull_cross(d_after_cross)
    d_cross_branch = d_pre_cross.astype(jnp.bfloat16)
    g_out_cross = left_grad(o_cross, d_cross_branch)
    d_o_cross = back_through(d_cross_branch, out_cross).astype(jnp.bfloat16)
    group_grads = lax.all_gather(d_o_cross, "mem", axis=0, tiled=True)
    group_flow, group_corr = flow_terms(group_grads, group_out, totals_cross)
    query_part, key_grad_c, value_grad_c = attend_back(
        group_queries,
        keys_cross,
        values_cross,
        group_low,
        group_high,
        member * src_rows,
        group_flow,
        group_corr,
    )
    query_grad_c = lax.psum_scatter(
        query_part.astype(jnp.bfloat16), "mem", scatter_dimension=0, tiled=True
    )
    dk_cross = key_grad_c.astype(jnp.bfloat16)
    dv_cross = value_grad_c.astype(jnp.bfloat16)
    g_query_cross = left_grad(after_self_b, query_grad_c)
    g_key_cross = left_grad(memory, dk_cross)
    g_value_cross = left_grad(memory, dv_cross)
    memory_grad = back_through(dk_cross, key_cross) + back_through(dv_cross, value_cross)
    d_after_self = d_pre_cross + back_through(query_grad_c, query_cross)
    d_pre_self, g_gain_attn, g_shift_attn = pull_self(d_after_self)
    d_self_branch = d_pre_self.astype(jnp.bfloat16)
    g_out_self = left_grad(o_self, d_self_branch)
    d_o_self = back_through(d_self_branch, out_self).astype(jnp.bfloat16)
    self_flow, self_corr = flow_terms(d_o_self, out_self_f, totals_self)
    query_grad_s, key_grad_s, value_grad_s = attend_back(
        queries_self, keys_self, values_self, self_low, self_high, 0, self_flow, self_corr
    )
    dq_self = query_grad_s.astype(jnp.bfloat16)
    dk_self = key_grad_s.astype(jnp.bfloat16)
    dv_self = value_grad_s.astype(jnp.bfloat16)
    g_query_self = left_grad(target_in, dq_self)
    g_key_self = left_grad(target_in, dk_self)
    g_value_self = left_grad(target_in, dv_self)
    target_grad = (
        d_pre_self
        + back_through(dq_self, query_self)
        + back_through(dk_self, key_self)
        + back_through(dv_self, value_self)
    )
    summed = (
        lax.psum_scatter(g_query_self, ("dp", "mem"), scatter_dimension=0, tiled=True),
        lax.psum_scatter(g_key_self, ("dp", "mem"), scatter_dimension=0, tiled=True),
        lax.psum_scatter(g_value_self, ("dp", "mem"), scatter_dimension=0, tiled=True),
        lax.psum_scatter(g_out_self, ("dp", "mem"), scatter_dimension=0, tiled=True),
        lax.psum_scatter(g_query_cross, ("dp", "mem"), scatter_dimension=0, tiled=True),
        lax.psum_scatter(g_key_cross, ("dp", "mem"), scatter_dimension=0, tiled=True),
        lax.psum_scatter(g_value_cross, ("dp", "mem"), scatter_dimension=0, tiled=True),
        lax.psum_scatter(g_out_cross, ("dp", "mem"), scatter_dimension=0, tiled=True),
        lax.psum_scatter(g_ffn_first, ("dp", "mem"), scatter_dimension=0, tiled=True),
        lax.psum_scatter(g_ffn_second, ("dp", "mem"), scatter_dimension=0, tiled=True),
        lax.psum_scatter(g_gain_attn, ("dp", "mem"), scatter_dimension=0, tiled=True),
        lax.psum_scatter(g_shift_attn, ("dp", "mem"), scatter_dimension=0, tiled=True),
        lax.psum_scatter(g_gain_cross, ("dp", "mem"), scatter_dimension=0, tiled=True),
        lax.psum_scatter(g_shift_cross, ("dp", "mem"), scatter_dimension=0, tiled=True),
        lax.psum_scatter(g_gain_ffn, ("dp", "mem"), scatter_dimension=0, tiled=True),
        lax.psum_scatter(g_shift_ffn, ("dp", "mem"), scatter_dimension=0, tiled=True),
    )
    return (layer_out, target_grad, memory_grad) + tuple(summed)


def solution(mesh):
    in_specs = (
        P(("dp", "mem"), None),
        P(("dp", "mem"), None),
        P(("dp", "mem"), None),
        P(("dp", "mem"), None),
        P(("dp", "mem"), None),
        P(("dp", "mem"), None),
        P(("dp", "mem"), None),
        P(("dp", "mem"), None),
        P(("dp", "mem"), None),
        P(("dp", "mem"), None),
        P(("dp", "mem"), None),
        P(("dp", "mem"), None),
        P(("dp", "mem"), None),
        P(("dp", "mem")),
        P(("dp", "mem")),
        P(("dp", "mem")),
        P(("dp", "mem")),
        P(("dp", "mem")),
        P(("dp", "mem")),
        P("dp", None),
        P("dp", None),
        P("dp", None),
    )
    out_specs = (
        P(("dp", "mem"), None),
        P(("dp", "mem"), None),
        P(("dp", "mem"), None),
        P(("dp", "mem"), None),
        P(("dp", "mem"), None),
        P(("dp", "mem"), None),
        P(("dp", "mem"), None),
        P(("dp", "mem"), None),
        P(("dp", "mem"), None),
        P(("dp", "mem"), None),
        P(("dp", "mem"), None),
        P(("dp", "mem"), None),
        P(("dp", "mem"), None),
        P(("dp", "mem")),
        P(("dp", "mem")),
        P(("dp", "mem")),
        P(("dp", "mem")),
        P(("dp", "mem")),
        P(("dp", "mem")),
    )
    return jax.shard_map(local, mesh=mesh, in_specs=in_specs, out_specs=out_specs, check_vma=False)
```

profile of v0, /device:TPU:0, one launch (start us, length us, event | category | flops | bytes accessed | tf_op | source)
XLA Modules:
  0.0 2035.2 jit_solution(13773584144659297796)
XLA Ops:
  17.7 42.1 %all-reduce.14 = (bf16[512]{0:T(512)(128)(2,1)S(1)}, bf16[512]{0:T(512)(128)(2,1)S(1)}, bf16[512]{0:T(512)(128)(2,1)S(1)}, bf16[512]{0:T(512)(128)(2,1)S(1)}, bf...) all-reduce(bf16[512]{0:T(512)(128)(2,1)S(1)} %dynamic-update-slice., ...), channel_id=1, replica_groups=mesh['dp'=8,'mem'=4] {'dp','mem'}, use_global_device_ids=true, to_apply=%add.1 | all-reduce | flops 3072 | bytes 12288
  60.4 41.9 %all_gather.55 = bf16[512,512]{1,0:T(8,128)(2,1)S(1)} all-gather(bf16[16,512]{1,0:T(8,128)(2,1)} %param.29), channel_id=1, replica_groups=mesh['dp'=8,'mem'=4] {'dp','mem'}, dimensions={0}, use_global_device_ids=true | all-gather | bytes 540672 | tf_op jit(solution)/shard_map/all_gather | solution.py:175
  102.2 38.3 %all_gather.56 = bf16[512,512]{1,0:T(8,128)(2,1)S(1)} all-gather(bf16[16,512]{1,0:T(8,128)(2,1)} %param.30), channel_id=1, replica_groups=mesh['dp'=8,'mem'=4] {'dp','mem'}, dimensions={0}, use_global_device_ids=true | all-gather | bytes 540672 | tf_op jit(solution)/shard_map/all_gather | solution.py:176
  140.5 39.6 %all_gather.54 = bf16[512,512]{1,0:T(8,128)(2,1)S(1)} all-gather(bf16[16,512]{1,0:T(8,128)(2,1)} %param.31), channel_id=1, replica_groups=mesh['dp'=8,'mem'=4] {'dp','mem'}, dimensions={0}, use_global_device_ids=true | all-gather | bytes 540672 | tf_op jit(solution)/shard_map/all_gather | solution.py:177
  180.1 38.3 %all_gather.57 = bf16[512,512]{1,0:T(8,128)(2,1)S(1)} all-gather(bf16[16,512]{1,0:T(8,128)(2,1)} %param.32), channel_id=1, replica_groups=mesh['dp'=8,'mem'=4] {'dp','mem'}, dimensions={0}, use_global_device_ids=true | all-gather | bytes 540672 | tf_op jit(solution)/shard_map/all_gather | solution.py:178
  218.4 42.2 %all_gather.60 = bf16[512,512]{1,0:T(8,128)(2,1)} all-gather(bf16[16,512]{1,0:T(8,128)(2,1)} %param.33), channel_id=1, replica_groups=mesh['dp'=8,'mem'=4] {'dp','mem'}, dimensions={0}, use_global_device_ids=true | all-gather | bytes 540672 | tf_op jit(solution)/shard_map/all_gather | solution.py:179
  278.5 38.4 %all_gather.62 = bf16[512,512]{1,0:T(8,128)(2,1)S(1)} all-gather(bf16[16,512]{1,0:T(8,128)(2,1)S(1)} %copy-done.55), channel_id=1, replica_groups=mesh['dp'=8,'mem'=4] {'dp','mem'}, dimensions={0}, use_global_device_ids=true | all-gather | bytes 540672 | tf_op jit(solution)/shard_map/all_gather | solution.py:180
  316.9 39.5 %all_gather.63 = bf16[512,512]{1,0:T(8,128)(2,1)S(1)} all-gather(bf16[16,512]{1,0:T(8,128)(2,1)S(1)} %copy-done.56), channel_id=1, replica_groups=mesh['dp'=8,'mem'=4] {'dp','mem'}, dimensions={0}, use_global_device_ids=true | all-gather | bytes 540672 | tf_op jit(solution)/shard_map/all_gather | solution.py:181
  362.7 33.7 %while.7 = (s32[]{:T(128)}, f32[4,512,512]{2,1,0:T(8,128)}, f32[4,512,8]{1,2,0:T(8,128)}, s32[]{:T(128)}, s32[4,512]{1,0:T(4,128)S(1)}, /*index=5*/s32[4,512]{1,...) while((s32[]{:T(128)}, f32[4,512,512]{2,1,0:T(8,128)}, ...), condition=%wide.region_10.11_spmd.clone, body=%wide.region_8.10_spmd.sunk.clone | while | flops 550236672 | bytes 25493624 | solution.py:72
  398.7 41.5 %all_gather.64 = bf16[512,512]{1,0:T(8,128)(2,1)} all-gather(bf16[16,512]{1,0:T(8,128)(2,1)S(1)} %copy-done.57), channel_id=1, replica_groups=mesh['dp'=8,'mem'=4] {'dp','mem'}, dimensions={0}, use_global_device_ids=true | all-gather | bytes 540672 | tf_op jit(solution)/shard_map/all_gather | solution.py:182
  440.2 48.5 %all-reduce.17.cloned.1.call-done = (f32[2048,8]{0,1:T(8,128)}, f32[2048,512]{1,0:T(8,128)}) async-done(((f32[2048,8]{0,1:T(8,128)}, f32[2048,512]{1,0:T(8,128)}), (f32[2048,8]{0,1:T(8,128)}, f32[2048,512]{1,0:T(8,128)})) %all-reduce.17.cloned.1.call-update) | async-done | bytes 4259856 | tf_op jit(solution)/shard_map/psum | solution.py:247
  500.4 35.6 %all-gather.9.cloned.1.call-done = bf16[2048,512]{1,0:T(8,128)(2,1)} async-done(((bf16[64,512]{1,0:T(8,128)(2,1)}), bf16[2048,512]{1,0:T(8,128)(2,1)}) %all-gather.9.cloned.1.call-update) | async-done | bytes 2097168 | tf_op jit(solution)/shard_map/all_gather | solution.py:184
  588.9 55.3 %while.8 = (s32[]{:T(128)}, f32[512,8,64]{0,2,1:T(8,128)}, f32[512,8,64]{0,2,1:T(8,128)S(1)}, bf16[4,512,512]{2,1,0:T(8,128)(2,1)}, bf16[4,512,512]{1,2,0:T(8,12...) while((s32[]{:T(128)}, f32[512,8,64]{0,2,1:T(8,128)}, ...), condition=%wide.region_23.24_spmd.clone.clone, body=%wide.region_22.23_spmd.clone.sunk.clone | while | flops 1361576448 | bytes 58523844 | solution.py:132
  719.3 39.4 %all-reduce.12 = (f32[512]{0:T(512)S(1)}, f32[512]{0:T(512)S(1)}, f32[512]{0:T(512)S(1)}, f32[512]{0:T(512)S(1)}, f32[512]{0:T(512)S(1)}, /*index=5*/f32[512]{0:T(512)S(1)}) all-reduce(f32[512]{0:T(512)S(1)} %get-tuple-element.409, f32[512]{0:T(512)S(1)} %get-tuple-element.416, ...), channel_id=13, replica_groups=mesh['dp'=8,'mem'=4] {'dp','mem'}, use_global_device_ids=true, to_apply=%region_39.40.clone | all-reduce | flops 3072 | bytes 24576
  767.0 46.4 %reduce-scatter.28.cloned.1.call-done = f32[16,512]{1,0:T(8,128)} async-done(((f32[512,512]{1,0:T(8,128)}), f32[16,512]{1,0:T(8,128)}) %reduce-scatter.28.cloned.1.call-update) | async-done | bytes 32784 | tf_op jit(solution)/shard_map/reduce_scatter | solution.py:322
  813.4 133.7 %reduce-scatter.40.cloned.1.call-done = f32[16,512]{1,0:T(8,128)} async-done(((f32[512,512]{1,0:T(8,128)}), f32[16,512]{1,0:T(8,128)}) %reduce-scatter.40.cloned.1.call-update) | async-done | bytes 32784
  947.1 133.5 %reduce-scatter.42.cloned.1.call-done = f32[16,512]{1,0:T(8,128)} async-done(((f32[512,512]{1,0:T(8,128)}), f32[16,512]{1,0:T(8,128)}) %reduce-scatter.42.cloned.1.call-update) | async-done | bytes 32784
  1080.6 140.0 %reduce-scatter.32.cloned.1.call-done = f32[64,512]{1,0:T(8,128)} async-done(((f32[2048,512]{1,0:T(8,128)}), f32[64,512]{1,0:T(8,128)}) %reduce-scatter.32.cloned.1.call-update) | async-done | bytes 131088 | tf_op jit(solution)/shard_map/reduce_scatter | solution.py:324
  1220.6 139.9 %reduce-scatter.30.cloned.1.call-done = f32[16,2048]{1,0:T(8,128)} async-done(((f32[512,2048]{1,0:T(8,128)}), f32[16,2048]{1,0:T(8,128)}) %reduce-scatter.30.cloned.1.call-update) | async-done | bytes 131088 | tf_op jit(solution)/shard_map/reduce_scatter | solution.py:323
  1360.4 133.4 %reduce-scatter.26.cloned.1.call-done = f32[16,512]{1,0:T(8,128)} async-done(((f32[512,512]{1,0:T(8,128)}), f32[16,512]{1,0:T(8,128)}) %reduce-scatter.26.cloned.1.call-update) | async-done | bytes 32784 | tf_op jit(solution)/shard_map/reduce_scatter | solution.py:319
  1493.9 133.5 %reduce-scatter.24.cloned.1.call-done = f32[16,512]{1,0:T(8,128)} async-done(((f32[512,512]{1,0:T(8,128)}), f32[16,512]{1,0:T(8,128)}) %reduce-scatter.24.cloned.1.call-update) | async-done | bytes 32784 | tf_op jit(solution)/shard_map/reduce_scatter | solution.py:318
  1627.4 133.5 %reduce-scatter.38.cloned.1.call-done = f32[16,512]{1,0:T(8,128)} async-done(((f32[512,512]{1,0:T(8,128)}), f32[16,512]{1,0:T(8,128)}) %reduce-scatter.38.cloned.1.call-update) | async-done | bytes 32784
  1760.9 133.5 %reduce-scatter.36.cloned.1.call-done = f32[16,512]{1,0:T(8,128)} async-done(((f32[512,512]{1,0:T(8,128)}), f32[16,512]{1,0:T(8,128)}) %reduce-scatter.36.cloned.1.call-update) | async-done | bytes 32784
  1894.4 133.5 %reduce-scatter.34.cloned.1.call-done = f32[16,512]{1,0:T(8,128)} async-done(((f32[512,512]{1,0:T(8,128)}), f32[16,512]{1,0:T(8,128)}) %reduce-scatter.34.cloned.1.call-update) | async-done | bytes 32784
  (373 shorter events, 272.1 us)
Async XLA Ops:
  8.0 348.3 %copy-start = (bf16[512,512]{1,0:T(8,128)(2,1)S(1)}, bf16[512,512]{1,0:T(8,128)(2,1)}, u32[]{:S(2)}) copy-start(bf16[512,512]{1,0:T(8,128)(2,1)} %param.27) | copy-start | bytes 1572868
  8.0 257.0 %copy-start.6 = (bf16[512,512]{1,0:T(8,128)(2,1)S(1)}, bf16[512,512]{1,0:T(8,128)(2,1)}, u32[]{:S(2)}) copy-start(bf16[512,512]{1,0:T(8,128)(2,1)} %param.26) | copy-start | bytes 1572868
  8.0 350.4 %all-gather.5.cloned.1.call-start = ((), (), s32[]{:S(2)}) async-start(), calls=%async_computation.11 | async-start | bytes 2621440 | tf_op jit(solution)/shard_map/all_gather | solution.py:243
  102.2 169.3 %copy-start.19 = (bf16[512,512]{1,0:T(8,128)(2,1)}, bf16[512,512]{1,0:T(8,128)(2,1)S(1)}, u32[]{:S(2)}) copy-start(bf16[512,512]{1,0:T(8,128)(2,1)S(1)} %all_gather.55) | copy-start | bytes 1572868
  140.5 131.1 %copy-start.17 = (bf16[512,512]{1,0:T(8,128)(2,1)}, bf16[512,512]{1,0:T(8,128)(2,1)S(1)}, u32[]{:S(2)}) copy-start(bf16[512,512]{1,0:T(8,128)(2,1)S(1)} %all_gather.56) | copy-start | bytes 1572868
  180.1 91.5 %copy-start.15 = (bf16[512,512]{1,0:T(8,128)(2,1)}, bf16[512,512]{1,0:T(8,128)(2,1)S(1)}, u32[]{:S(2)}) copy-start(bf16[512,512]{1,0:T(8,128)(2,1)S(1)} %all_gather.54) | copy-start | bytes 1572868
  218.4 56.8 %copy-start.28 = (bf16[512,512]{1,0:T(8,128)(2,1)}, bf16[512,512]{1,0:T(8,128)(2,1)S(1)}, u32[]{:S(2)}) copy-start(bf16[512,512]{1,0:T(8,128)(2,1)S(1)} %all_gather.57) | copy-start | bytes 1572868
  276.1 86.5 %copy-start.53 = (f32[512]{0:T(512)}, f32[512]{0:T(512)S(1)}, u32[]{:S(2)}) copy-start(f32[512]{0:T(512)S(1)} %multiply_reduce_fusion.7) | copy-start | bytes 6148
  278.4 210.4 %all-reduce.17.cloned.1.call-start = ((), (), s32[]{:S(2)}) async-start(), calls=%async_computation.26 | async-start | bytes 8519680 | tf_op jit(solution)/shard_map/psum | solution.py:247
  396.4 98.9 %all-gather.7.cloned.1.call-start = ((), (), s32[]{:S(2)}) async-start(), calls=%async_computation.12 | async-start | bytes 2162688 | tf_op jit(solution)/shard_map/all_gather | solution.py:183
  397.0 139.1 %all-gather.9.cloned.1.call-start = ((), (), s32[]{:S(2)}) async-start(), calls=%async_computation.13 | async-start | bytes 2162688 | tf_op jit(solution)/shard_map/all_gather | solution.py:184
  397.6 173.9 %all-gather.11.cloned.1.call-start = ((), (), s32[]{:S(2)}) async-start(), calls=%async_computation.14 | async-start | bytes 2621440 | tf_op jit(solution)/shard_map/all_gather | solution.py:272
  495.1 52.1 %copy-start.4 = (f32[512,512]{0,1:T(8,128)}, f32[512,512]{0,1:T(8,128)S(1)}, u32[]{:S(2)}) copy-start(f32[512,512]{0,1:T(8,128)S(1)} %get-tuple-element.499) | copy-start | bytes 3145732
  549.8 126.1 %reduce-scatter.22.cloned.1.call-start = ((), (), s32[]{:S(2)}) async-start(), calls=%async_computation.15 | async-start | bytes 2621440 | tf_op jit(solution)/shard_map/reduce_scatter | solution.py:284
  644.2 169.2 %reduce-scatter.28.cloned.1.call-start = ((), (), s32[]{:S(2)}) async-start(), calls=%async_computation.18 | async-start | bytes 1081344 | tf_op jit(solution)/shard_map/reduce_scatter | solution.py:322
  647.2 299.9 %reduce-scatter.40.cloned.1.call-start = ((), (), s32[]{:S(2)}) async-start(), calls=%async_computation.24 | async-start | bytes 1081344
  651.2 429.4 %reduce-scatter.42.cloned.1.call-start = ((), (), s32[]{:S(2)}) async-start(), calls=%async_computation.25 | async-start | bytes 1081344
  653.9 566.7 %reduce-scatter.32.cloned.1.call-start = ((), (), s32[]{:S(2)}) async-start(), calls=%async_computation.20 | async-start | bytes 4325376 | tf_op jit(solution)/shard_map/reduce_scatter | solution.py:324
  660.1 700.3 %reduce-scatter.30.cloned.1.call-start = ((), (), s32[]{:S(2)}) async-start(), calls=%async_computation.19 | async-start | bytes 4325376 | tf_op jit(solution)/shard_map/reduce_scatter | solution.py:323
  666.3 827.6 %reduce-scatter.26.cloned.1.call-start = ((), (), s32[]{:S(2)}) async-start(), calls=%async_computation.17 | async-start | bytes 1081344 | tf_op jit(solution)/shard_map/reduce_scatter | solution.py:319
  678.4 949.0 %reduce-scatter.24.cloned.1.call-start = ((), (), s32[]{:S(2)}) async-start(), calls=%async_computation.16 | async-start | bytes 1081344 | tf_op jit(solution)/shard_map/reduce_scatter | solution.py:318
  682.3 1078.6 %reduce-scatter.38.cloned.1.call-start = ((), (), s32[]{:S(2)}) async-start(), calls=%async_computation.23 | async-start | bytes 1081344
  693.3 1201.1 %reduce-scatter.36.cloned.1.call-start = ((), (), s32[]{:S(2)}) async-start(), calls=%async_computation.22 | async-start | bytes 1081344
  706.0 1321.9 %reduce-scatter.34.cloned.1.call-start = ((), (), s32[]{:S(2)}) async-start(), calls=%async_computation.21 | async-start | bytes 1081344
  (57 other events, 473.1 us)
Sparse Core Ops, SparseCore 0:
  278.5 21.1 all-gather.4
  396.5 92.2 all-reduce.16
  549.9 21.4 all-gather.10
  644.4 31.4 reduce-scatter.21
  678.5 134.8 reduce-scatter.27
  816.2 130.8 reduce-scatter.39
  949.9 130.6 reduce-scatter.41
  1083.5 136.9 reduce-scatter.31
  1223.5 136.8 reduce-scatter.29
  1363.2 130.6 reduce-scatter.25
  1496.7 130.6 reduce-scatter.23
  1630.1 130.6 reduce-scatter.37
  1763.7 130.6 reduce-scatter.35
  1897.1 130.6 reduce-scatter.33
Sparse Core Ops, SparseCore 1:
  399.7 78.5 all-gather.6
  481.0 54.9 all-gather.8
where the time goes:
time: 2050 us; the launch traced here: 2040 us
  waiting for transfers between devices  1370 us (67%)
  blocking collectives  401 us (20%)
  matrix products  146 us (7%)
  local copies, waits for them, and re-layouts  80.1 us (4%)
    unnamed x21, waiting for transfers between devices  669 us
    reduce_scatter x1, waiting for transfers between devices, local(): lax.psum_scatter(g_ffn_second, ('dp', 'mem'), scatter_dimension=0, tiled=...  140 us
    reduce_scatter x1, waiting for transfers between devices, local(): lax.psum_scatter(g_ffn_first, ('dp', 'mem'), scatter_dimension=0, tiled=T...  140 us
    reduce_scatter x1, waiting for transfers between devices, local(): lax.psum_scatter(g_out_self, ('dp', 'mem'), scatter_dimension=0, tiled=True)  134 us
    reduce_scatter x1, waiting for transfers between devices, local(): lax.psum_scatter(g_query_cross, ('dp', 'mem'), scatter_dimension=0, tiled...  133 us
    unnamed x2, blocking collectives  81.5 us
    psum x1, waiting for transfers between devices, local(): numer_cross, totals_cross = lax.psum((numer_part, totals_part), 'mem')  48.5 us
    reduce_scatter x1, waiting for transfers between devices, local(): lax.psum_scatter(g_out_cross, ('dp', 'mem'), scatter_dimension=0, tiled=T...  46.4 us
  transfers between devices with their start and end apart: 16, of which 14 were waited for; matrix products, arithmetic and copies ran while one was open for 4% of the time, Pallas kernels for 0%

commit v1 on v0

v1 whole, which is shorter than its diff:
```python
import jax
import jax.numpy as jnp
from jax import lax
from jax.experimental import pallas as pl
from jax.experimental.pallas import tpu as pltpu
from jax.sharding import PartitionSpec as P

MESH = pl.DeviceIdType.MESH
SLAB = 512
NORM = 128
LANES = NORM + 16 * SLAB
ROWS = 16


def here():
    dp, mem = lax.axis_index("dp"), lax.axis_index("mem")
    return dp // 2, dp % 2, mem // 2, mem % 2


def device(z, x, y, c):
    return (z * 2 + x, y * 2 + c)


def greet(peers):
    barrier = pltpu.get_barrier_semaphore()
    for peer in peers:
        pl.semaphore_signal(barrier, inc=1, device_id=peer, device_id_type=MESH)
    pl.semaphore_wait(barrier, len(peers))


def remote(src, dst, sems, index, peer):
    send, recv = sems
    return pltpu.make_async_remote_copy(
        src_ref=src,
        dst_ref=dst,
        send_sem=send.at[index],
        recv_sem=recv.at[index],
        device_id=peer,
        device_id_type=MESH,
    )


GATHER_ROUNDS = ((0, 640, 2176), (2176, 2688, 4224), (4224, 5248, 8320))


def gather_kernel(*refs):
    shards = refs[:11]
    norm_ref, memory_ref = refs[11], refs[12]
    out, mem_out = refs[13], refs[14]
    local_sem, mem_local = refs[15], refs[16]
    zs = refs[17:19]
    first, second, across = refs[19:21], refs[21:23], refs[23:25]
    mems = refs[25:27]
    shards = shards[:10]
    z, x, y, c = here()
    xp, yp, cp_ = device(z, 1 - x, y, c), device(z, x, 1 - y, c), device(z, x, y, 1 - c)
    zp = [device((z + k) % 4, x, y, c) for k in (1, 2, 3)]
    own = out.at[z, x, y, c]

    local = []

    def bring(src, start, width):
        local.append(
            pltpu.make_async_copy(src, own.at[:, pl.ds(start, width)], local_sem.at[len(local)])
        )

    bring(norm_ref, 0, NORM)
    for i in range(8):
        bring(shards[i], NORM + SLAB * i, SLAB)
    bring(shards[8], NORM + SLAB * 8, 4 * SLAB)
    for k in range(4):
        bring(shards[9].at[pl.ds(ROWS * k, ROWS)], NORM + SLAB * (12 + k), SLAB)
    for one in local:
        one.start()
    keep = pltpu.make_async_copy(memory_ref, mem_out.at[y, c], mem_local)
    keep.start()
    greet([xp, yp, cp_] + zp)
    for one in local:
        one.wait()

    sent = []

    def go(copy):
        copy.start()
        sent.append(copy)

    def zcopy(r, k, source_z):
        a, _, b = GATHER_ROUNDS[r]
        ref = out.at[source_z, x, y, c, :, pl.ds(a, b - a)]
        return remote(ref, ref, zs, (r, k), zp[k])

    def one(r, stage, part, zz, other, kk):
        a, m, b = GATHER_ROUNDS[r]
        lanes = pl.ds(a, m - a) if part == 0 else pl.ds(m, b - m)
        if part == 0:
            ref = out.at[zz, other, y, c, :, lanes]
            peer = xp if stage == 0 else yp
        else:
            ref = out.at[zz, x, other, c, :, lanes]
            peer = yp if stage == 0 else xp
        if stage == 0:
            return remote(ref, ref, first, (r, part, kk), peer)
        return remote(ref, ref, second, (r, part, kk), peer)

    def over(r, zz, xx, yy, cc, kk, part):
        a, m, b = GATHER_ROUNDS[r]
        lanes = pl.ds(a, m - a) if part == 0 else pl.ds(m, b - m)
        ref = out.at[zz, xx, yy, cc, :, lanes]
        return remote(ref, ref, across, (r, kk, part), cp_)

    zz = [z, (z + 1) % 4, (z + 2) % 4, (z + 3) % 4]

    mem_own = mem_out.at[y, c]

    def block(r, k, hop):
        for part in (0, 1):
            mine = x if part == 0 else y
            go(one(r, 0, part, zz[k], mine, k))
            go(one(r, 1, part, zz[k], mine, 2 * k))

    rounds = range(len(GATHER_ROUNDS))
    for r in rounds:
        for k in range(3):
            go(zcopy(r, k, z))
        block(r, 0, 0)
        if r == 0:
            keep.wait()
            go(remote(mem_own, mem_own, mems, 0, yp))
            go(remote(mem_own, mem_own, mems, 1, cp_))
    for r in rounds:
        for part in (0, 1):
            go(over(r, z, x, y, c, 0, part))

    def arrive_z(r):
        for j in (0, 2, 1):
            k = 3 - j
            zcopy(r, j, zz[k]).wait_recv()
            block(r, k, 0)
            for part in (0, 1):
                go(over(r, zz[k], x, y, c, 4 * k, part))

    def arrive_first(r):
        for k in (0, 1, 3, 2):
            for part in (0, 1):
                theirs = (1 - x) if part == 0 else (1 - y)
                one(r, 0, part, zz[k], theirs, k).wait_recv()
                go(one(r, 1, part, zz[k], theirs, 2 * k + 1))
                if part == 0:
                    go(over(r, zz[k], 1 - x, y, c, 4 * k + 1, 0))
                else:
                    go(over(r, zz[k], x, 1 - y, c, 4 * k + 2, 1))

    def arrive_second(r):
        for k in (0, 1, 3, 2):
            for h in (0, 1):
                for part in (0, 1):
                    if part == 0:
                        xx = x if h == 0 else 1 - x
                        a, m, b = GATHER_ROUNDS[r]
                        ref = out.at[zz[k], xx, 1 - y, c, :, pl.ds(a, m - a)]
                        remote(ref, ref, second, (r, 0, 2 * k + h), yp).wait_recv()
                        go(over(r, zz[k], xx, 1 - y, c, 4 * k + 2 + h, 0))
                    else:
                        yy = y if h == 0 else 1 - y
                        a, m, b = GATHER_ROUNDS[r]
                        ref = out.at[zz[k], 1 - x, yy, c, :, pl.ds(m, b - m)]
                        remote(ref, ref, second, (r, 1, 2 * k + h), xp).wait_recv()
                        go(over(r, zz[k], 1 - x, yy, c, 4 * k + 1 + 2 * h, 1))

    def arrive_over(r):
        for k in range(4):
            for o, (xx, yy) in enumerate(((x, y), (1 - x, y), (x, 1 - y), (1 - x, 1 - y))):
                for part in (0, 1):
                    over(r, zz[k], xx, yy, 1 - c, 4 * k + o, part).wait_recv()

    arrive_z(0)
    arrive_z(1)
    arrive_first(0)
    arrive_z(2)
    arrive_first(1)
    arrive_second(0)
    there = mem_out.at[1 - y, c]
    remote(there, there, mems, 0, yp).wait_recv()
    go(remote(there, there, mems, 2, cp_))
    arrive_first(2)
    arrive_second(1)
    arrive_over(0)
    arrive_second(2)
    arrive_over(1)
    arrive_over(2)
    across_own = mem_out.at[y, 1 - c]
    remote(across_own, across_own, mems, 1, cp_).wait_recv()
    across_far = mem_out.at[1 - y, 1 - c]
    remote(across_far, across_far, mems, 2, cp_).wait_recv()
    for copy in sent:
        copy.wait_send()


def gather_all(shards, norms, memory):
    any_space = pl.BlockSpec(memory_space=pl.ANY)
    dma = pltpu.SemaphoreType.DMA
    n = len(GATHER_ROUNDS)

    def kernel(*refs):
        gather_kernel(*refs[:10], None, *refs[10:])

    gathered, whole_memory = pl.pallas_call(
        kernel,
        out_shape=(
            jax.ShapeDtypeStruct((4, 2, 2, 2, ROWS, LANES), jnp.bfloat16),
            jax.ShapeDtypeStruct((2, 2) + memory.shape, jnp.bfloat16),
        ),
        in_specs=[any_space] * 12,
        out_specs=(any_space, any_space),
        scratch_shapes=[
            dma((14,)),
            dma(()),
            dma((n, 3)),
            dma((n, 3)),
            dma((n, 2, 4)),
            dma((n, 2, 4)),
            dma((n, 2, 8)),
            dma((n, 2, 8)),
            dma((n, 16, 2)),
            dma((n, 16, 2)),
            dma((3,)),
            dma((3,)),
        ],
        compiler_params=pltpu.CompilerParams(collective_id=1, has_side_effects=True),
        name="gather",
    )(*shards, norms, memory)
    return gathered.reshape(32, ROWS, LANES), whole_memory.reshape(-1, SLAB)
SCATTER_ROUNDS = ((4224, 4736, 6272), (6272, 6784, 8320), (2176, 2688, 4224), (0, 640, 2176))


def scatter_kernel(grads, mem_grads, out, mem_out, acc, from_core, from_first, from_second, from_z,
                   macc, mfrom_core, mfrom_y, own_sems, mown_sem, core_s, core_r, first_s, first_r,
                   second_s, second_r, zs_s, zs_r, mem_s, mem_r):
    z, x, y, c = here()
    xp, yp, cp_ = device(z, 1 - x, y, c), device(z, x, 1 - y, c), device(z, x, y, 1 - c)
    zp = [device((z + k) % 4, x, y, c) for k in (1, 2, 3)]
    count = len(SCATTER_ROUNDS)
    core_sems, first_sems, second_sems = (core_s, core_r), (first_s, first_r), (second_s, second_r)
    z_sems, mem_sems = (zs_s, zs_r), (mem_s, mem_r)
    sent = []

    def go(copy):
        copy.start()
        sent.append(copy)

    def span(r, part=None):
        a, m, b = SCATTER_ROUNDS[r]
        return {None: (a, b - a), 0: (a, m - a), 1: (m, b - m)}[part]

    def own(r):
        a, n = span(r)
        return pltpu.make_async_copy(
            grads.at[:, :, :, c, :, pl.ds(a, n)], acc.at[:, :, :, :, pl.ds(a, n)], own_sems.at[r])

    def core(r):
        a, n = span(r)
        return remote(grads.at[:, :, :, 1 - c, :, pl.ds(a, n)],
                      from_core.at[:, :, :, :, pl.ds(a, n)], core_sems, r, cp_)

    def first(r, part):
        lanes = pl.ds(*span(r, part))
        src = acc.at[:, :, 1 - y, :, lanes] if part == 0 else acc.at[:, 1 - x, :, :, lanes]
        return remote(src, from_first.at[:, :, :, lanes], first_sems, (r, part),
                      yp if part == 0 else xp)

    def second(r, part):
        lanes = pl.ds(*span(r, part))
        src = acc.at[:, 1 - x, y, :, lanes] if part == 0 else acc.at[:, x, 1 - y, :, lanes]
        return remote(src, from_second.at[:, :, lanes], second_sems, (r, part),
                      xp if part == 0 else yp)

    def along(r, k):
        lanes = pl.ds(*span(r))
        return remote(acc.at[(z + k + 1) % 4, x, y, :, lanes], from_z.at[k, :, lanes], z_sems,
                      (r, k), zp[k])

    mem_own = pltpu.make_async_copy(mem_grads.at[:, c], macc, mown_sem)
    mem_core = remote(mem_grads.at[:, 1 - c], mfrom_core, mem_sems, 0, cp_)
    mem_far = remote(macc.at[1 - y], mfrom_y, mem_sems, 1, yp)

    own(0).start()
    mem_own.start()
    for r in range(1, count):
        own(r).start()
    greet([xp, yp, cp_] + zp)
    go(core(0))
    go(mem_core)
    for r in range(1, count):
        go(core(r))

    def add_core(r):
        own(r).wait()
        core(r).wait_recv()
        for part in (0, 1):
            lanes = pl.ds(*span(r, part))
            for theirs in (True, False):
                def body(zi, carry, part=part, lanes=lanes, theirs=theirs):
                    for o in (0, 1):
                        if part == 0:
                            xi, yi = o, (1 - y) if theirs else y
                        else:
                            xi, yi = (1 - x) if theirs else x, o
                        acc[zi, xi, yi, :, lanes] = (
                            acc[zi, xi, yi, :, lanes] + from_core[zi, xi, yi, :, lanes])
                    return carry
                lax.fori_loop(0, 4, body, 0)
                if theirs:
                    go(first(r, part))

    def add_first(r):
        for part in (0, 1):
            first(r, part).wait_recv()
            lanes = pl.ds(*span(r, part))
            for theirs in (True, False):
                def body(zi, carry, part=part, lanes=lanes, theirs=theirs):
                    if part == 0:
                        xi, yi = (1 - x) if theirs else x, y
                        slot = xi
                    else:
                        xi, yi = x, (1 - y) if theirs else y
                        slot = yi
                    acc[zi, xi, yi, :, lanes] = (
                        acc[zi, xi, yi, :, lanes] + from_first[zi, slot, :, lanes])
                    return carry
                lax.fori_loop(0, 4, body, 0)
                if theirs:
                    go(second(r, part))

    def add_second(r):
        for part in (0, 1):
            second(r, part).wait_recv()
            lanes = pl.ds(*span(r, part))

            def body(zi, carry, lanes=lanes):
                acc[zi, x, y, :, lanes] = acc[zi, x, y, :, lanes] + from_second[zi, :, lanes]
                return carry
            lax.fori_loop(0, 4, body, 0)
        for k in (1, 0, 2):
            go(along(r, k))

    def add_z(r):
        lanes = pl.ds(*span(r))
        total = acc[z, x, y, :, lanes].astype(jnp.float32)
        for k in (0, 2, 1):
            along(r, k).wait_recv()
            total = total + from_z[k, :, lanes].astype(jnp.float32)
        out[:, lanes] = total

    def memory_core():
        mem_own.wait()
        mem_core.wait_recv()
        for theirs in (True, False):
            side = (1 - y) if theirs else y

            def body(i, carry, side=side):
                rows = pl.ds(pl.multiple_of(i * 64, 64), 64)
                macc[side, rows] = macc[side, rows] + mfrom_core[side, rows]
                return carry
            lax.fori_loop(0, 8, body, 0)
            if theirs:
                go(mem_far)

    def memory_end():
        mem_far.wait_recv()

        def body(i, carry):
            rows = pl.ds(pl.multiple_of(i * 64, 64), 64)
            mem_out[rows] = macc[y, rows].astype(jnp.float32) + mfrom_y[rows].astype(jnp.float32)
            return carry
        lax.fori_loop(0, 8, body, 0)

    for t in range(count + 3):
        if t < count:
            add_core(t)
        if t == 0:
            memory_core()
        if 0 <= t - 1 < count:
            add_first(t - 1)
        if 0 <= t - 2 < count:
            add_second(t - 2)
        if 0 <= t - 3 < count:
            add_z(t - 3)
        if t == 3:
            memory_end()
    for copy in sent:
        copy.wait_send()


def scatter_all(grads, mem_grads):
    any_space = pl.BlockSpec(memory_space=pl.ANY)
    vmem = pl.BlockSpec(memory_space=pltpu.VMEM)
    dma = pltpu.SemaphoreType.DMA
    n = len(SCATTER_ROUNDS)
    rows = mem_grads.shape[2]
    low = jnp.bfloat16
    return pl.pallas_call(
        scatter_kernel,
        out_shape=(
            jax.ShapeDtypeStruct((ROWS, LANES), jnp.float32),
            jax.ShapeDtypeStruct((rows, SLAB), jnp.float32),
        ),
        in_specs=[any_space] * 2,
        out_specs=(vmem, vmem),
        scratch_shapes=[
            pltpu.VMEM((4, 2, 2, ROWS, LANES), low),
            pltpu.VMEM((4, 2, 2, ROWS, LANES), low),
            pltpu.VMEM((4, 2, ROWS, LANES), low),
            pltpu.VMEM((4, ROWS, LANES), low),
            pltpu.VMEM((3, ROWS, LANES), low),
            pltpu.VMEM((2, rows, SLAB), low),
            pltpu.VMEM((2, rows, SLAB), low),
            pltpu.VMEM((rows, SLAB), low),
            dma((n,)),
            dma(()),
            dma((n,)),
            dma((n,)),
            dma((n, 2)),
            dma((n, 2)),
            dma((n, 2)),
            dma((n, 2)),
            dma((n, 3)),
            dma((n, 3)),
            dma((2,)),
            dma((2,)),
        ],
        compiler_params=pltpu.CompilerParams(
            collective_id=2, has_side_effects=True, vmem_limit_bytes=48 << 20),
        name="scatter",
    )(grads, mem_grads)


def two_by_two(mesh_axes):
    return mesh_axes == (8, 4)


def gather_any(shards, norms, memory):
    everyone = ("dp", "mem")
    packed = jnp.concatenate([norms] + list(shards[:9]), axis=1)
    rows = lax.all_gather(packed, everyone, axis=0, tiled=True).reshape(32, ROWS, -1)
    last = lax.all_gather(shards[9], everyone, axis=0, tiled=True)
    last = last.reshape(32, 4, ROWS, SLAB).transpose(0, 2, 1, 3).reshape(32, ROWS, 4 * SLAB)
    return (
        jnp.concatenate([rows, last], axis=2),
        lax.all_gather(memory, "mem", axis=0, tiled=True),
    )


def scatter_any(grads, mem_grads):
    everyone = ("dp", "mem")
    wide = grads.reshape(32, ROWS, LANES).astype(jnp.float32)
    cut = LANES - 4 * SLAB
    rows = lax.psum_scatter(
        wide[:, :, :cut].reshape(512, cut), everyone, scatter_dimension=0, tiled=True
    )
    last = wide[:, :, cut:].reshape(32, ROWS, 4, SLAB).transpose(0, 2, 1, 3).reshape(2048, SLAB)
    last = lax.psum_scatter(last, everyone, scatter_dimension=0, tiled=True)
    mem = lax.psum_scatter(
        mem_grads.astype(jnp.float32), "mem", scatter_dimension=0, tiled=True
    )
    return rows, last, mem
HEADS = 8
HEAD = 64
eps_norm = 1e-05
score_scale = 0.125


def layer_norm(values, gain, shift):
    centre = values - jnp.mean(values, axis=-1, keepdims=True)
    spread = jnp.mean(centre * centre, axis=-1, keepdims=True)
    return centre * lax.rsqrt(spread + eps_norm) * gain + shift


def head_split(values):
    return values.reshape(values.shape[0], HEADS, HEAD)


def matmul(left, right):
    return jnp.dot(left, right, preferred_element_type=jnp.float32)


def left_grad(inputs, grads):
    return jnp.einsum("ra,rb->ab", inputs, grads, preferred_element_type=jnp.float32)


def back_through(grads, weight):
    return jnp.einsum("rb,ab->ra", grads, weight, preferred_element_type=jnp.float32)


def exp_scores(q_block, keys, low_edge, high_edge):
    raw = jnp.einsum("qhd,khd->hqk", head_split(q_block), head_split(keys),
                     preferred_element_type=jnp.float32) * score_scale
    position = lax.broadcasted_iota(jnp.int32, (q_block.shape[0], keys.shape[0]), 1)
    allowed = (position >= low_edge[:, None]) & (position < high_edge[:, None])
    return jnp.where(allowed[None], jnp.exp(raw), 0.0)


def attend(queries, keys, values, low_edge, high_edge):
    expo = exp_scores(queries, keys, low_edge, high_edge)
    numer = jnp.einsum("hqk,khd->qhd", expo.astype(jnp.bfloat16), head_split(values),
                       preferred_element_type=jnp.float32)
    totals = jnp.sum(expo, axis=2).T
    return (numer / totals[:, :, None]).reshape(queries.shape[0], -1), totals


def attend_back(queries, keys, values, low_edge, high_edge, upstream, output, totals):
    expo = exp_scores(queries, keys, low_edge, high_edge)
    up = head_split(upstream.astype(jnp.float32))
    numer_grad = (up / totals[:, :, None]).astype(jnp.bfloat16)
    corr = -jnp.sum(up * head_split(output), axis=2) / totals
    flow = jnp.einsum("qhd,khd->hqk", numer_grad, head_split(values),
                      preferred_element_type=jnp.float32) + corr.T[:, :, None]
    ds = (expo * flow).astype(jnp.bfloat16)
    dq = jnp.einsum("hqk,khd->qhd", ds, head_split(keys), preferred_element_type=jnp.float32)
    dk = jnp.einsum("hqk,qhd->khd", ds, head_split(queries), preferred_element_type=jnp.float32)
    dv = jnp.einsum("hqk,qhd->khd", expo.astype(jnp.bfloat16), numer_grad,
                    preferred_element_type=jnp.float32)
    flat = lambda v: v.reshape(v.shape[0], -1)
    return ((flat(dq) * score_scale).astype(jnp.bfloat16), (flat(dk) * score_scale).astype(jnp.bfloat16),
            flat(dv).astype(jnp.bfloat16))


def local(target_in, memory, out_grad, *rest):
    weights, (tgt_lens, src_lens, src_offsets) = rest[:16], rest[16:]
    member = lax.axis_index("mem")
    per_device = tgt_lens.shape[1] // lax.axis_size("mem")
    pick = lambda table: lax.dynamic_slice_in_dim(table[0], member * per_device, per_device, 0)
    lengths, spans, offsets = pick(tgt_lens), pick(src_lens), pick(src_offsets)
    norms = jnp.stack(weights[10:], axis=1)
    norms = jnp.pad(norms, ((0, 0), (0, NORM - norms.shape[1])))
    fast = two_by_two((lax.axis_size("dp"), lax.axis_size("mem")))
    gathered, all_memory = (gather_all if fast else gather_any)(weights[:10], norms, memory)
    W = gathered.reshape(512, LANES)
    mat = lambda i: W[:, NORM + SLAB * i : NORM + SLAB * (i + 1)]
    wsq, wsk, wsv, wso, wcq, wck, wcv, wco = [mat(i) for i in range(8)]
    w1 = W[:, NORM + 8 * SLAB : NORM + 12 * SLAB]
    w2 = gathered[:, :, NORM + 12 * SLAB :].reshape(32, 16, 4, SLAB).transpose(0, 2, 1, 3).reshape(2048, SLAB)
    ga, sa, gc, sc, gf, sf = [W[:, i].astype(jnp.float32) for i in range(6)]
    rows = target_in.shape[0]
    starts = jnp.cumsum(lengths) - lengths
    position = lax.iota(jnp.int32, rows)
    sentence = jnp.sum((position[:, None] >= starts[None, :]).astype(jnp.int32), axis=1) - 1
    picker = sentence[:, None] == lax.iota(jnp.int32, per_device)[None, :]
    choose = lambda v: jnp.sum(jnp.where(picker, v[None, :], 0), axis=1)
    self_low, self_high = choose(starts), position + 1
    cross_low = choose(offsets)
    cross_high = cross_low + choose(spans)
    low = jnp.bfloat16
    q, k, v = [matmul(target_in, w).astype(low) for w in (wsq, wsk, wsv)]
    o_self_f, tot_self = attend(q, k, v, self_low, self_high)
    o_self = o_self_f.astype(low)
    after_self, pull_self = jax.vjp(layer_norm, target_in.astype(jnp.float32) + matmul(o_self, wso), ga, sa)
    a_b = after_self.astype(low)
    qc = matmul(a_b, wcq).astype(low)
    kc, vc = matmul(all_memory, wck).astype(low), matmul(all_memory, wcv).astype(low)
    if fast:
        o_c_f, tot_c = attend(qc, kc, vc, cross_low, cross_high)
    else:
        cut = lambda v: v.reshape((4, -1) + v.shape[1:])
        o_c_f, tot_c = lax.map(
            lambda p: attend(p[0], kc, vc, p[1], p[2]), (cut(qc), cut(cross_low), cut(cross_high))
        )
        o_c_f, tot_c = o_c_f.reshape(rows, -1), tot_c.reshape(rows, -1)
    o_c = o_c_f.astype(low)
    after_cross, pull_cross = jax.vjp(layer_norm, after_self + matmul(o_c, wco), gc, sc)
    c_b = after_cross.astype(low)
    hidden = matmul(c_b, w1)
    activated, pull_silu = jax.vjp(jax.nn.silu, hidden)
    act = activated.astype(low)
    final, pull_ffn = jax.vjp(layer_norm, after_cross + matmul(act, w2), gf, sf)
    d_pre_out, g_gf, g_sf = pull_ffn(out_grad.astype(jnp.float32))
    d_branch = d_pre_out.astype(low)
    g_w2 = left_grad(act, d_branch)
    d_hidden = pull_silu(back_through(d_branch, w2))[0].astype(low)
    g_w1 = left_grad(c_b, d_hidden)
    d_pre_cross, g_gc, g_sc = pull_cross(d_pre_out + back_through(d_hidden, w1))
    d_cb = d_pre_cross.astype(low)
    g_wco = left_grad(o_c, d_cb)
    d_oc = back_through(d_cb, wco).astype(low)
    if fast:
        dq_c, dk_c, dv_c = attend_back(qc, kc, vc, cross_low, cross_high, d_oc, o_c_f, tot_c)
    else:
        def piece(carry, p):
            dq, dk, dv = attend_back(p[0], kc, vc, p[1], p[2], p[3], p[4], p[5])
            return (carry[0] + dk, carry[1] + dv), dq

        empty = jnp.zeros(kc.shape, jnp.bfloat16)
        (dk_c, dv_c), dq_c = lax.scan(
            piece,
            (empty, empty),
            tuple(cut(v) for v in (qc, cross_low, cross_high, d_oc, o_c_f, tot_c)),
        )
        dq_c = dq_c.reshape(rows, -1)
    g_wcq, g_wck, g_wcv = left_grad(a_b, dq_c), left_grad(all_memory, dk_c), left_grad(all_memory, dv_c)
    mem_grad = back_through(dk_c, wck) + back_through(dv_c, wcv)
    d_pre_self, g_ga, g_sa = pull_self(d_pre_cross + back_through(dq_c, wcq))
    d_sb = d_pre_self.astype(low)
    g_wso = left_grad(o_self, d_sb)
    d_os = back_through(d_sb, wso).astype(low)
    dq, dk, dv = attend_back(q, k, v, self_low, self_high, d_os, o_self_f, tot_self)
    g_wsq, g_wsk, g_wsv = left_grad(target_in, dq), left_grad(target_in, dk), left_grad(target_in, dv)
    target_grad = d_pre_self + back_through(dq, wsq) + back_through(dk, wsk) + back_through(dv, wsv)
    n_g = jnp.pad(jnp.stack([g_ga, g_sa, g_gc, g_sc, g_gf, g_sf], axis=1), ((0, 0), (0, NORM - 6)))
    g_w2p = g_w2.reshape(32, 4, 16, SLAB).transpose(0, 2, 1, 3).reshape(512, 4 * SLAB)
    grads = jnp.concatenate([g.astype(low) for g in (n_g, g_wsq, g_wsk, g_wsv, g_wso, g_wcq, g_wck, g_wcv, g_wco, g_w1, g_w2p)], axis=1)
    part = lambda i, n=1: out[:, NORM + SLAB * i : NORM + SLAB * (i + n)]
    if fast:
        out, mem_out = scatter_all(grads.reshape(4, 2, 2, 2, 16, LANES), mem_grad.astype(low).reshape(2, 2, rows, SLAB))
        w2_grad = jnp.concatenate([part(12 + k) for k in range(4)], axis=0)
    else:
        out, w2_grad, mem_out = scatter_any(grads, mem_grad.astype(low))
    return (final.astype(low), target_grad, mem_out) + tuple(part(i) for i in range(8)) + (part(8, 4), w2_grad) + tuple(out[:, i] for i in range(6))


def solution(mesh):
    both = P(("dp", "mem"), None)
    flat = P(("dp", "mem"))
    in_specs = (both,) * 13 + (flat,) * 6 + (P("dp", None),) * 3
    out_specs = (both,) * 13 + (flat,) * 6
    return jax.shard_map(local, mesh=mesh, in_specs=in_specs, out_specs=out_specs, check_vma=False)
```

time: 2050 us -> 386 us (0.19)
  waiting for transfers between devices: 1370 us -> 0 us
  blocking collectives: 401 us -> 0 us
  Pallas kernels: 0 us -> 139 us
  matrix products: 146 us -> 179 us
  local copies, waits for them, and re-layouts: 80.1 us -> 47.7 us
    unnamed x21 -> x0, waiting for transfers between devices: 669 us -> none
    reduce_scatter x6 -> x0, waiting for transfers between devices: 603 us -> none  [the longest x1 140 us: local(): lax.psum_scatter(g_ffn_second, ('dp', 'mem'), scatter_dimension=0, tiled=...]
    all_gather x8 -> x0, blocking collectives: 320 us -> none  [the longest x1 42.2 us: local(): lax.all_gather(cross_query, ('dp', 'mem'), axis=0, tiled=True)]
    pallas_call x0 -> x2, Pallas kernels: none -> 139 us  [the longest x1 78.7 us: gather_all(): pl.pallas_call(kernel, out_shape=(jax.ShapeDtypeStruct((4, 2, 2, 2, ROWS,...]
    unnamed x2 -> x0, blocking collectives: 81.5 us -> none
    all_gather x4 -> x0, waiting for transfers between devices: 49.7 us -> none  [the longest x1 35.6 us: local(): lax.all_gather(ffn_out, ('dp', 'mem'), axis=0, tiled=True)]
    psum x1 -> x0, waiting for transfers between devices: 48.5 us -> none  [local(): numer_cross, totals_cross = lax.psum((numer_part, totals_part), 'mem')]
    dot_general x25 -> x10, matrix products: 67.6 us -> 91.3 us  [the longest x2 26.6 us: attend_back(): jnp.einsum('qhd,khd->hqk', numer_grad, head_split(values), preferred_elem...]
  transfers between devices with their start and end apart: 16 -> 0, of which waited for: 14 -> 0; matrix products, arithmetic and copies ran while one was open for 4% -> 0% of each run, Pallas kernels for 0% -> 0%
where the time goes in v1:
time: 386 us; the launch traced here: 379 us
  matrix products  179 us (46%)
  Pallas kernels  139 us (36%)
  local copies, waits for them, and re-layouts  47.7 us (12%)
  other arithmetic  11.9 us (3%)
    pallas_call x1, Pallas kernels, gather_all(): pl.pallas_call(kernel, out_shape=(jax.ShapeDtypeStruct((4, 2, 2, 2, ROWS,...  78.7 us
    pallas_call x1, Pallas kernels, scatter_all(): pl.pallas_call(scatter_kernel, out_shape=(jax.ShapeDtypeStruct((ROWS, LAN...  60.2 us
    dot_general x2, matrix products, attend_back(): jnp.einsum('qhd,khd->hqk', numer_grad, head_split(values), preferred_elem...  26.6 us
    dot_general x10, matrix products, back_through(): jnp.einsum('rb,ab->ra', grads, weight, preferred_element_type=jnp.float32)  25.3 us
    dot_general x10, matrix products, matmul(): return jnp.dot(left, right, preferred_element_type=jnp.float32)  24.8 us
    dot_general x2, matrix products, attend_back(): jnp.einsum('hqk,qhd->khd', expo.astype(jnp.bfloat16), numer_grad, preferr...  21.1 us
    dot_general x10, matrix products, left_grad(): jnp.einsum('ra,rb->ab', inputs, grads, preferred_element_type=jnp.float32)  19.8 us
    dot_general x2, matrix products, attend(): jnp.einsum('hqk,khd->qhd', expo.astype(jnp.bfloat16), head_split(values),...  18.5 us

profile of v1, /device:TPU:0, one launch (start us, length us, event | category | flops | bytes accessed | tf_op | source)
XLA Modules:
  0.0 379.0 jit_solution(684940350634257128)
XLA Ops:
  14.6 78.7 %gather.1 = (bf16[4,2,2,2,16,8320]{5,4,3,2,1,0:T(8,128)(2,1)}, bf16[2,2,512,512]{3,2,1,0:T(8,128)(2,1)}) custom-call(bf16[16,512]{1,0:T(8,128)(2,1)} %refs_0_.1, bf16[16,512]{1,0:T(8,128)(2,1)} %refs_1_.1, bf16[16,512]{1,0:T(8,128)(2,1)} %refs_2_.1, bf16[16,512]{1,0:T(8,128)(2,1)} %refs_3_.1, bf16[16,512]{1,0:T(8,128)(2,1)} %refs_4_.1, ...), custom_call_target="tpu_custom_call" | custom-call | tf_op jit(solution)/shard_map/gather/pallas_call | solution.py:207
  103.3 3.2 slice.153
  106.5 3.5 reshape.359
  112.0 3.1 convolution_convert_fusion.3
  115.1 4.2 %convolution_convert_fusion.4 = bf16[2048,512]{0,1:T(8,128)(2,1)} fusion(bf16[2048,512]{1,0:T(8,128)(2,1)S(1)} %bitcast.227, bf16[512,8320]{1,0:T(8,128)(2,1)} %bitcast.143), kind=kOutput, calls=%fused_computation.24 | convolution fusion | flops 1074790400 | bytes 4718592 | tf_op jit(solution)/shard_map/dot_general | solution.py:483
  121.7 3.1 fusion.88
  128.7 15.1 %fusion = (f32[8,512]{1,0:T(8,128)S(1)}, f32[8,512,2048]{2,1,0:T(8,128)}) fusion(pred[512,2048]{1,0:T(8,128)(4,1)S(1)} %copy-done.18, bf16[512,8,64]{0,2,1:T(8,128)(2,1)S(1)} %bitcast.182, bf16[2048,8,64]{0,2,1:T(8,128)(2,1)S(1)} %bitcast.165), kind=kOutput, calls=%fused_computation.2 | convolution fusion | flops 1098903552 | bytes 37240832 | tf_op jit(solution)/shard_map/qhd,khd->hqk/dot_general | solution.py:495
  143.8 15.5 %fusion.90 = (bf16[512,8,64]{0,2,1:T(8,128)(2,1)S(1)}, f32[512,8,64]{0,2,1:T(8,128)}) fusion(f32[512,8]{0,1:T(8,128)S(1)} %bitcast.211, bf16[2048,8,64]{0,2,1:T(8,128)(2,1)} %bitcast.228, f32[8,512,2048]{2,1,0:T(8,128)} %get-tuple-element.173, pred[512,2048]{1,0:T(8,128)(4,1)S(1)} %copy-done.18), kind=kOutput, calls=%fused_computation.187 | convolution fusion | flops 1099431936 | bytes 38289408 | tf_op jit(solution)/shard_map/hqk,khd->qhd/dot_general | solution.py:504
  161.3 3.0 fusion.14
  167.7 2.9 fusion.6
  172.5 3.4 multiply_reduce_fusion
  187.9 15.3 %convolution_convert_fusion.2 = bf16[8,64,2048]{2,1,0:T(8,128)(2,1)} fusion(f32[8,512,2048]{2,1,0:T(8,128)} %get-tuple-element.173, pred[512,2048]{1,0:T(8,128)(4,1)} %fusion.7, bf16[512,8,64]{0,2,1:T(8,128)(2,1)} %bitcast.188, f32[512,8]{0,1:T(8,128)S(1)} %bitcast.212), kind=kOutput, calls=%fused_computation.22 | convolution fusion | flops 1100742656 | bytes 37240832 | tf_op jit(solution)/shard_map/hqk,qhd->khd/dot_general | solution.py:520
  203.3 21.0 %multiply_convert_fusion = bf16[8,512,2048]{2,1,0:T(8,128)(2,1)} fusion(f32[8,512,2048]{2,1,0:T(8,128)} %get-tuple-element.173, bf16[2048,8,64]{0,2,1:T(8,128)(2,1)} %bitcast.229, f32[8,512]{1,0:T(8,128)S(1)} %bitcast_divide_fusion.1, pred[512,2048]{1,0:T(8,128)(4,1)S(1)} %copy-done.19, bf16[512,8,64]{0,2,1:T(8,128)(2,1)S(1)} %bitcast.189, ...), kind=kOutput, calls=%fused_computation | convolution fusion | flops 1116471296 | bytes 54034432 | tf_op jit(solution)/shard_map/qhd,khd->hqk/dot_general | solution.py:515
  224.3 12.4 %fusion.23 = bf16[8,64,512]{2,1,0:T(8,128)(2,1)} fusion(bf16[2048,8,64]{0,2,1:T(8,128)(2,1)} %bitcast.166, bf16[8,512,2048]{2,1,0:T(8,128)(2,1)} %multiply_convert_fusion), kind=kOutput, calls=%fused_computation.53 | convolution fusion | flops 1074266112 | bytes 19398656 | tf_op jit(solution)/shard_map/hqk,khd->qhd/dot_general | solution.py:518
  236.7 10.4 %multiply_convert_fusion.2 = bf16[8,64,2048]{2,1,0:T(8,128)(2,1)} fusion(bf16[512,8,64]{0,2,1:T(8,128)(2,1)} %bitcast.183, bf16[8,512,2048]{2,1,0:T(8,128)(2,1)} %multiply_convert_fusion), kind=kOutput, calls=%fused_computation.13 | convolution fusion | flops 1075838976 | bytes 19398656 | tf_op jit(solution)/shard_map/hqk,qhd->khd/dot_general | solution.py:519
  247.1 2.7 multiply_reduce_fusion.1
  258.4 5.8 %convolution_convert_fusion.15 = bf16[8,64,512]{2,1,0:T(8,128)(2,1)} fusion(f32[8,512,512]{1,2,0:T(8,128)} %copy-done.38, pred[512,512]{0,1:T(8,128)(4,1)S(1)} %fusion.37, bf16[512,8,64]{0,2,1:T(8,128)(2,1)S(1)} %bitcast.186, f32[512,8]{0,1:T(8,128)} %bitcast.209), kind=kOutput, calls=%fused_computation.64 | convolution fusion | flops 275775488 | bytes 9715712 | tf_op jit(solution)/shard_map/hqk,qhd->khd/dot_general | solution.py:520
  264.2 5.6 %multiply_convert_fusion.1 = bf16[8,512,512]{1,2,0:T(8,128)(2,1)S(1)} fusion(f32[8,512,512]{1,2,0:T(8,128)} %copy-done.38, f32[8,512]{1,0:T(8,128)S(1)} %copy-done.34, pred[512,512]{0,1:T(8,128)(4,1)S(1)} %fusion.37, bf16[512,8,64]{0,2,1:T(8,128)(2,1)S(1)} %bitcast.231, bf16[512,8,64]{0,2,1:T(8,128)(2,1)} %bitcast.187, f32[512,8]{0,1:T(8,128)S(1)} %bitcast.210), kind=kOutput, calls=%fused_computation.4 | convolution fusion | flops 279707648 | bytes 13926400 | tf_op jit(solution)/shard_map/qhd,khd->hqk/dot_general | solution.py:515
  277.6 3.1 convolution_add_fusion
  285.2 2.5 copy.226
  292.2 4.3 %convolution_convert_fusion.5 = bf16[512,512]{0,1:T(8,128)(2,1)} fusion(bf16[2048,512]{0,1:T(8,128)(2,1)} %bitcast.167, bf16[2048,512]{1,0:T(8,128)(2,1)} %bitcast.225), kind=kOutput, calls=%fused_computation.54 | convolution fusion | flops 1074003968 | bytes 4718592 | tf_op jit(solution)/shard_map/ra,rb->ab/dot_general | solution.py:487
  296.5 3.6 convolution_convert_fusion.6
  311.4 3.3 copy-done.1
  314.6 60.2 %scatter.1 = (f32[16,8320]{1,0:T(8,128)S(1)}, f32[512,512]{1,0:T(8,128)S(1)}) custom-call(bf16[4,2,2,2,16,8320]{5,4,3,2,1,0:T(8,128)(2,1)} %bitcast.157, bf16[2,2,512,512]{3,2,1,0:T(8,128)(2,1)S(1)} %bitcast.134), custom_call_target="tpu_custom_call" | custom-call | tf_op jit(solution)/shard_map/scatter/pallas_call | solution.py:401
  (188 shorter events, 91.3 us)
Async XLA Ops:
  102.8 61.5 %copy-start.30 = (f32[512,1]{0,1:T(1,128)}, f32[512,1]{0,1:T(1,128)S(1)}, u32[]{:S(2)}) copy-start(f32[512,1]{0,1:T(1,128)S(1)} %copy.247) | copy-start | bytes 6148
  112.0 7.3 %copy-start.21 = (bf16[512,512]{1,0:T(8,128)(2,1)S(1)}, bf16[512,512]{1,0:T(8,128)(2,1)}, u32[]{:S(2)}) copy-start(bf16[512,512]{1,0:T(8,128)(2,1)} %convolution_convert_fusion.17) | copy-start | bytes 1572868
  112.0 7.3 %copy-start.23 = (bf16[512,512]{1,0:T(8,128)(2,1)S(1)}, bf16[512,512]{1,0:T(8,128)(2,1)}, u32[]{:S(2)}) copy-start(bf16[512,512]{1,0:T(8,128)(2,1)} %convolution_convert_fusion.18) | copy-start | bytes 1572868
  115.1 13.5 %copy-start.5 = (bf16[2048,512]{0,1:T(8,128)(2,1)}, bf16[2048,512]{0,1:T(8,128)(2,1)S(1)}, u32[]{:S(2)}) copy-start(bf16[2048,512]{0,1:T(8,128)(2,1)S(1)} %convolution_convert_fusion.3) | copy-start | bytes 6291460
  115.1 6.6 %copy-start.36 = (bf16[512,512]{1,0:T(8,128)(2,1)S(1)}, bf16[512,512]{1,0:T(8,128)(2,1)}, u32[]{:S(2)}) copy-start(bf16[512,512]{1,0:T(8,128)(2,1)} %convolution_convert_fusion.19) | copy-start | bytes 1572868
  121.7 5.2 %copy-start.38 = (f32[8,512,512]{1,2,0:T(8,128)}, f32[8,512,512]{1,2,0:T(8,128)S(1)}, u32[]{:S(2)}) copy-start(f32[8,512,512]{1,2,0:T(8,128)S(1)} %get-tuple-element.167) | copy-start | bytes 25165828
  121.7 133.2 %copy-start.32 = (f32[8,512]{1,0:T(8,128)}, f32[8,512]{1,0:T(8,128)S(1)}, u32[]{:S(2)}) copy-start(f32[8,512]{1,0:T(8,128)S(1)} %get-tuple-element.166) | copy-start | bytes 49156
  121.7 6.9 %copy-start.18 = (pred[512,2048]{1,0:T(8,128)(4,1)S(1)}, pred[512,2048]{1,0:T(8,128)(4,1)}, u32[]{:S(2)}) copy-start(pred[512,2048]{1,0:T(8,128)(4,1)} %fusion.7) | copy-start | bytes 3145732
  124.8 19.0 %copy-start.9 = (bf16[512,8,64]{0,2,1:T(8,128)(2,1)}, bf16[512,8,64]{0,2,1:T(8,128)(2,1)S(1)}, u32[]{:S(2)}) copy-start(bf16[512,8,64]{0,2,1:T(8,128)(2,1)S(1)} %get-tuple-element.168) | copy-start | bytes 1572868
  128.6 15.2 %copy-start.25 = (bf16[512,512]{0,1:T(8,128)(2,1)}, bf16[512,512]{0,1:T(8,128)(2,1)S(1)}, u32[]{:S(2)}) copy-start(bf16[512,512]{0,1:T(8,128)(2,1)S(1)} %convolution_convert_fusion.16) | copy-start | bytes 1572868
  159.3 6.7 %copy-start.26 = (bf16[512,8,64]{0,2,1:T(8,128)(2,1)}, bf16[512,8,64]{0,2,1:T(8,128)(2,1)S(1)}, u32[]{:S(2)}) copy-start(bf16[512,8,64]{0,2,1:T(8,128)(2,1)S(1)} %get-tuple-element.174) | copy-start | bytes 1572868
  175.9 6.6 %copy-start.27 = (bf16[512,8,64]{0,2,1:T(8,128)(2,1)S(1)}, bf16[512,8,64]{0,2,1:T(8,128)(2,1)}, u32[]{:S(2)}) copy-start(bf16[512,8,64]{0,2,1:T(8,128)(2,1)} %copy-done.26) | copy-start | bytes 1572868
  187.9 15.3 %copy-start.19 = (pred[512,2048]{1,0:T(8,128)(4,1)S(1)}, pred[512,2048]{1,0:T(8,128)(4,1)}, u32[]{:S(2)}) copy-start(pred[512,2048]{1,0:T(8,128)(4,1)} %fusion.7) | copy-start | bytes 3145732
  187.9 15.3 %copy-start.29 = (bf16[512,512]{0,1:T(8,128)(2,1)S(1)}, bf16[512,512]{0,1:T(8,128)(2,1)}, u32[]{:S(2)}) copy-start(bf16[512,512]{0,1:T(8,128)(2,1)} %get-tuple-element.182) | copy-start | bytes 1572868
  236.7 10.4 %copy-start.7 = (bf16[8,64,512]{2,1,0:T(8,128)(2,1)S(1)}, bf16[8,64,512]{2,1,0:T(8,128)(2,1)}, u32[]{:S(2)}) copy-start(bf16[8,64,512]{2,1,0:T(8,128)(2,1)} %fusion.23) | copy-start | bytes 1572868
  258.1 6.1 %copy-start.33 = (f32[8,512]{1,0:T(8,128)S(1)}, f32[8,512]{1,0:T(8,128)}, u32[]{:S(2)}) copy-start(f32[8,512]{1,0:T(8,128)} %copy-done.32) | copy-start | bytes 49156
  258.1 6.1 %copy-start.34 = (f32[8,512]{1,0:T(8,128)S(1)}, f32[8,512]{1,0:T(8,128)}, u32[]{:S(2)}) copy-start(f32[8,512]{1,0:T(8,128)} %bitcast_divide_fusion) | copy-start | bytes 49156
  258.4 5.8 %copy-start.37 = (bf16[512,512]{1,0:T(8,128)(2,1)S(1)}, bf16[512,512]{1,0:T(8,128)(2,1)}, u32[]{:S(2)}) copy-start(bf16[512,512]{1,0:T(8,128)(2,1)} %convolution_convert_fusion.19) | copy-start | bytes 1572868
  264.2 5.6 %copy-start.24 = (bf16[512,512]{1,0:T(8,128)(2,1)S(1)}, bf16[512,512]{1,0:T(8,128)(2,1)}, u32[]{:S(2)}) copy-start(bf16[512,512]{1,0:T(8,128)(2,1)} %convolution_convert_fusion.18) | copy-start | bytes 1572868
  264.2 7.0 %copy-start.22 = (bf16[512,512]{1,0:T(8,128)(2,1)S(1)}, bf16[512,512]{1,0:T(8,128)(2,1)}, u32[]{:S(2)}) copy-start(bf16[512,512]{1,0:T(8,128)(2,1)} %convolution_convert_fusion.17) | copy-start | bytes 1572868
  269.8 6.3 %copy-start.2 = (bf16[512,512]{1,0:T(8,128)(2,1)S(1)}, bf16[512,512]{1,0:T(8,128)(2,1)}, u32[]{:S(2)}) copy-start(bf16[512,512]{1,0:T(8,128)(2,1)} %param.22) | copy-start | bytes 1572868
  277.6 18.9 %copy-start = (bf16[8,64,2048]{2,1,0:T(8,128)(2,1)S(1)}, bf16[8,64,2048]{2,1,0:T(8,128)(2,1)}, u32[]{:S(2)}) copy-start(bf16[8,64,2048]{2,1,0:T(8,128)(2,1)} %multiply_convert_fusion.2) | copy-start | bytes 6291460
  304.2 5.2 %copy-start.13 = (bf16[512,512]{1,0:T(8,128)(2,1)S(1)}, bf16[512,512]{1,0:T(8,128)(2,1)}, u32[]{:S(2)}) copy-start(bf16[512,512]{1,0:T(8,128)(2,1)} %copy.218) | copy-start | bytes 1572868
  304.2 5.3 %copy-start.14 = (bf16[512,512]{1,0:T(8,128)(2,1)S(1)}, bf16[512,512]{1,0:T(8,128)(2,1)}, u32[]{:S(2)}) copy-start(bf16[512,512]{1,0:T(8,128)(2,1)} %copy.219) | copy-start | bytes 1572868
  (17 other events, 57.7 us)

commit v2 on v1

--- a/solution.py
+++ b/solution.py
@@ -524,7 +524,7 @@
             flat(dv).astype(jnp.bfloat16))
 
 
-def local(target_in, memory, out_grad, *rest):
+def plain(target_in, memory, out_grad, *rest):
     weights, (tgt_lens, src_lens, src_offsets) = rest[:16], rest[16:]
     member = lax.axis_index("mem")
     per_device = tgt_lens.shape[1] // lax.axis_size("mem")
@@ -532,8 +532,7 @@
     lengths, spans, offsets = pick(tgt_lens), pick(src_lens), pick(src_offsets)
     norms = jnp.stack(weights[10:], axis=1)
     norms = jnp.pad(norms, ((0, 0), (0, NORM - norms.shape[1])))
-    fast = two_by_two((lax.axis_size("dp"), lax.axis_size("mem")))
-    gathered, all_memory = (gather_all if fast else gather_any)(weights[:10], norms, memory)
+    gathered, all_memory = gather_any(weights[:10], norms, memory)
     W = gathered.reshape(512, LANES)
     mat = lambda i: W[:, NORM + SLAB * i : NORM + SLAB * (i + 1)]
     wsq, wsk, wsv, wso, wcq, wck, wcv, wco = [mat(i) for i in range(8)]
@@ -557,14 +556,11 @@
     a_b = after_self.astype(low)
     qc = matmul(a_b, wcq).astype(low)
     kc, vc = matmul(all_memory, wck).astype(low), matmul(all_memory, wcv).astype(low)
-    if fast:
-        o_c_f, tot_c = attend(qc, kc, vc, cross_low, cross_high)
-    else:
-        cut = lambda v: v.reshape((4, -1) + v.shape[1:])
-        o_c_f, tot_c = lax.map(
-            lambda p: attend(p[0], kc, vc, p[1], p[2]), (cut(qc), cut(cross_low), cut(cross_high))
-        )
-        o_c_f, tot_c = o_c_f.reshape(rows, -1), tot_c.reshape(rows, -1)
+    cut = lambda v: v.reshape((4, -1) + v.shape[1:])
+    o_c_f, tot_c = lax.map(
+        lambda p: attend(p[0], kc, vc, p[1], p[2]), (cut(qc), cut(cross_low), cut(cross_high))
+    )
+    o_c_f, tot_c = o_c_f.reshape(rows, -1), tot_c.reshape(rows, -1)
     o_c = o_c_f.astype(low)
     after_cross, pull_cross = jax.vjp(layer_norm, after_self + matmul(o_c, wco), gc, sc)
     c_b = after_cross.astype(low)
@@ -581,20 +577,18 @@
     d_cb = d_pre_cross.astype(low)
     g_wco = left_grad(o_c, d_cb)
     d_oc = back_through(d_cb, wco).astype(low)
-    if fast:
-        dq_c, dk_c, dv_c = attend_back(qc, kc, vc, cross_low, cross_high, d_oc, o_c_f, tot_c)
-    else:
-        def piece(carry, p):
-            dq, dk, dv = attend_back(p[0], kc, vc, p[1], p[2], p[3], p[4], p[5])
-            return (carry[0] + dk, carry[1] + dv), dq
-
-        empty = jnp.zeros(kc.shape, jnp.bfloat16)
-        (dk_c, dv_c), dq_c = lax.scan(
-            piece,
-            (empty, empty),
-            tuple(cut(v) for v in (qc, cross_low, cross_high, d_oc, o_c_f, tot_c)),
-        )
-        dq_c = dq_c.reshape(rows, -1)
+
+    def piece(carry, p):
+        dq, dk, dv = attend_back(p[0], kc, vc, p[1], p[2], p[3], p[4], p[5])
+        return (carry[0] + dk, carry[1] + dv), dq
+
+    empty = jnp.zeros(kc.shape, jnp.bfloat16)
+    (dk_c, dv_c), dq_c = lax.scan(
+        piece,
+        (empty, empty),
+        tuple(cut(v) for v in (qc, cross_low, cross_high, d_oc, o_c_f, tot_c)),
+    )
+    dq_c = dq_c.reshape(rows, -1)
     g_wcq, g_wck, g_wcv = left_grad(a_b, dq_c), left_grad(all_memory, dk_c), left_grad(all_memory, dv_c)
     mem_grad = back_through(dk_c, wck) + back_through(dv_c, wcv)
     d_pre_self, g_ga, g_sa = pull_self(d_pre_cross + back_through(dq_c, wcq))
@@ -608,12 +602,569 @@
     g_w2p = g_w2.reshape(32, 4, 16, SLAB).transpose(0, 2, 1, 3).reshape(512, 4 * SLAB)
     grads = jnp.concatenate([g.astype(low) for g in (n_g, g_wsq, g_wsk, g_wsv, g_wso, g_wcq, g_wck, g_wcv, g_wco, g_w1, g_w2p)], axis=1)
     part = lambda i, n=1: out[:, NORM + SLAB * i : NORM + SLAB * (i + n)]
-    if fast:
-        out, mem_out = scatter_all(grads.reshape(4, 2, 2, 2, 16, LANES), mem_grad.astype(low).reshape(2, 2, rows, SLAB))
-        w2_grad = jnp.concatenate([part(12 + k) for k in range(4)], axis=0)
-    else:
-        out, w2_grad, mem_out = scatter_any(grads, mem_grad.astype(low))
+    out, w2_grad, mem_out = scatter_any(grads, mem_grad.astype(low))
     return (final.astype(low), target_grad, mem_out) + tuple(part(i) for i in range(8)) + (part(8, 4), w2_grad) + tuple(out[:, i] for i in range(6))
+
+
+TILE = 128
+EPS = 1e-05
+HIDE = -1e30
+LOW = jnp.bfloat16
+F32 = jnp.float32
+DEV = 32
+CUT = NORM + 12 * SLAB
+
+
+def mm(a, b):
+    return jnp.dot(a, b, preferred_element_type=F32)
+
+
+def mmt(a, b):
+    return lax.dot_general(a, b, (((1,), (1,)), ((), ())), preferred_element_type=F32)
+
+
+def tmm(a, b):
+    return lax.dot_general(a, b, (((0,), (0,)), ((), ())), preferred_element_type=F32)
+
+
+def lane_iota(shape):
+    return lax.broadcasted_iota(jnp.int32, shape, len(shape) - 1)
+
+
+def row_iota(shape):
+    return lax.broadcasted_iota(jnp.int32, shape, 0)
+
+
+def halves():
+    lane = lane_iota((1, TILE))
+    even = jnp.where(lane < 64, 1.0, 0.0).astype(LOW)
+    odd = jnp.where(lane < 64, 0.0, 1.0).astype(LOW)
+    return even, odd
+
+
+def stacked(block, even, odd):
+    return jnp.concatenate([block * even, block * odd], axis=0)
+
+
+def fold(pair):
+    lane = lane_iota((TILE, TILE))
+    return jnp.where(lane < 64, pair[:TILE], pair[TILE:])
+
+
+def totals_block(even, odd):
+    wide = lambda v: jnp.broadcast_to(v, (TILE, TILE))
+    return jnp.concatenate([wide(even), wide(odd)], axis=0)
+
+
+def corr_block():
+    lane = lane_iota((TILE, TILE))
+    a = jnp.where(lane < 2, 1.0, 0.0).astype(LOW)
+    b = jnp.where((lane >= 64) & (lane < 66), 1.0, 0.0).astype(LOW)
+    return jnp.concatenate([a, b], axis=0)
+
+
+def tile_forward(rows, keys, bias, q, k, v, num, tot):
+    even, odd = halves()
+    ones = totals_block(even, odd)
+    bias2 = jnp.concatenate([bias, bias], axis=1)
+    for h in range(4):
+        cols = pl.ds(TILE * h, TILE)
+        s = mmt(q[rows, cols], stacked(k[keys, cols], even, odd))
+        e = jnp.exp(s + bias2).astype(LOW)
+        both = mm(e, jnp.concatenate([stacked(v[keys, cols], even, odd), ones], axis=1))
+        num[rows, cols] += both[:, :TILE]
+        tot[rows, cols] += both[:, TILE:]
+
+
+def tile_backward(rows, keys, bias, q, k, v, dnx, dq, dk, dv):
+    even, odd = halves()
+    ones = corr_block()
+    bias2 = jnp.concatenate([bias, bias], axis=1)
+    for h in range(4):
+        cols = pl.ds(TILE * h, TILE)
+        qb = q[rows, cols]
+        ks = stacked(k[keys, cols], even, odd)
+        e = jnp.exp(mmt(qb, ks) + bias2)
+        vs = jnp.concatenate([stacked(v[keys, cols], even, odd), ones], axis=1)
+        flow = mmt(dnx[rows, pl.ds(2 * TILE * h, 2 * TILE)], vs)
+        ds = (e * flow).astype(LOW)
+        dq[rows, cols] += mm(ds, ks)
+        dk[keys, cols] += fold(tmm(ds, qb))
+        dv[keys, cols] += fold(tmm(e.astype(LOW), dnx[rows, pl.ds(2 * TILE * h, TILE)]))
+
+
+def each(count, body):
+    def step(i, carry):
+        body(i)
+        return carry
+    lax.fori_loop(0, count, step, 0)
+
+
+def zero(ref, step=128):
+    def body(i):
+        rows = pl.ds(pl.multiple_of(i * step, step), step)
+        ref[rows] = jnp.zeros((step,) + ref.shape[1:], ref.dtype)
+    each(ref.shape[0] // step, body)
+
+
+def compute_kernel(lens_ref, spans_ref, offs_ref, target, out_grad, memory, gathered,
+                   layer_out, target_grad, grads, mem_grads,
+                   w, w2, x, og, mem, qs, ks, vs, qc, kc, vc, big, act, dhid, dv,
+                   num_s, tot_s, num_c, tot_c, xh1, xh2, t1, dpre, dq, rs1, rs2, low_s, o_b, oc_b, a_b, c_b,
+                   g_b, dnx, ng, gb, lout,
+                   starts, in_sem, w_sem, out_sem):
+    n_src = mem.shape[0]
+    rows_all = x.shape[0]
+    n_sent = starts.shape[0] - 1
+    member = lax.axis_index("mem")
+    base = member * n_sent
+
+    loads = {}
+
+    def load(name, src, dst, sem):
+        loads[name] = pltpu.make_async_copy(src, dst, sem)
+        loads[name].start()
+
+    load("x", target, x, in_sem.at[0])
+    load("norm", gathered.at[:, :, pl.ds(0, NORM)], w.at[:, :, pl.ds(0, NORM)], w_sem.at[12])
+    for i in range(3):
+        lanes = pl.ds(NORM + SLAB * i, SLAB)
+        load(i, gathered.at[:, :, lanes], w.at[:, :, lanes], w_sem.at[i])
+    load("mem", memory, mem, in_sem.at[1])
+    for i in (3, 5, 6, 4, 7):
+        lanes = pl.ds(NORM + SLAB * i, SLAB)
+        load(i, gathered.at[:, :, lanes], w.at[:, :, lanes], w_sem.at[i])
+    lanes = pl.ds(NORM + SLAB * 8, 4 * SLAB)
+    load("w1", gathered.at[:, :, lanes], w.at[:, :, lanes], w_sem.at[8])
+    for k in range(4):
+        load(("w2", k), gathered.at[:, :, pl.ds(CUT + SLAB * k, SLAB)], w2.at[:, k], w_sem.at[13 + k])
+    load("og", out_grad, og, in_sem.at[2])
+
+    outs = []
+
+    def send(src, dst):
+        copy = pltpu.make_async_copy(src, dst, out_sem.at[len(outs)])
+        copy.start()
+        outs.append(copy)
+
+    def weight(i, part=None, width=256):
+        if part is None:
+            return w[:, :, pl.ds(NORM + SLAB * i, SLAB)].reshape(SLAB, SLAB)
+        start = pl.multiple_of(NORM + SLAB * i + part * width, TILE)
+        return w[:, :, pl.ds(start, width)].reshape(SLAB, width)
+
+    def weight_rows(i, part, width=256, lanes=SLAB):
+        devs = pl.ds(pl.multiple_of(part * (width // ROWS), width // ROWS), width // ROWS)
+        return w[devs, :, pl.ds(NORM + SLAB * i, lanes)].reshape(width, lanes)
+
+    def put_weight(i, part, value, width=256):
+        start = pl.multiple_of(NORM + SLAB * i + part * width, TILE)
+        w[:, :, pl.ds(start, width)] = value.astype(LOW).reshape(DEV, ROWS, width)
+
+    def columns(part, width=256):
+        return pl.ds(pl.multiple_of(part * width, width), width)
+
+    def block(i, width=TILE):
+        return pl.ds(pl.multiple_of(i * width, width), width)
+
+    def count(j, at):
+        starts[j] = at
+        return at + lens_ref[0, base + j]
+    starts[n_sent] = lax.fori_loop(0, n_sent, count, jnp.int32(0))
+
+    def lows(i):
+        row = i * TILE + row_iota((TILE, TILE))
+
+        def pick(j, found):
+            return jnp.where(row >= starts[j], starts[j], found)
+        low_s[block(i)] = lax.fori_loop(0, n_sent, pick, jnp.zeros((TILE, TILE), jnp.int32))
+    each(rows_all // TILE, lows)
+    zero(num_s)
+    zero(tot_s)
+    zero(num_c)
+    zero(tot_c)
+    ng[...] = jnp.zeros_like(ng)
+
+    loads["norm"].wait()
+    gb[...] = jnp.transpose(w[:, :, pl.ds(0, NORM)].reshape(SLAB, NORM).astype(F32))[:8]
+    loads["x"].wait()
+    for i, dst in ((0, qs), (1, ks), (2, vs)):
+        loads[i].wait()
+
+        def project(n, i=i, dst=dst):
+            value = mm(x[...], weight(i, n)).astype(LOW)
+            dst[:, columns(n)] = value * jnp.asarray(0.125, LOW) if i == 0 else value
+        each(2, project)
+
+    def self_bias(i, kt):
+        key = kt * TILE + lane_iota((TILE, TILE))
+        row = i * TILE + row_iota((TILE, TILE))
+        return jnp.where((key >= low_s[block(i)]) & (key <= row), 0.0, HIDE)
+
+    def first_key(i):
+        def pick(j, found):
+            return jnp.where(starts[j] <= i * TILE, starts[j], found)
+        return lax.fori_loop(0, n_sent, pick, jnp.int32(0)) // TILE
+
+    def self_tiles(body):
+        def outer(i, carry):
+            def inner(kt, carry):
+                body(block(i), block(kt), self_bias(i, kt))
+                return carry
+            return lax.fori_loop(first_key(i), i + 1, inner, carry)
+        lax.fori_loop(0, rows_all // TILE, outer, 0)
+
+    def cross_tiles(body):
+        def outer(j, carry):
+            begin, end = starts[j], starts[j + 1]
+            low = offs_ref[0, base + j]
+            high = low + spans_ref[0, base + j]
+            at = pl.multiple_of(jnp.minimum((low // ROWS) * ROWS, n_src - TILE), ROWS)
+
+            def inner(b, carry):
+                key = at + lane_iota((TILE, TILE))
+                row = b * TILE + row_iota((TILE, TILE))
+                inside = (key >= low) & (key < high) & (row >= begin) & (row < end)
+                body(block(b), pl.ds(at, TILE), jnp.where(inside, 0.0, HIDE))
+                return carry
+            return lax.fori_loop(begin // TILE, (end - 1) // TILE + 1, inner, carry)
+        lax.fori_loop(0, n_sent, outer, 0)
+
+    self_tiles(lambda r, k, bias: tile_forward(r, k, bias, qs, ks, vs, num_s, tot_s))
+
+    def divide(num, tot, out):
+        def body(i):
+            r = block(i, 64)
+            o = num[r] / tot[r]
+            num[r] = o
+            out[r] = o.astype(LOW)
+        each(rows_all // 64, body)
+
+    divide(num_s, tot_s, o_b)
+
+    def normalize(y):
+        mean = jnp.mean(y, axis=1, keepdims=True)
+        centre = y - mean
+        r = lax.rsqrt(jnp.mean(centre * centre, axis=1, keepdims=True) + EPS)
+        return centre * r, r
+
+    def back_norm(u, gain, xh, r):
+        gu = u * gain
+        a = jnp.mean(gu, axis=1, keepdims=True)
+        b = jnp.mean(gu * xh, axis=1, keepdims=True)
+        return (gu - a - xh * b) * r
+
+    loads[3].wait()
+
+    def self_out(n):
+        t1[:, columns(n)] = x[:, columns(n)].astype(F32) + mm(o_b[...], weight(3, n))
+    each(2, self_out)
+
+    def norm_self(i):
+        r = block(i, 64)
+        xh, rs = normalize(t1[r])
+        xh1[r] = xh
+        rs1[r] = jnp.broadcast_to(rs, (64, TILE))
+        after = xh * gb[0:1] + gb[1:2]
+        t1[r] = after
+        a_b[r] = after.astype(LOW)
+    each(rows_all // 64, norm_self)
+
+    for i in (4, 5, 6):
+        loads[i].wait()
+    loads["mem"].wait()
+
+    def query(n):
+        qc[:, columns(n)] = mm(a_b[...], weight(4, n)).astype(LOW) * jnp.asarray(0.125, LOW)
+    each(2, query)
+
+    def keys(i):
+        r = block(i // 2, SLAB)
+        n = i % 2
+        kc[r, columns(n)] = mm(mem[r], weight(5, n)).astype(LOW)
+        vc[r, columns(n)] = mm(mem[r], weight(6, n)).astype(LOW)
+    each(2 * n_src // SLAB, keys)
+
+    cross_tiles(lambda r, k, bias: tile_forward(r, k, bias, qc, kc, vc, num_c, tot_c))
+    divide(num_c, tot_c, oc_b)
+    loads[7].wait()
+
+    def cross_out(n):
+        t1[:, columns(n)] += mm(oc_b[...], weight(7, n))
+    each(2, cross_out)
+
+    def norm_cross(i):
+        r = block(i, 64)
+        xh, rs = normalize(t1[r])
+        xh2[r] = xh
+        rs2[r] = jnp.broadcast_to(rs, (64, TILE))
+        after = xh * gb[2:3] + gb[3:4]
+        t1[r] = after
+        c_b[r] = after.astype(LOW)
+    each(rows_all // 64, norm_cross)
+
+    loads["w1"].wait()
+
+    def hidden(n):
+        v = mm(c_b[...], weight(8, n))
+        sig = 1.0 / (1.0 + jnp.exp(-v))
+        act[:, columns(n)] = (v * sig).astype(LOW)
+        big[block(n // 2, SLAB), columns(n % 2)] = sig * (1.0 + v * (1.0 - sig))
+    each(8, hidden)
+    for k in range(4):
+        loads[("w2", k)].wait()
+
+    def ffn_out(n):
+        cols = columns(n)
+        t1[:, cols] += mm(act[...], w2[:, :, :, cols].reshape(4 * SLAB, 256))
+    each(2, ffn_out)
+    loads["og"].wait()
+
+    def norm_ffn(i):
+        r = block(i, 64)
+        xh, rs = normalize(t1[r])
+        gain = gb[4:5]
+        lout[r] = (xh * gain + gb[5:6]).astype(LOW)
+        u = og[r].astype(F32)
+        ng[4:5] += jnp.sum(u * xh, axis=0, keepdims=True)
+        ng[5:6] += jnp.sum(u, axis=0, keepdims=True)
+        d = back_norm(u, gain, xh, rs)
+        dpre[r] = d
+        g_b[r] = d.astype(LOW)
+    each(rows_all // 64, norm_ffn)
+    send(lout, layer_out)
+
+    def hidden_back(n):
+        devs = pl.ds(pl.multiple_of(n * 4, 4), 4)
+        part = mmt(g_b[...], w2[devs].reshape(256, SLAB))
+        d = (part * big[block(n // 2, SLAB), columns(n % 2)]).astype(LOW)
+        dhid[:, columns(n)] = d
+        w2[devs] = tmm(act[:, columns(n)], g_b[...]).astype(LOW).reshape(4, 4, ROWS, SLAB)
+    each(8, hidden_back)
+    for k in range(4):
+        send(w2.at[:, k], grads.at[:, :, pl.ds(CUT + SLAB * k, SLAB)])
+
+    def input_back(n):
+        dpre[:, columns(n)] += mmt(dhid[...], weight_rows(8, n, 256, 4 * SLAB))
+    each(2, input_back)
+
+    def first_grad(n):
+        put_weight(8, n, tmm(c_b[...], dhid[:, columns(n)]))
+    each(8, first_grad)
+    lanes = pl.ds(NORM + SLAB * 8, 4 * SLAB)
+    send(w.at[:, :, lanes], grads.at[:, :, lanes])
+
+    def back_cross(i):
+        r = block(i, 64)
+        u, xh = dpre[r], xh2[r]
+        ng[2:3] += jnp.sum(u * xh, axis=0, keepdims=True)
+        ng[3:4] += jnp.sum(u, axis=0, keepdims=True)
+        d = back_norm(u, gb[2:3], xh, rs2[r][:, :1])
+        dpre[r] = d
+        g_b[r] = d.astype(LOW)
+    each(rows_all // 64, back_cross)
+
+    def out_back(i, o_low, num, tot):
+        lane = lane_iota((TILE, TILE))
+        same = jnp.where((lane < 64) == (row_iota((TILE, TILE)) < 64), 1.0, 0.0).astype(LOW)
+        half = lane % 64
+
+        def body(n):
+            up = mmt(g_b[...], weight_rows(i, n)).astype(LOW).astype(F32)
+            for h in range(2):
+                cols = pl.ds(pl.multiple_of(n * 256 + h * TILE, TILE), TILE)
+                wide = lambda k: pl.ds(pl.multiple_of(n * 512 + h * 256 + k * TILE, TILE), TILE)
+                d = up[:, h * TILE:(h + 1) * TILE]
+                t = tot[:, cols]
+                dnx[:, wide(0)] = (d / t).astype(LOW)
+                p = d * num[:, cols]
+                p1 = p.astype(LOW)
+                p2 = (p - p1.astype(F32)).astype(LOW)
+                corr = -(mm(p1, same) + mm(p2, same)) / t
+                c1 = corr.astype(LOW)
+                c2 = (corr - c1.astype(F32)).astype(LOW)
+                place = lane_iota(c1.shape) % 64
+                nothing = jnp.zeros_like(c1)
+                dnx[:, wide(1)] = jnp.where(place == 0, c1, jnp.where(place == 1, c2, nothing))
+        each(2, body)
+
+        def grad(n):
+            put_weight(i, n, tmm(o_low[...], g_b[:, columns(n)]))
+        each(2, grad)
+
+    def send_slab(i):
+        lanes = pl.ds(NORM + SLAB * i, SLAB)
+        send(w.at[:, :, lanes], grads.at[:, :, lanes])
+
+    out_back(7, oc_b, num_c, tot_c)
+    send_slab(7)
+    zero(dq)
+    zero(big)
+    zero(dv)
+    cross_tiles(lambda r, k, bias: tile_backward(r, k, bias, qc, kc, vc, dnx, dq, big, dv))
+
+    def scaled(src, dst, factor, step=64):
+        def body(i):
+            r = block(i, step)
+            dst[r] = (src[r] * factor).astype(LOW)
+        each(src.shape[0] // step, body)
+
+    scaled(dq, qc, 0.125)
+    scaled(big, kc, 1.0)
+    scaled(dv, vc, 1.0)
+
+    def query_back(n):
+        dpre[:, columns(n)] += mmt(qc[...], weight_rows(4, n))
+    each(2, query_back)
+
+    def query_grad(n):
+        put_weight(4, n, tmm(a_b[...], qc[:, columns(n)]))
+    each(2, query_grad)
+    send_slab(4)
+
+    def memory_back(i):
+        r = block(i // 2, SLAB)
+        n = i % 2
+        big[r, columns(n)] = mmt(kc[r], weight_rows(5, n)) + mmt(vc[r], weight_rows(6, n))
+    each(2 * n_src // SLAB, memory_back)
+
+    def memory_low(i):
+        r = block(i, SLAB)
+        dhid[:, pl.ds(0, SLAB)] = big[r].astype(LOW)
+        copy = pltpu.make_async_copy(dhid.at[:, pl.ds(0, SLAB)], mem_grads.at[r], in_sem.at[3])
+        copy.start()
+        copy.wait()
+    each(n_src // SLAB, memory_low)
+
+    def key_grad(n):
+        put_weight(5, n, tmm(mem[...], kc[:, columns(n)]))
+        put_weight(6, n, tmm(mem[...], vc[:, columns(n)]))
+    each(2, key_grad)
+    send_slab(5)
+    send_slab(6)
+
+    def back_self(i):
+        r = block(i, 64)
+        u, xh = dpre[r], xh1[r]
+        ng[0:1] += jnp.sum(u * xh, axis=0, keepdims=True)
+        ng[1:2] += jnp.sum(u, axis=0, keepdims=True)
+        d = back_norm(u, gb[0:1], xh, rs1[r][:, :1])
+        dpre[r] = d
+        g_b[r] = d.astype(LOW)
+    each(rows_all // 64, back_self)
+    out_back(3, o_b, num_s, tot_s)
+    send_slab(3)
+    zero(dq)
+    dk_s, dv_s = t1, dv.at[pl.ds(0, rows_all)]
+    zero(dk_s)
+    zero(dv_s)
+    self_tiles(lambda r, k, bias: tile_backward(r, k, bias, qs, ks, vs, dnx, dq, dk_s, dv_s))
+    scaled(dq, qs, 0.125)
+    scaled(dk_s, ks, 1.0)
+    scaled(dv_s, vs, 1.0)
+
+    def target_back(n):
+        total = mmt(qs[...], weight_rows(0, n)) + mmt(ks[...], weight_rows(1, n))
+        dpre[:, columns(n)] += total + mmt(vs[...], weight_rows(2, n))
+    each(2, target_back)
+    send(dpre, target_grad)
+    for i, src in ((0, qs), (1, ks), (2, vs)):
+        def grad(n, i=i, src=src):
+            put_weight(i, n, tmm(x[...], src[:, columns(n)]))
+        each(2, grad)
+        send_slab(i)
+    padded = jnp.concatenate([ng[...], jnp.zeros((NORM - 8, SLAB), F32)], axis=0)
+    w[:, :, pl.ds(0, NORM)] = jnp.transpose(padded).astype(LOW).reshape(DEV, ROWS, NORM)
+    send(w.at[:, :, pl.ds(0, NORM)], grads.at[:, :, pl.ds(0, NORM)])
+    for copy in outs:
+        copy.wait()
+
+
+def compute(lens, spans, offs, target, out_grad, memory, gathered):
+    rows, n_src = target.shape[0], memory.shape[0]
+    n_sent = 16
+    any_space = pl.BlockSpec(memory_space=pl.ANY)
+    smem = pl.BlockSpec(memory_space=pltpu.SMEM)
+    dma = pltpu.SemaphoreType.DMA
+    f32 = lambda *s: pltpu.VMEM(s, F32)
+    low = lambda *s: pltpu.VMEM(s, LOW)
+    return pl.pallas_call(
+        compute_kernel,
+        out_shape=(
+            jax.ShapeDtypeStruct((rows, SLAB), LOW),
+            jax.ShapeDtypeStruct((rows, SLAB), F32),
+            jax.ShapeDtypeStruct((DEV, ROWS, LANES), LOW),
+            jax.ShapeDtypeStruct((n_src, SLAB), LOW),
+        ),
+        in_specs=[smem] * 3 + [any_space] * 4,
+        out_specs=(any_space,) * 4,
+        scratch_shapes=[
+            low(DEV, ROWS, CUT),
+            low(DEV, 4, ROWS, SLAB),
+            low(rows, SLAB),
+            low(rows, SLAB),
+            low(n_src, SLAB),
+            low(rows, SLAB),
+            low(rows, SLAB),
+            low(rows, SLAB),
+            low(rows, SLAB),
+            low(n_src, SLAB),
+            low(n_src, SLAB),
+            f32(max(n_src, 4 * SLAB), SLAB),
+            low(rows, 4 * SLAB),
+            low(rows, 4 * SLAB),
+            f32(n_src, SLAB),
+            f32(rows, SLAB),
+            f32(rows, SLAB),
+            f32(rows, SLAB),
+            f32(rows, SLAB),
+            f32(rows, SLAB),
+            f32(rows, SLAB),
+            f32(rows, SLAB),
+            f32(rows, SLAB),
+            f32(rows, SLAB),
+            f32(rows, TILE),
+            f32(rows, TILE),
+            pltpu.VMEM((rows, TILE), jnp.int32),
+            low(rows, SLAB),
+            low(rows, SLAB),
+            low(rows, SLAB),
+            low(rows, SLAB),
+            low(rows, SLAB),
+            low(rows, 2 * SLAB),
+            f32(8, SLAB),
+            f32(8, SLAB),
+            low(rows, SLAB),
+            pltpu.SMEM((n_sent + 1,), jnp.int32),
+            dma((4,)),
+            dma((17,)),
+            dma((17,)),
+        ],
+        compiler_params=pltpu.CompilerParams(vmem_limit_bytes=60 << 20),
+        name="compute",
+    )(lens, spans, offs, target, out_grad, memory, gathered)
+
+
+def local(target_in, memory, out_grad, *rest):
+    fast = two_by_two((lax.axis_size("dp"), lax.axis_size("mem")))
+    if not fast:
+        return plain(target_in, memory, out_grad, *rest)
+    weights, tables = rest[:16], rest[16:]
+    norms = jnp.stack(weights[10:], axis=1)
+    norms = jnp.pad(norms, ((0, 0), (0, NORM - norms.shape[1])))
+    gathered, all_memory = gather_all(weights[:10], norms, memory)
+    layer_out, target_grad, grads, mem_grads = compute(*tables, target_in, out_grad, all_memory, gathered)
+    rows = target_in.shape[0]
+    out, mem_out = scatter_all(
+        grads.reshape(4, 2, 2, 2, ROWS, LANES), mem_grads.reshape(2, 2, rows, SLAB))
+    part = lambda i, n=1: out[:, NORM + SLAB * i : NORM + SLAB * (i + n)]
+    w2_grad = jnp.concatenate([part(12 + k) for k in range(4)], axis=0)
+    return (
+        (layer_out, target_grad, mem_out)
+        + tuple(part(i) for i in range(8))
+        + (part(8, 4), w2_grad)
+        + tuple(out[:, i] for i in range(6))
+    )
 
 
 def solution(mesh):

time: 386 us -> 248 us (0.64); the launches traced: 379 us -> 248 us
  matrix products: 179 us -> 0 us
  Pallas kernels: 139 us -> 237 us
  local copies, waits for them, and re-layouts: 47.7 us -> 9.85 us
  other arithmetic: 11.9 us -> 0.66 us
    dot_general x42 -> x0, matrix products: 179 us -> none  [the longest x2 26.6 us: attend_back(): jnp.einsum('qhd,khd->hqk', numer_grad, head_split(values), preferred_elem...]
    pallas_call x0 -> x1, Pallas kernels: none -> 98.2 us  [compute(): pl.pallas_call(compute_kernel, out_shape=(jax.ShapeDtypeStruct((rows, SLA...]
    convert_element_type x9 -> x0, local copies, waits for them, and re-layouts: 15.3 us -> none  [local(): g.astype(low)]
    unnamed x103 -> x3, local copies, waits for them, and re-layouts: 14.5 us -> 2.55 us
    reduce_sum x9 -> x0, other arithmetic: 5.19 us -> none  [the longest x3 2.81 us: layer_norm(): return centre * lax.rsqrt(spread + eps_norm) * gain + shift]
where the time goes in v2:
time: 248 us
  Pallas kernels  237 us (96%)
  local copies, waits for them, and re-layouts  9.85 us (4%)
    pallas_call x1, Pallas kernels, compute(): pl.pallas_call(compute_kernel, out_shape=(jax.ShapeDtypeStruct((rows, SLA...  98.2 us
    pallas_call x1, Pallas kernels, gather_all(): pl.pallas_call(kernel, out_shape=(jax.ShapeDtypeStruct((4, 2, 2, 2, ROWS,...  78.7 us
    pallas_call x1, Pallas kernels, scatter_all(): pl.pallas_call(scatter_kernel, out_shape=(jax.ShapeDtypeStruct((ROWS, LAN...  60.2 us

profile of v2, /device:TPU:0, one launch (start us, length us, event | category | flops | bytes accessed | tf_op | source)
XLA Modules:
  0.0 248.2 jit_solution(18440936085947958262)
XLA Ops:
  0.7 0.7 copy.47
  1.4 0.7 copy.48
  2.1 0.7 copy.49
  2.9 0.7 copy.50
  3.6 0.7 copy.51
  4.4 0.7 copy.52
  5.1 0.1 stack.27
  5.2 0.6 pad.4.refs_10_
  5.8 78.7 %gather.1 = (bf16[4,2,2,2,16,8320]{5,4,3,2,1,0:T(8,128)(2,1)}, bf16[2,2,512,512]{3,2,1,0:T(8,128)(2,1)}) custom-call(bf16[16,512]{1,0:T(8,128)(2,1)} %refs_0_.1, bf16[16,512]{1,0:T(8,128)(2,1)} %refs_1_.1, bf16[16,512]{1,0:T(8,128)(2,1)} %refs_2_.1, bf16[16,512]{1,0:T(8,128)(2,1)} %refs_3_.1, bf16[16,512]{1,0:T(8,128)(2,1)} %refs_4_.1, ...), custom_call_target="tpu_custom_call" | custom-call | tf_op jit(solution)/shard_map/gather/pallas_call | solution.py:207
  84.5 98.2 %compute.1 = (bf16[512,512]{1,0:T(8,128)(2,1)}, f32[512,512]{1,0:T(8,128)}, bf16[32,16,8320]{2,1,0:T(8,128)(2,1)}, bf16[2048,512]{1,0:T(8,128)(2,1)}) custom-call(s32[1,64]{1,0:T(1,128)} %lens_ref.1, s32[1,64]{1,0:T(1,128)} %spans_ref.1, s32[1,64]{1,0:T(1,128)} %offs_ref.1, bf16[512,512]{1,0:T(8,128)(2,1)} %target.1, bf16[512,512]{1,0:T(8,128)(2,1)} %out_grad.1, ...), custom_call_target="tpu_custom_call" | custom-call | tf_op jit(solution)/shard_map/compute/pallas_call | solution.py:1091
  182.7 0.0 copy-start
  182.7 1.6 copy-done
  184.3 60.2 %scatter.1 = (f32[16,8320]{1,0:T(8,128)S(1)}, f32[512,512]{1,0:T(8,128)S(1)}) custom-call(bf16[4,2,2,2,16,8320]{5,4,3,2,1,0:T(8,128)(2,1)} %bitcast.12, bf16[2,2,512,512]{3,2,1,0:T(8,128)(2,1)S(1)} %bitcast.10), custom_call_target="tpu_custom_call" | custom-call | tf_op jit(solution)/shard_map/scatter/pallas_call | solution.py:401
  244.5 0.8 slice_reduce_fusion
  245.2 0.7 slice.65
  245.9 0.7 fusion
  246.6 0.7 pad_maximum_fusion
  247.2 1.0 copy.54
Async XLA Ops:
  182.7 1.6 copy-start

commit v3 on v2

--- a/solution.py
+++ b/solution.py
@@ -1,3 +1,5 @@
+import functools
+
 import jax
 import jax.numpy as jnp
 from jax import lax
@@ -40,22 +42,28 @@
     )
 
 
-GATHER_ROUNDS = ((0, 640, 2176), (2176, 2688, 4224), (4224, 5248, 8320))
+def cuts(widths, share):
+    spans, at = [], 0
+    for tiles in widths:
+        n = tiles * 128
+        spans.append((at, at + max(1, round(tiles * share)) * 128, at + n))
+        at += n
+    assert at == LANES
+    return tuple(spans)
+
+
+GATHER_ROUNDS = cuts((33, 32), 0.25)
 
 
 def gather_kernel(*refs):
-    shards = refs[:11]
-    norm_ref, memory_ref = refs[11], refs[12]
-    out, mem_out = refs[13], refs[14]
-    local_sem, mem_local = refs[15], refs[16]
-    zs = refs[17:19]
-    first, second, across = refs[19:21], refs[21:23], refs[23:25]
-    mems = refs[25:27]
-    shards = shards[:10]
+    shards, norm_ref, memory_ref = refs[:10], refs[10], refs[11]
+    out, mem_out, local_sem, mem_local = refs[12:16]
+    z_sems, first_sems, second_sems = refs[16:18], refs[18:20], refs[20:22]
+    across, mems = refs[22:24], refs[24:26]
     z, x, y, c = here()
     xp, yp, cp_ = device(z, 1 - x, y, c), device(z, x, 1 - y, c), device(z, x, y, 1 - c)
-    zp = [device((z + k) % 4, x, y, c) for k in (1, 2, 3)]
     own = out.at[z, x, y, c]
+    rounds = range(len(GATHER_ROUNDS))
 
     local = []
 
@@ -74,158 +82,152 @@
         one.start()
     keep = pltpu.make_async_copy(memory_ref, mem_out.at[y, c], mem_local)
     keep.start()
-    greet([xp, yp, cp_] + zp)
+    zn = [device((z + k) % 4, x, y, c) for k in (1, 3)]
+    greet([xp, yp, cp_] + zn)
     for one in local:
         one.wait()
 
+    def column(slot):
+        return z if slot == 0 else (z - slot if slot < 4 else z + (slot - 3))
+
+    def there(slot):
+        return None if slot == 0 else (z >= slot if slot < 4 else z <= 6 - slot)
+
+    def both(a, b):
+        return b if a is None else (a if b is None else jnp.logical_and(a, b))
+
+    def guarded(cond, body):
+        if cond is None:
+            body()
+        else:
+            pl.when(cond)(body)
+
     sent = []
 
-    def go(copy):
-        copy.start()
-        sent.append(copy)
-
-    def zcopy(r, k, source_z):
+    def go(make, cond=None):
+        guarded(cond, lambda: make().start())
+        sent.append((cond, make))
+
+    def along(slot, r, up):
         a, _, b = GATHER_ROUNDS[r]
-        ref = out.at[source_z, x, y, c, :, pl.ds(a, b - a)]
-        return remote(ref, ref, zs, (r, k), zp[k])
-
-    def one(r, stage, part, zz, other, kk):
+        ref = out.at[column(slot), x, y, c, :, pl.ds(a, b - a)]
+        d = 0 if slot == 0 else (slot if slot < 4 else slot - 3)
+        peer = device((z + (1 if up else 3)) % 4, x, y, c)
+        return remote(ref, ref, z_sems, (0 if up else 1, d, r), peer)
+
+    def arrived(slot, r):
+        a, _, b = GATHER_ROUNDS[r]
+        ref = out.at[column(slot), x, y, c, :, pl.ds(a, b - a)]
+        up = slot < 4
+        index = (0 if up else 1, (slot if up else slot - 3) - 1, r)
+        return remote(ref, ref, z_sems, index, xp)
+
+    def first(slot, r, part, arriving=False):
         a, m, b = GATHER_ROUNDS[r]
-        lanes = pl.ds(a, m - a) if part == 0 else pl.ds(m, b - m)
+        zz = column(slot)
         if part == 0:
-            ref = out.at[zz, other, y, c, :, lanes]
-            peer = xp if stage == 0 else yp
+            ref = out.at[zz, (1 - x) if arriving else x, y, c, :, pl.ds(a, m - a)]
         else:
-            ref = out.at[zz, x, other, c, :, lanes]
-            peer = yp if stage == 0 else xp
-        if stage == 0:
-            return remote(ref, ref, first, (r, part, kk), peer)
-        return remote(ref, ref, second, (r, part, kk), peer)
-
-    def over(r, zz, xx, yy, cc, kk, part):
+            ref = out.at[zz, x, (1 - y) if arriving else y, c, :, pl.ds(m, b - m)]
+        return remote(ref, ref, first_sems, (slot, part, r), xp if part == 0 else yp)
+
+    def second(slot, r, part, hop, arriving=False):
         a, m, b = GATHER_ROUNDS[r]
-        lanes = pl.ds(a, m - a) if part == 0 else pl.ds(m, b - m)
-        ref = out.at[zz, xx, yy, cc, :, lanes]
-        return remote(ref, ref, across, (r, kk, part), cp_)
-
-    zz = [z, (z + 1) % 4, (z + 2) % 4, (z + 3) % 4]
-
+        zz = column(slot)
+        if part == 0:
+            side = (1 - x) if hop else x
+            ref = out.at[zz, side, (1 - y) if arriving else y, c, :, pl.ds(a, m - a)]
+        else:
+            side = (1 - y) if hop else y
+            ref = out.at[zz, (1 - x) if arriving else x, side, c, :, pl.ds(m, b - m)]
+        return remote(ref, ref, second_sems, (slot, part, hop, r), yp if part == 0 else xp)
+
+    def over(slot, r, arriving=False):
+        a, _, b = GATHER_ROUNDS[r]
+        ref = out.at[column(slot), :, :, (1 - c) if arriving else c, :, pl.ds(a, b - a)]
+        return remote(ref, ref, across, (slot, r), cp_)
+
+    def spread(slot, r):
+        cond = there(slot)
+        for part in (1, 0):
+            go(functools.partial(first, slot, r, part), cond)
+        for part in (1, 0):
+            go(functools.partial(second, slot, r, part, 0), cond)
+
+    def from_z(d):
+        for r in rounds:
+            for slot in (d, d + 3):
+                cond = there(slot)
+                guarded(cond, lambda slot=slot, r=r: arrived(slot, r).wait_recv())
+                if d < 3:
+                    onward = z < 3 if slot < 4 else z > 0
+                    go(functools.partial(along, slot, r, slot < 4), both(cond, onward))
+                spread(slot, r)
+
+    def pass_on(slots):
+        for r in rounds:
+            for slot in slots:
+                cond = there(slot)
+                for part in (1, 0):
+                    guarded(cond, lambda s=slot, r=r, p=part: first(s, r, p, True).wait_recv())
+                    go(functools.partial(second, slot, r, part, 1), cond)
+
+    def hand_over(slots):
+        for r in rounds:
+            for slot in slots:
+                cond = there(slot)
+                for part in (0, 1):
+                    for hop in (0, 1):
+                        guarded(cond, lambda s=slot, r=r, p=part, h=hop: second(s, r, p, h, True).wait_recv())
+                go(functools.partial(over, slot, r), cond)
+
+    for r in rounds:
+        go(functools.partial(along, 0, r, True), z < 3)
+        go(functools.partial(along, 0, r, False), z > 0)
+        spread(0, r)
     mem_own = mem_out.at[y, c]
-
-    def block(r, k, hop):
-        for part in (0, 1):
-            mine = x if part == 0 else y
-            go(one(r, 0, part, zz[k], mine, k))
-            go(one(r, 1, part, zz[k], mine, 2 * k))
-
-    rounds = range(len(GATHER_ROUNDS))
-    for r in rounds:
-        for k in range(3):
-            go(zcopy(r, k, z))
-        block(r, 0, 0)
-        if r == 0:
-            keep.wait()
-            go(remote(mem_own, mem_own, mems, 0, yp))
-            go(remote(mem_own, mem_own, mems, 1, cp_))
-    for r in rounds:
-        for part in (0, 1):
-            go(over(r, z, x, y, c, 0, part))
-
-    def arrive_z(r):
-        for j in (0, 2, 1):
-            k = 3 - j
-            zcopy(r, j, zz[k]).wait_recv()
-            block(r, k, 0)
-            for part in (0, 1):
-                go(over(r, zz[k], x, y, c, 4 * k, part))
-
-    def arrive_first(r):
-        for k in (0, 1, 3, 2):
-            for part in (0, 1):
-                theirs = (1 - x) if part == 0 else (1 - y)
-                one(r, 0, part, zz[k], theirs, k).wait_recv()
-                go(one(r, 1, part, zz[k], theirs, 2 * k + 1))
-                if part == 0:
-                    go(over(r, zz[k], 1 - x, y, c, 4 * k + 1, 0))
-                else:
-                    go(over(r, zz[k], x, 1 - y, c, 4 * k + 2, 1))
-
-    def arrive_second(r):
-        for k in (0, 1, 3, 2):
-            for h in (0, 1):
-                for part in (0, 1):
-                    if part == 0:
-                        xx = x if h == 0 else 1 - x
-                        a, m, b = GATHER_ROUNDS[r]
-                        ref = out.at[zz[k], xx, 1 - y, c, :, pl.ds(a, m - a)]
-                        remote(ref, ref, second, (r, 0, 2 * k + h), yp).wait_recv()
-                        go(over(r, zz[k], xx, 1 - y, c, 4 * k + 2 + h, 0))
-                    else:
-                        yy = y if h == 0 else 1 - y
-                        a, m, b = GATHER_ROUNDS[r]
-                        ref = out.at[zz[k], 1 - x, yy, c, :, pl.ds(m, b - m)]
-                        remote(ref, ref, second, (r, 1, 2 * k + h), xp).wait_recv()
-                        go(over(r, zz[k], 1 - x, yy, c, 4 * k + 1 + 2 * h, 1))
-
-    def arrive_over(r):
-        for k in range(4):
-            for o, (xx, yy) in enumerate(((x, y), (1 - x, y), (x, 1 - y), (1 - x, 1 - y))):
-                for part in (0, 1):
-                    over(r, zz[k], xx, yy, 1 - c, 4 * k + o, part).wait_recv()
-
-    arrive_z(0)
-    arrive_z(1)
-    arrive_first(0)
-    arrive_z(2)
-    arrive_first(1)
-    arrive_second(0)
-    there = mem_out.at[1 - y, c]
-    remote(there, there, mems, 0, yp).wait_recv()
-    go(remote(there, there, mems, 2, cp_))
-    arrive_first(2)
-    arrive_second(1)
-    arrive_over(0)
-    arrive_second(2)
-    arrive_over(1)
-    arrive_over(2)
-    across_own = mem_out.at[y, 1 - c]
-    remote(across_own, across_own, mems, 1, cp_).wait_recv()
-    across_far = mem_out.at[1 - y, 1 - c]
-    remote(across_far, across_far, mems, 2, cp_).wait_recv()
-    for copy in sent:
-        copy.wait_send()
+    from_z(1)
+    pass_on((0,))
+    from_z(2)
+    pass_on((1, 4))
+    hand_over((0,))
+    keep.wait()
+    go(lambda: remote(mem_own, mem_own, mems, 0, yp))
+    go(lambda: remote(mem_own, mem_own, mems, 1, cp_))
+    from_z(3)
+    pass_on((2, 5))
+    hand_over((1, 4))
+    far = mem_out.at[1 - y, c]
+    remote(far, far, mems, 0, yp).wait_recv()
+    go(lambda: remote(far, far, mems, 2, cp_))
+    pass_on((3, 6))
+    hand_over((2, 5))
+    hand_over((3, 6))
+    for slot in (0, 1, 4, 2, 5, 3, 6):
+        for r in rounds:
+            guarded(there(slot), lambda s=slot, r=r: over(s, r, True).wait_recv())
+    for i, side in ((1, y), (2, 1 - y)):
+        block = mem_out.at[side, 1 - c]
+        remote(block, block, mems, i, cp_).wait_recv()
+    for cond, make in sent:
+        guarded(cond, lambda make=make: make().wait_send())
 
 
 def gather_all(shards, norms, memory):
     any_space = pl.BlockSpec(memory_space=pl.ANY)
     dma = pltpu.SemaphoreType.DMA
     n = len(GATHER_ROUNDS)
-
-    def kernel(*refs):
-        gather_kernel(*refs[:10], None, *refs[10:])
-
+    both = lambda *s: [dma(s), dma(s)]
     gathered, whole_memory = pl.pallas_call(
-        kernel,
+        gather_kernel,
         out_shape=(
             jax.ShapeDtypeStruct((4, 2, 2, 2, ROWS, LANES), jnp.bfloat16),
             jax.ShapeDtypeStruct((2, 2) + memory.shape, jnp.bfloat16),
         ),
         in_specs=[any_space] * 12,
         out_specs=(any_space, any_space),
-        scratch_shapes=[
-            dma((14,)),
-            dma(()),
-            dma((n, 3)),
-            dma((n, 3)),
-            dma((n, 2, 4)),
-            dma((n, 2, 4)),
-            dma((n, 2, 8)),
-            dma((n, 2, 8)),
-            dma((n, 16, 2)),
-            dma((n, 16, 2)),
-            dma((3,)),
-            dma((3,)),
-        ],
+        scratch_shapes=[dma((14,)), dma(())]
+        + both(2, 3, n) + both(7, 2, n) + both(7, 2, 2, n) + both(7, n) + both(3),
         compiler_params=pltpu.CompilerParams(collective_id=1, has_side_effects=True),
         name="gather",
     )(*shards, norms, memory)
@@ -607,6 +609,8 @@
 
 
 TILE = 128
+RT = 256
+CHUNK = 256
 EPS = 1e-05
 HIDE = -1e30
 LOW = jnp.bfloat16
@@ -712,7 +716,8 @@
                    w, w2, x, og, mem, qs, ks, vs, qc, kc, vc, big, act, dhid, dv,
                    num_s, tot_s, num_c, tot_c, xh1, xh2, t1, dpre, dq, rs1, rs2, low_s, o_b, oc_b, a_b, c_b,
                    g_b, dnx, ng, gb, lout,
-                   starts, in_sem, w_sem, out_sem):
+                   low_c, high_c, memc, sel, idx,
+                   starts, packed, in_sem, w_sem, out_sem):
     n_src = mem.shape[0]
     rows_all = x.shape[0]
     n_sent = starts.shape[0] - 1
@@ -772,12 +777,23 @@
         return at + lens_ref[0, base + j]
     starts[n_sent] = lax.fori_loop(0, n_sent, count, jnp.int32(0))
 
+    def count_packed(j, at):
+        packed[j] = at
+        return at + spans_ref[0, base + j]
+    n_keys = lax.fori_loop(0, n_sent, count_packed, jnp.int32(0))
+    packed[n_sent] = n_keys
+    chunks = (n_keys + CHUNK - 1) // CHUNK
+
     def lows(i):
         row = i * TILE + row_iota((TILE, TILE))
+        nothing = jnp.zeros((TILE, TILE), jnp.int32)
 
         def pick(j, found):
-            return jnp.where(row >= starts[j], starts[j], found)
-        low_s[block(i)] = lax.fori_loop(0, n_sent, pick, jnp.zeros((TILE, TILE), jnp.int32))
+            here_on = row >= starts[j]
+            values = (starts[j], packed[j], packed[j + 1])
+            return tuple(jnp.where(here_on, v, f) for v, f in zip(values, found))
+        low_s[block(i)], low_c[block(i)], high_c[block(i)] = lax.fori_loop(
+            0, n_sent, pick, (nothing, nothing, nothing))
     each(rows_all // TILE, lows)
     zero(num_s)
     zero(tot_s)
@@ -796,39 +812,33 @@
             dst[:, columns(n)] = value * jnp.asarray(0.125, LOW) if i == 0 else value
         each(2, project)
 
-    def self_bias(i, kt):
-        key = kt * TILE + lane_iota((TILE, TILE))
-        row = i * TILE + row_iota((TILE, TILE))
-        return jnp.where((key >= low_s[block(i)]) & (key <= row), 0.0, HIDE)
-
-    def first_key(i):
+    def last_at(table, row):
         def pick(j, found):
-            return jnp.where(starts[j] <= i * TILE, starts[j], found)
-        return lax.fori_loop(0, n_sent, pick, jnp.int32(0)) // TILE
-
-    def self_tiles(body):
+            return jnp.where(starts[j] <= row, table(j), found)
+        return lax.fori_loop(0, n_sent, pick, jnp.int32(0))
+
+    def tiles(body, bias, first, last):
         def outer(i, carry):
             def inner(kt, carry):
-                body(block(i), block(kt), self_bias(i, kt))
+                body(block(i, RT), block(kt), bias(i, kt))
                 return carry
-            return lax.fori_loop(first_key(i), i + 1, inner, carry)
-        lax.fori_loop(0, rows_all // TILE, outer, 0)
+            return lax.fori_loop(first(i) // TILE, (last(i) - 1) // TILE + 1, inner, carry)
+        lax.fori_loop(0, rows_all // RT, outer, 0)
+
+    def self_tiles(body):
+        def bias(i, kt):
+            key = kt * TILE + lane_iota((RT, TILE))
+            row = i * RT + row_iota((RT, TILE))
+            return jnp.where((key >= low_s[block(i, RT)]) & (key <= row), 0.0, HIDE)
+        tiles(body, bias, lambda i: last_at(lambda j: starts[j], i * RT), lambda i: (i + 1) * RT)
 
     def cross_tiles(body):
-        def outer(j, carry):
-            begin, end = starts[j], starts[j + 1]
-            low = offs_ref[0, base + j]
-            high = low + spans_ref[0, base + j]
-            at = pl.multiple_of(jnp.minimum((low // ROWS) * ROWS, n_src - TILE), ROWS)
-
-            def inner(b, carry):
-                key = at + lane_iota((TILE, TILE))
-                row = b * TILE + row_iota((TILE, TILE))
-                inside = (key >= low) & (key < high) & (row >= begin) & (row < end)
-                body(block(b), pl.ds(at, TILE), jnp.where(inside, 0.0, HIDE))
-                return carry
-            return lax.fori_loop(begin // TILE, (end - 1) // TILE + 1, inner, carry)
-        lax.fori_loop(0, n_sent, outer, 0)
+        def bias(i, kt):
+            key = kt * TILE + lane_iota((RT, TILE))
+            r = block(i, RT)
+            return jnp.where((key >= low_c[r]) & (key < high_c[r]), 0.0, HIDE)
+        tiles(body, bias, lambda i: last_at(lambda j: packed[j], i * RT),
+              lambda i: last_at(lambda j: packed[j + 1], (i + 1) * RT - 1))
 
     self_tiles(lambda r, k, bias: tile_forward(r, k, bias, qs, ks, vs, num_s, tot_s))
 
@@ -878,12 +888,31 @@
         qc[:, columns(n)] = mm(a_b[...], weight(4, n)).astype(LOW) * jnp.asarray(0.125, LOW)
     each(2, query)
 
-    def keys(i):
-        r = block(i // 2, SLAB)
-        n = i % 2
-        kc[r, columns(n)] = mm(mem[r], weight(5, n)).astype(LOW)
-        vc[r, columns(n)] = mm(mem[r], weight(6, n)).astype(LOW)
-    each(2 * n_src // SLAB, keys)
+    def choose(ct):
+        r = block(ct, CHUNK)
+        for g in range(n_src // TILE):
+            hit = idx[r] == g * TILE + lane_iota((CHUNK, TILE))
+            sel[:, g * TILE:(g + 1) * TILE] = jnp.where(hit, 1.0, 0.0).astype(LOW)
+
+    def keys(ct):
+        r = block(ct, CHUNK)
+        key = ct * CHUNK + row_iota((CHUNK, TILE))
+
+        def pick(j, found):
+            return jnp.where(key >= packed[j], offs_ref[0, base + j] - packed[j] + key, found)
+        at = lax.fori_loop(0, n_sent, pick, jnp.zeros((CHUNK, TILE), jnp.int32))
+        idx[r] = jnp.where(key < n_keys, at, -1)
+        choose(ct)
+
+        def bring(n):
+            memc[r, columns(n)] = mm(sel[...], mem[:, columns(n)]).astype(LOW)
+        each(2, bring)
+
+        def project(n):
+            kc[r, columns(n)] = mm(memc[r], weight(5, n)).astype(LOW)
+            vc[r, columns(n)] = mm(memc[r], weight(6, n)).astype(LOW)
+        each(2, project)
+    each(chunks, keys)
 
     cross_tiles(lambda r, k, bias: tile_forward(r, k, bias, qc, kc, vc, num_c, tot_c))
     divide(num_c, tot_c, oc_b)
@@ -999,8 +1028,12 @@
     out_back(7, oc_b, num_c, tot_c)
     send_slab(7)
     zero(dq)
-    zero(big)
-    zero(dv)
+
+    def clear(ct):
+        r = block(ct, CHUNK)
+        big[r] = jnp.zeros((CHUNK, SLAB), F32)
+        dv[r] = jnp.zeros((CHUNK, SLAB), F32)
+    each(chunks, clear)
     cross_tiles(lambda r, k, bias: tile_backward(r, k, bias, qc, kc, vc, dnx, dq, big, dv))
 
     def scaled(src, dst, factor, step=64):
@@ -1010,8 +1043,6 @@
         each(src.shape[0] // step, body)
 
     scaled(dq, qc, 0.125)
-    scaled(big, kc, 1.0)
-    scaled(dv, vc, 1.0)
 
     def query_back(n):
         dpre[:, columns(n)] += mmt(qc[...], weight_rows(4, n))
@@ -1022,24 +1053,38 @@
     each(2, query_grad)
     send_slab(4)
 
-    def memory_back(i):
-        r = block(i // 2, SLAB)
-        n = i % 2
-        big[r, columns(n)] = mmt(kc[r], weight_rows(5, n)) + mmt(vc[r], weight_rows(6, n))
-    each(2 * n_src // SLAB, memory_back)
-
-    def memory_low(i):
-        r = block(i, SLAB)
-        dhid[:, pl.ds(0, SLAB)] = big[r].astype(LOW)
-        copy = pltpu.make_async_copy(dhid.at[:, pl.ds(0, SLAB)], mem_grads.at[r], in_sem.at[3])
-        copy.start()
-        copy.wait()
-    each(n_src // SLAB, memory_low)
-
-    def key_grad(n):
-        put_weight(5, n, tmm(mem[...], kc[:, columns(n)]))
-        put_weight(6, n, tmm(mem[...], vc[:, columns(n)]))
-    each(2, key_grad)
+    zero(num_c)
+    zero(tot_c)
+
+    def memory_back(ct):
+        r = block(ct, CHUNK)
+        kc[r] = big[r].astype(LOW)
+        vc[r] = dv[r].astype(LOW)
+
+        def key_grad(n):
+            cols = columns(n)
+            num_c[:, cols] += tmm(memc[r], kc[r, cols])
+            tot_c[:, cols] += tmm(memc[r], vc[r, cols])
+        each(2, key_grad)
+
+        def rows_grad(n):
+            memc[r, columns(n)] = (
+                mmt(kc[r], weight_rows(5, n)) + mmt(vc[r], weight_rows(6, n))).astype(LOW)
+        each(2, rows_grad)
+        choose(ct)
+
+        def spread(n):
+            rows = block(n, 256)
+            found = tmm(sel[:, columns(n)], memc[r]).astype(LOW)
+            mem[rows] = jnp.where(ct == 0, found, mem[rows] + found)
+        each(n_src // 256, spread)
+    each(chunks, memory_back)
+    send(mem, mem_grads)
+
+    def key_store(n):
+        put_weight(5, n, num_c[:, columns(n)])
+        put_weight(6, n, tot_c[:, columns(n)])
+    each(2, key_store)
     send_slab(5)
     send_slab(6)
 
@@ -1083,6 +1128,7 @@
 def compute(lens, spans, offs, target, out_grad, memory, gathered):
     rows, n_src = target.shape[0], memory.shape[0]
     n_sent = 16
+    n_keys = n_sent * 112
     any_space = pl.BlockSpec(memory_space=pl.ANY)
     smem = pl.BlockSpec(memory_space=pltpu.SMEM)
     dma = pltpu.SemaphoreType.DMA
@@ -1108,12 +1154,12 @@
             low(rows, SLAB),
             low(rows, SLAB),
             low(rows, SLAB),
-            low(n_src, SLAB),
-            low(n_src, SLAB),
-            f32(max(n_src, 4 * SLAB), SLAB),
+            low(n_keys, SLAB),
+            low(n_keys, SLAB),
+            f32(4 * SLAB, SLAB),
             low(rows, 4 * SLAB),
             low(rows, 4 * SLAB),
-            f32(n_src, SLAB),
+            f32(n_keys, SLAB),
             f32(rows, SLAB),
             f32(rows, SLAB),
             f32(rows, SLAB),
@@ -1135,6 +1181,12 @@
             f32(8, SLAB),
             f32(8, SLAB),
             low(rows, SLAB),
+            pltpu.VMEM((rows, TILE), jnp.int32),
+            pltpu.VMEM((rows, TILE), jnp.int32),
+            low(n_keys, SLAB),
+            low(CHUNK, n_src),
+            pltpu.VMEM((n_keys, TILE), jnp.int32),
+            pltpu.SMEM((n_sent + 1,), jnp.int32),
             pltpu.SMEM((n_sent + 1,), jnp.int32),
             dma((4,)),
             dma((17,)),

time: 248 us -> 195 us (0.79)
  Pallas kernels: 237 us -> 184 us
    pallas_call x1, Pallas kernels: 98.2 us -> 64.9 us  [compute(): pl.pallas_call(compute_kernel, out_shape=(jax.ShapeDtypeStruct((rows, SLA...]
    pallas_call x1, Pallas kernels: 78.7 us -> 59.1 us  [gather_all(): pl.pallas_call(gather_kernel, out_shape=(jax.ShapeDtypeStruct((4, 2, 2, 2...]
where the time goes in v3:
time: 195 us
  Pallas kernels  184 us (94%)
  local copies, waits for them, and re-layouts  9.85 us (5%)
    pallas_call x1, Pallas kernels, compute(): pl.pallas_call(compute_kernel, out_shape=(jax.ShapeDtypeStruct((rows, SLA...  64.9 us
    pallas_call x1, Pallas kernels, scatter_all(): pl.pallas_call(scatter_kernel, out_shape=(jax.ShapeDtypeStruct((ROWS, LAN...  59.7 us
    pallas_call x1, Pallas kernels, gather_all(): pl.pallas_call(gather_kernel, out_shape=(jax.ShapeDtypeStruct((4, 2, 2, 2...  59.1 us
    another operation x7, local copies, waits for them, and re-layouts, local(): norms = jnp.stack(weights[10:], axis=1)  4.56 us

profile of v3, /device:TPU:0, one launch (start us, length us, event | category | flops | bytes accessed | tf_op | source)
XLA Modules:
  0.0 194.9 jit_solution(14204360442628626925)
XLA Ops:
  0.7 0.7 copy.47
  1.4 0.7 copy.48
  2.1 0.7 copy.49
  2.9 0.7 copy.50
  3.6 0.7 copy.51
  4.4 0.7 copy.52
  5.1 0.1 stack.27
  5.2 0.6 pad.4.refs_10_
  5.8 59.1 %gather.1 = (bf16[4,2,2,2,16,8320]{5,4,3,2,1,0:T(8,128)(2,1)}, bf16[2,2,512,512]{3,2,1,0:T(8,128)(2,1)}) custom-call(bf16[16,512]{1,0:T(8,128)(2,1)} %refs_0_.1, bf16[16,512]{1,0:T(8,128)(2,1)} %refs_1_.1, bf16[16,512]{1,0:T(8,128)(2,1)} %refs_2_.1, bf16[16,512]{1,0:T(8,128)(2,1)} %refs_3_.1, bf16[16,512]{1,0:T(8,128)(2,1)} %refs_4_.1, ...), custom_call_target="tpu_custom_call" | custom-call | tf_op jit(solution)/shard_map/gather/pallas_call | solution.py:221
  64.9 64.9 %compute.1 = (bf16[512,512]{1,0:T(8,128)(2,1)}, f32[512,512]{1,0:T(8,128)}, bf16[32,16,8320]{2,1,0:T(8,128)(2,1)}, bf16[2048,512]{1,0:T(8,128)(2,1)}) custom-call(s32[1,64]{1,0:T(1,128)} %lens_ref.1, s32[1,64]{1,0:T(1,128)} %spans_ref.1, s32[1,64]{1,0:T(1,128)} %offs_ref.1, bf16[512,512]{1,0:T(8,128)(2,1)} %target.1, bf16[512,512]{1,0:T(8,128)(2,1)} %out_grad.1, ...), custom_call_target="tpu_custom_call" | custom-call | tf_op jit(solution)/shard_map/compute/pallas_call | solution.py:1137
  129.9 0.0 copy-start
  129.9 1.6 copy-done
  131.4 59.7 %scatter.1 = (f32[16,8320]{1,0:T(8,128)S(1)}, f32[512,512]{1,0:T(8,128)S(1)}) custom-call(bf16[4,2,2,2,16,8320]{5,4,3,2,1,0:T(8,128)(2,1)} %bitcast.12, bf16[2,2,512,512]{3,2,1,0:T(8,128)(2,1)S(1)} %bitcast.10), custom_call_target="tpu_custom_call" | custom-call | tf_op jit(solution)/shard_map/scatter/pallas_call | solution.py:403
  191.1 0.8 slice_reduce_fusion
  191.9 0.7 slice.65
  192.6 0.7 fusion
  193.2 0.7 pad_maximum_fusion
  193.9 1.0 copy.54
Async XLA Ops:
  129.9 1.6 copy-start

commit v4 on v3

--- a/solution.py
+++ b/solution.py
@@ -232,208 +232,6 @@
         name="gather",
     )(*shards, norms, memory)
     return gathered.reshape(32, ROWS, LANES), whole_memory.reshape(-1, SLAB)
-SCATTER_ROUNDS = ((4224, 4736, 6272), (6272, 6784, 8320), (2176, 2688, 4224), (0, 640, 2176))
-
-
-def scatter_kernel(grads, mem_grads, out, mem_out, acc, from_core, from_first, from_second, from_z,
-                   macc, mfrom_core, mfrom_y, own_sems, mown_sem, core_s, core_r, first_s, first_r,
-                   second_s, second_r, zs_s, zs_r, mem_s, mem_r):
-    z, x, y, c = here()
-    xp, yp, cp_ = device(z, 1 - x, y, c), device(z, x, 1 - y, c), device(z, x, y, 1 - c)
-    zp = [device((z + k) % 4, x, y, c) for k in (1, 2, 3)]
-    count = len(SCATTER_ROUNDS)
-    core_sems, first_sems, second_sems = (core_s, core_r), (first_s, first_r), (second_s, second_r)
-    z_sems, mem_sems = (zs_s, zs_r), (mem_s, mem_r)
-    sent = []
-
-    def go(copy):
-        copy.start()
-        sent.append(copy)
-
-    def span(r, part=None):
-        a, m, b = SCATTER_ROUNDS[r]
-        return {None: (a, b - a), 0: (a, m - a), 1: (m, b - m)}[part]
-
-    def own(r):
-        a, n = span(r)
-        return pltpu.make_async_copy(
-            grads.at[:, :, :, c, :, pl.ds(a, n)], acc.at[:, :, :, :, pl.ds(a, n)], own_sems.at[r])
-
-    def core(r):
-        a, n = span(r)
-        return remote(grads.at[:, :, :, 1 - c, :, pl.ds(a, n)],
-                      from_core.at[:, :, :, :, pl.ds(a, n)], core_sems, r, cp_)
-
-    def first(r, part):
-        lanes = pl.ds(*span(r, part))
-        src = acc.at[:, :, 1 - y, :, lanes] if part == 0 else acc.at[:, 1 - x, :, :, lanes]
-        return remote(src, from_first.at[:, :, :, lanes], first_sems, (r, part),
-                      yp if part == 0 else xp)
-
-    def second(r, part):
-        lanes = pl.ds(*span(r, part))
-        src = acc.at[:, 1 - x, y, :, lanes] if part == 0 else acc.at[:, x, 1 - y, :, lanes]
-        return remote(src, from_second.at[:, :, lanes], second_sems, (r, part),
-                      xp if part == 0 else yp)
-
-    def along(r, k):
-        lanes = pl.ds(*span(r))
-        return remote(acc.at[(z + k + 1) % 4, x, y, :, lanes], from_z.at[k, :, lanes], z_sems,
-                      (r, k), zp[k])
-
-    mem_own = pltpu.make_async_copy(mem_grads.at[:, c], macc, mown_sem)
-    mem_core = remote(mem_grads.at[:, 1 - c], mfrom_core, mem_sems, 0, cp_)
-    mem_far = remote(macc.at[1 - y], mfrom_y, mem_sems, 1, yp)
-
-    own(0).start()
-    mem_own.start()
-    for r in range(1, count):
-        own(r).start()
-    greet([xp, yp, cp_] + zp)
-    go(core(0))
-    go(mem_core)
-    for r in range(1, count):
-        go(core(r))
-
-    def add_core(r):
-        own(r).wait()
-        core(r).wait_recv()
-        for part in (0, 1):
-            lanes = pl.ds(*span(r, part))
-            for theirs in (True, False):
-                def body(zi, carry, part=part, lanes=lanes, theirs=theirs):
-                    for o in (0, 1):
-                        if part == 0:
-                            xi, yi = o, (1 - y) if theirs else y
-                        else:
-                            xi, yi = (1 - x) if theirs else x, o
-                        acc[zi, xi, yi, :, lanes] = (
-                            acc[zi, xi, yi, :, lanes] + from_core[zi, xi, yi, :, lanes])
-                    return carry
-                lax.fori_loop(0, 4, body, 0)
-                if theirs:
-                    go(first(r, part))
-
-    def add_first(r):
-        for part in (0, 1):
-            first(r, part).wait_recv()
-            lanes = pl.ds(*span(r, part))
-            for theirs in (True, False):
-                def body(zi, carry, part=part, lanes=lanes, theirs=theirs):
-                    if part == 0:
-                        xi, yi = (1 - x) if theirs else x, y
-                        slot = xi
-                    else:
-                        xi, yi = x, (1 - y) if theirs else y
-                        slot = yi
-                    acc[zi, xi, yi, :, lanes] = (
-                        acc[zi, xi, yi, :, lanes] + from_first[zi, slot, :, lanes])
-                    return carry
-                lax.fori_loop(0, 4, body, 0)
-                if theirs:
-                    go(second(r, part))
-
-    def add_second(r):
-        for part in (0, 1):
-            second(r, part).wait_recv()
-            lanes = pl.ds(*span(r, part))
-
-            def body(zi, carry, lanes=lanes):
-                acc[zi, x, y, :, lanes] = acc[zi, x, y, :, lanes] + from_second[zi, :, lanes]
-                return carry
-            lax.fori_loop(0, 4, body, 0)
-        for k in (1, 0, 2):
-            go(along(r, k))
-
-    def add_z(r):
-        lanes = pl.ds(*span(r))
-        total = acc[z, x, y, :, lanes].astype(jnp.float32)
-        for k in (0, 2, 1):
-            along(r, k).wait_recv()
-            total = total + from_z[k, :, lanes].astype(jnp.float32)
-        out[:, lanes] = total
-
-    def memory_core():
-        mem_own.wait()
-        mem_core.wait_recv()
-        for theirs in (True, False):
-            side = (1 - y) if theirs else y
-
-            def body(i, carry, side=side):
-                rows = pl.ds(pl.multiple_of(i * 64, 64), 64)
-                macc[side, rows] = macc[side, rows] + mfrom_core[side, rows]
-                return carry
-            lax.fori_loop(0, 8, body, 0)
-            if theirs:
-                go(mem_far)
-
-    def memory_end():
-        mem_far.wait_recv()
-
-        def body(i, carry):
-            rows = pl.ds(pl.multiple_of(i * 64, 64), 64)
-            mem_out[rows] = macc[y, rows].astype(jnp.float32) + mfrom_y[rows].astype(jnp.float32)
-            return carry
-        lax.fori_loop(0, 8, body, 0)
-
-    for t in range(count + 3):
-        if t < count:
-            add_core(t)
-        if t == 0:
-            memory_core()
-        if 0 <= t - 1 < count:
-            add_first(t - 1)
-        if 0 <= t - 2 < count:
-            add_second(t - 2)
-        if 0 <= t - 3 < count:
-            add_z(t - 3)
-        if t == 3:
-            memory_end()
-    for copy in sent:
-        copy.wait_send()
-
-
-def scatter_all(grads, mem_grads):
-    any_space = pl.BlockSpec(memory_space=pl.ANY)
-    vmem = pl.BlockSpec(memory_space=pltpu.VMEM)
-    dma = pltpu.SemaphoreType.DMA
-    n = len(SCATTER_ROUNDS)
-    rows = mem_grads.shape[2]
-    low = jnp.bfloat16
-    return pl.pallas_call(
-        scatter_kernel,
-        out_shape=(
-            jax.ShapeDtypeStruct((ROWS, LANES), jnp.float32),
-            jax.ShapeDtypeStruct((rows, SLAB), jnp.float32),
-        ),
-        in_specs=[any_space] * 2,
-        out_specs=(vmem, vmem),
-        scratch_shapes=[
-            pltpu.VMEM((4, 2, 2, ROWS, LANES), low),
-            pltpu.VMEM((4, 2, 2, ROWS, LANES), low),
-            pltpu.VMEM((4, 2, ROWS, LANES), low),
-            pltpu.VMEM((4, ROWS, LANES), low),
-            pltpu.VMEM((3, ROWS, LANES), low),
-            pltpu.VMEM((2, rows, SLAB), low),
-            pltpu.VMEM((2, rows, SLAB), low),
-            pltpu.VMEM((rows, SLAB), low),
-            dma((n,)),
-            dma(()),
-            dma((n,)),
-            dma((n,)),
-            dma((n, 2)),
-            dma((n, 2)),
-            dma((n, 2)),
-            dma((n, 2)),
-            dma((n, 3)),
-            dma((n, 3)),
-            dma((2,)),
-            dma((2,)),
-        ],
-        compiler_params=pltpu.CompilerParams(
-            collective_id=2, has_side_effects=True, vmem_limit_bytes=48 << 20),
-        name="scatter",
-    )(grads, mem_grads)
 
 
 def two_by_two(mesh_axes):
@@ -701,7 +499,11 @@
     def step(i, carry):
         body(i)
         return carry
-    lax.fori_loop(0, count, step, 0)
+    if isinstance(count, int) and count <= 2:
+        for i in range(count):
+            body(i)
+        return
+    lax.fori_loop(0, count, step, 0, unroll=8 if isinstance(count, int) else 1)
 
 
 def zero(ref, step=128):
@@ -711,13 +513,53 @@
     each(ref.shape[0] // step, body)
 
 
+def columns(part, width=256):
+    return pl.ds(pl.multiple_of(part * width, width), width)
+
+
+def block(i, width=TILE):
+    return pl.ds(pl.multiple_of(i * width, width), width)
+
+
+def back_norm(u, gain, xh, r):
+    gu = u * gain
+    a = jnp.mean(gu, axis=1, keepdims=True)
+    b = jnp.mean(gu * xh, axis=1, keepdims=True)
+    return (gu - a - xh * b) * r
+
+
+def out_back(g_b, weight_rows, num, tot, dnx):
+    lane = lane_iota((TILE, TILE))
+    same = jnp.where((lane < 64) == (row_iota((TILE, TILE)) < 64), 1.0, 0.0).astype(LOW)
+
+    def body(n):
+        up = mmt(g_b[...], weight_rows(n)).astype(LOW).astype(F32)
+        for h in range(2):
+            cols = pl.ds(pl.multiple_of(n * 256 + h * TILE, TILE), TILE)
+            wide = lambda k: pl.ds(pl.multiple_of(n * 512 + h * 256 + k * TILE, TILE), TILE)
+            d = up[:, h * TILE:(h + 1) * TILE]
+            t = tot[:, cols]
+            dnx[:, wide(0)] = (d / t).astype(LOW)
+            p = d * num[:, cols]
+            p1 = p.astype(LOW)
+            p2 = (p - p1.astype(F32)).astype(LOW)
+            corr = -(mm(p1, same) + mm(p2, same)) / t
+            c1 = corr.astype(LOW)
+            c2 = (corr - c1.astype(F32)).astype(LOW)
+            place = lane_iota(c1.shape) % 64
+            nothing = jnp.zeros_like(c1)
+            dnx[:, wide(1)] = jnp.where(place == 0, c1, jnp.where(place == 1, c2, nothing))
+    each(2, body)
+
+
 def compute_kernel(lens_ref, spans_ref, offs_ref, target, out_grad, memory, gathered,
-                   layer_out, target_grad, grads, mem_grads,
+                   layer_out, grads, mem_grads, *rest):
+    (dpre_out, xh1_out, rs1_out, num_out, tot_out, q_out, k_out, v_out, o_out, gb_out, ng_out, low_out,
                    w, w2, x, og, mem, qs, ks, vs, qc, kc, vc, big, act, dhid, dv,
                    num_s, tot_s, num_c, tot_c, xh1, xh2, t1, dpre, dq, rs1, rs2, low_s, o_b, oc_b, a_b, c_b,
                    g_b, dnx, ng, gb, lout,
                    low_c, high_c, memc, sel, idx,
-                   starts, packed, in_sem, w_sem, out_sem):
+     starts, packed, in_sem, w_sem, out_sem) = rest
     n_src = mem.shape[0]
     rows_all = x.shape[0]
     n_sent = starts.shape[0] - 1
@@ -766,12 +608,6 @@
         start = pl.multiple_of(NORM + SLAB * i + part * width, TILE)
         w[:, :, pl.ds(start, width)] = value.astype(LOW).reshape(DEV, ROWS, width)
 
-    def columns(part, width=256):
-        return pl.ds(pl.multiple_of(part * width, width), width)
-
-    def block(i, width=TILE):
-        return pl.ds(pl.multiple_of(i * width, width), width)
-
     def count(j, at):
         starts[j] = at
         return at + lens_ref[0, base + j]
@@ -851,18 +687,15 @@
         each(rows_all // 64, body)
 
     divide(num_s, tot_s, o_b)
+    for src, dst in ((num_s, num_out), (tot_s, tot_out), (qs, q_out), (ks, k_out), (vs, v_out),
+                     (o_b, o_out), (gb, gb_out), (low_s, low_out)):
+        send(src, dst)
 
     def normalize(y):
         mean = jnp.mean(y, axis=1, keepdims=True)
         centre = y - mean
         r = lax.rsqrt(jnp.mean(centre * centre, axis=1, keepdims=True) + EPS)
         return centre * r, r
-
-    def back_norm(u, gain, xh, r):
-        gu = u * gain
-        a = jnp.mean(gu, axis=1, keepdims=True)
-        b = jnp.mean(gu * xh, axis=1, keepdims=True)
-        return (gu - a - xh * b) * r
 
     loads[3].wait()
 
@@ -880,6 +713,8 @@
         a_b[r] = after.astype(LOW)
     each(rows_all // 64, norm_self)
 
+    send(xh1, xh1_out)
+    send(rs1, rs1_out)
     for i in (4, 5, 6):
         loads[i].wait()
     loads["mem"].wait()
@@ -993,39 +828,16 @@
         g_b[r] = d.astype(LOW)
     each(rows_all // 64, back_cross)
 
-    def out_back(i, o_low, num, tot):
-        lane = lane_iota((TILE, TILE))
-        same = jnp.where((lane < 64) == (row_iota((TILE, TILE)) < 64), 1.0, 0.0).astype(LOW)
-        half = lane % 64
-
-        def body(n):
-            up = mmt(g_b[...], weight_rows(i, n)).astype(LOW).astype(F32)
-            for h in range(2):
-                cols = pl.ds(pl.multiple_of(n * 256 + h * TILE, TILE), TILE)
-                wide = lambda k: pl.ds(pl.multiple_of(n * 512 + h * 256 + k * TILE, TILE), TILE)
-                d = up[:, h * TILE:(h + 1) * TILE]
-                t = tot[:, cols]
-                dnx[:, wide(0)] = (d / t).astype(LOW)
-                p = d * num[:, cols]
-                p1 = p.astype(LOW)
-                p2 = (p - p1.astype(F32)).astype(LOW)
-                corr = -(mm(p1, same) + mm(p2, same)) / t
-                c1 = corr.astype(LOW)
-                c2 = (corr - c1.astype(F32)).astype(LOW)
-                place = lane_iota(c1.shape) % 64
-                nothing = jnp.zeros_like(c1)
-                dnx[:, wide(1)] = jnp.where(place == 0, c1, jnp.where(place == 1, c2, nothing))
-        each(2, body)
-
-        def grad(n):
-            put_weight(i, n, tmm(o_low[...], g_b[:, columns(n)]))
-        each(2, grad)
+    out_back(g_b, lambda n: weight_rows(7, n), num_c, tot_c, dnx)
+
+    def out_grad_store(n):
+        put_weight(7, n, tmm(oc_b[...], g_b[:, columns(n)]))
+    each(2, out_grad_store)
 
     def send_slab(i):
         lanes = pl.ds(NORM + SLAB * i, SLAB)
         send(w.at[:, :, lanes], grads.at[:, :, lanes])
 
-    out_back(7, oc_b, num_c, tot_c)
     send_slab(7)
     zero(dq)
 
@@ -1047,6 +859,8 @@
     def query_back(n):
         dpre[:, columns(n)] += mmt(qc[...], weight_rows(4, n))
     each(2, query_back)
+
+    send(dpre, dpre_out)
 
     def query_grad(n):
         put_weight(4, n, tmm(a_b[...], qc[:, columns(n)]))
@@ -1088,41 +902,27 @@
     send_slab(5)
     send_slab(6)
 
-    def back_self(i):
-        r = block(i, 64)
-        u, xh = dpre[r], xh1[r]
-        ng[0:1] += jnp.sum(u * xh, axis=0, keepdims=True)
-        ng[1:2] += jnp.sum(u, axis=0, keepdims=True)
-        d = back_norm(u, gb[0:1], xh, rs1[r][:, :1])
-        dpre[r] = d
-        g_b[r] = d.astype(LOW)
-    each(rows_all // 64, back_self)
-    out_back(3, o_b, num_s, tot_s)
-    send_slab(3)
-    zero(dq)
-    dk_s, dv_s = t1, dv.at[pl.ds(0, rows_all)]
-    zero(dk_s)
-    zero(dv_s)
-    self_tiles(lambda r, k, bias: tile_backward(r, k, bias, qs, ks, vs, dnx, dq, dk_s, dv_s))
-    scaled(dq, qs, 0.125)
-    scaled(dk_s, ks, 1.0)
-    scaled(dv_s, vs, 1.0)
-
-    def target_back(n):
-        total = mmt(qs[...], weight_rows(0, n)) + mmt(ks[...], weight_rows(1, n))
-        dpre[:, columns(n)] += total + mmt(vs[...], weight_rows(2, n))
-    each(2, target_back)
-    send(dpre, target_grad)
-    for i, src in ((0, qs), (1, ks), (2, vs)):
-        def grad(n, i=i, src=src):
-            put_weight(i, n, tmm(x[...], src[:, columns(n)]))
-        each(2, grad)
-        send_slab(i)
-    padded = jnp.concatenate([ng[...], jnp.zeros((NORM - 8, SLAB), F32)], axis=0)
-    w[:, :, pl.ds(0, NORM)] = jnp.transpose(padded).astype(LOW).reshape(DEV, ROWS, NORM)
-    send(w.at[:, :, pl.ds(0, NORM)], grads.at[:, :, pl.ds(0, NORM)])
+    send(ng, ng_out)
     for copy in outs:
         copy.wait()
+
+
+def state_shapes(rows):
+    full = lambda dtype, lanes=SLAB, n=rows: jax.ShapeDtypeStruct((n, lanes), dtype)
+    return (
+        full(F32),
+        full(F32),
+        full(F32, TILE),
+        full(F32),
+        full(F32),
+        full(LOW),
+        full(LOW),
+        full(LOW),
+        full(LOW),
+        full(F32, SLAB, 8),
+        full(F32, SLAB, 8),
+        full(jnp.int32, TILE),
+    )
 
 
 def compute(lens, spans, offs, target, out_grad, memory, gathered):
@@ -1138,12 +938,11 @@
         compute_kernel,
         out_shape=(
             jax.ShapeDtypeStruct((rows, SLAB), LOW),
-            jax.ShapeDtypeStruct((rows, SLAB), F32),
             jax.ShapeDtypeStruct((DEV, ROWS, LANES), LOW),
             jax.ShapeDtypeStruct((n_src, SLAB), LOW),
-        ),
+        ) + state_shapes(rows),
         in_specs=[smem] * 3 + [any_space] * 4,
-        out_specs=(any_space,) * 4,
+        out_specs=(any_space,) * 15,
         scratch_shapes=[
             low(DEV, ROWS, CUT),
             low(DEV, 4, ROWS, SLAB),
@@ -1190,11 +989,333 @@
             pltpu.SMEM((n_sent + 1,), jnp.int32),
             dma((4,)),
             dma((17,)),
-            dma((17,)),
+            dma((32,)),
         ],
         compiler_params=pltpu.CompilerParams(vmem_limit_bytes=60 << 20),
         name="compute",
     )(lens, spans, offs, target, out_grad, memory, gathered)
+def scatter_rounds(share=0.25):
+    spans = []
+    for at, tiles in ((33, 6), (39, 12), (51, 14), (17, 16), (0, 11), (11, 6)):
+        split = at + max(1, round(tiles * share))
+        spans.append((at * 128, split * 128, (at + tiles) * 128))
+    return tuple(spans)
+
+
+SCATTER_ROUNDS = scatter_rounds()
+SELF_LANES = NORM + 4 * SLAB
+SELF_ROUNDS = (4, 5)
+
+
+def scatter_kernel(grads, mem_grads, gathered, target, *rest):
+    state, (out, mem_out, target_grad), rest = rest[:12], rest[12:15], rest[15:]
+    (acc, from_core, from_first, from_second, from_z, macc, mfrom_core, mfrom_y), rest = rest[:8], rest[8:]
+    held, rest = rest[:12], rest[12:]
+    (w, tgt, gs, dq, dk, dv, dnx, g_b), rest = rest[:8], rest[8:]
+    (own_sems, mown_sem, state_sems, core_s, core_r, first_s, first_r,
+     second_s, second_r, zs_s, zs_r, mem_s, mem_r) = rest
+    dpre, xh1, rs1, num_s, tot_s, qs, ks, vs, o_b, gb, ng, low_s = held
+    z, x, y, c = here()
+    xp, yp, cp_ = device(z, 1 - x, y, c), device(z, x, 1 - y, c), device(z, x, y, 1 - c)
+    zp = [device((z + k) % 4, x, y, c) for k in (1, 2, 3)]
+    count = len(SCATTER_ROUNDS)
+    core_sems, first_sems, second_sems = (core_s, core_r), (first_s, first_r), (second_s, second_r)
+    z_sems, mem_sems = (zs_s, zs_r), (mem_s, mem_r)
+    sent = []
+
+    def go(copy):
+        copy.start()
+        sent.append(copy)
+
+    def span(r, part=None):
+        a, m, b = SCATTER_ROUNDS[r]
+        return {None: (a, b - a), 0: (a, m - a), 1: (m, b - m)}[part]
+
+    def own(r):
+        a, n = span(r)
+        return pltpu.make_async_copy(
+            grads.at[:, :, :, c, :, pl.ds(a, n)], acc.at[:, :, :, :, pl.ds(a, n)], own_sems.at[r])
+
+    def core(r):
+        a, n = span(r)
+        source = gs if r in SELF_ROUNDS else grads
+        return remote(source.at[:, :, :, 1 - c, :, pl.ds(a, n)],
+                      from_core.at[:, :, :, :, pl.ds(a, n)], core_sems, r, cp_)
+
+    def first(r, part):
+        lanes = pl.ds(*span(r, part))
+        src = acc.at[:, :, 1 - y, :, lanes] if part == 0 else acc.at[:, 1 - x, :, :, lanes]
+        return remote(src, from_first.at[:, :, :, lanes], first_sems, (r, part),
+                      yp if part == 0 else xp)
+
+    def second(r, part):
+        lanes = pl.ds(*span(r, part))
+        src = acc.at[:, 1 - x, y, :, lanes] if part == 0 else acc.at[:, x, 1 - y, :, lanes]
+        return remote(src, from_second.at[:, :, lanes], second_sems, (r, part),
+                      xp if part == 0 else yp)
+
+    def along(r, k):
+        lanes = pl.ds(*span(r))
+        return remote(acc.at[(z + k + 1) % 4, x, y, :, lanes], from_z.at[k, :, lanes], z_sems,
+                      (r, k), zp[k])
+
+    mem_own = pltpu.make_async_copy(mem_grads.at[:, c], macc, mown_sem)
+    mem_core = remote(mem_grads.at[:, 1 - c], mfrom_core, mem_sems, 0, cp_)
+    mem_far = remote(macc.at[1 - y], mfrom_y, mem_sems, 1, yp)
+
+    def bring(i, src, dst):
+        copy = pltpu.make_async_copy(src, dst, state_sems.at[i])
+        copy.start()
+        return copy
+
+    early = [r for r in range(count) if r not in SELF_ROUNDS]
+    own(0).start()
+    mem_own.start()
+    for r in early[1:]:
+        own(r).start()
+    copies = [bring(i, src, dst) for i, (src, dst) in enumerate(zip(state, held))]
+    copies.append(bring(12, gathered.at[:, :, pl.ds(NORM, 4 * SLAB)], w))
+    copies.append(bring(13, target, tgt))
+    greet([xp, yp, cp_] + zp)
+    go(core(early[0]))
+    go(mem_core)
+    for r in early[1:]:
+        go(core(r))
+
+    def add_core(r):
+        if r not in SELF_ROUNDS:
+            own(r).wait()
+        core(r).wait_recv()
+        for part in (0, 1):
+            lanes = pl.ds(*span(r, part))
+            for theirs in (True, False):
+                def body(zi, carry, part=part, lanes=lanes, theirs=theirs):
+                    for o in (0, 1):
+                        if part == 0:
+                            xi, yi = o, (1 - y) if theirs else y
+                        else:
+                            xi, yi = (1 - x) if theirs else x, o
+                        mine = gs[zi, xi, yi, c, :, lanes] if r in SELF_ROUNDS else acc[zi, xi, yi, :, lanes]
+                        acc[zi, xi, yi, :, lanes] = mine + from_core[zi, xi, yi, :, lanes]
+                    return carry
+                lax.fori_loop(0, 4, body, 0)
+                if theirs:
+                    go(first(r, part))
+
+    def add_first(r):
+        for part in (0, 1):
+            first(r, part).wait_recv()
+            lanes = pl.ds(*span(r, part))
+            for theirs in (True, False):
+                def body(zi, carry, part=part, lanes=lanes, theirs=theirs):
+                    if part == 0:
+                        xi, yi = (1 - x) if theirs else x, y
+                        slot = xi
+                    else:
+                        xi, yi = x, (1 - y) if theirs else y
+                        slot = yi
+                    acc[zi, xi, yi, :, lanes] = (
+                        acc[zi, xi, yi, :, lanes] + from_first[zi, slot, :, lanes])
+                    return carry
+                lax.fori_loop(0, 4, body, 0)
+                if theirs:
+                    go(second(r, part))
+
+    def add_second(r):
+        for part in (0, 1):
+            second(r, part).wait_recv()
+            lanes = pl.ds(*span(r, part))
+
+            def body(zi, carry, lanes=lanes):
+                acc[zi, x, y, :, lanes] = acc[zi, x, y, :, lanes] + from_second[zi, :, lanes]
+                return carry
+            lax.fori_loop(0, 4, body, 0)
+        for k in (1, 0, 2):
+            go(along(r, k))
+
+    def add_z(r):
+        lanes = pl.ds(*span(r))
+        total = acc[z, x, y, :, lanes].astype(jnp.float32)
+        for k in (0, 2, 1):
+            along(r, k).wait_recv()
+            total = total + from_z[k, :, lanes].astype(jnp.float32)
+        out[:, lanes] = total
+
+    def memory_core():
+        mem_own.wait()
+        mem_core.wait_recv()
+        for theirs in (True, False):
+            side = (1 - y) if theirs else y
+
+            def body(i, carry, side=side):
+                rows = pl.ds(pl.multiple_of(i * 64, 64), 64)
+                macc[side, rows] = macc[side, rows] + mfrom_core[side, rows]
+                return carry
+            lax.fori_loop(0, 8, body, 0)
+            if theirs:
+                go(mem_far)
+
+    def memory_end():
+        mem_far.wait_recv()
+
+        def body(i, carry):
+            rows = pl.ds(pl.multiple_of(i * 64, 64), 64)
+            mem_out[rows] = macc[y, rows].astype(jnp.float32) + mfrom_y[rows].astype(jnp.float32)
+            return carry
+        lax.fori_loop(0, 8, body, 0)
+
+    def weight_rows(i, part):
+        devs = pl.ds(part * 16, 16)
+        return w[devs, :, pl.ds(SLAB * i, SLAB)].reshape(256, SLAB)
+
+    def put(i, n, value):
+        gs[:, :, :, :, :, pl.ds(NORM + SLAB * i + 256 * n, 256)] = value.astype(LOW).reshape(4, 2, 2, 2, ROWS, 256)
+
+    rows_all = tgt.shape[0]
+
+    def norm_back(i):
+        r = block(i, 64)
+        u, xh = dpre[r], xh1[r]
+        ng[0:1] += jnp.sum(u * xh, axis=0, keepdims=True)
+        ng[1:2] += jnp.sum(u, axis=0, keepdims=True)
+        d = back_norm(u, gb[0:1], xh, rs1[r][:, :1])
+        dpre[r] = d
+        g_b[r] = d.astype(LOW)
+
+    def self_norm():
+        for copy in copies:
+            copy.wait()
+        each(rows_all // 64, norm_back)
+
+    def self_out():
+        out_back(g_b, lambda n: weight_rows(3, n), num_s, tot_s, dnx)
+        for n in (0, 1):
+            put(3, n, tmm(o_b[...], g_b[:, pl.ds(256 * n, 256)]))
+        for ref in (dq, dk, dv):
+            zero(ref)
+
+    def self_tiles(i, first, last):
+        def inner(kt, carry):
+            r = pl.ds(i * RT, RT)
+            key = kt * TILE + lane_iota((RT, TILE))
+            row = i * RT + row_iota((RT, TILE))
+            bias = jnp.where((key >= low_s[r]) & (key <= row), 0.0, HIDE)
+            tile_backward(r, block(kt), bias, qs, ks, vs, dnx, dq, dk, dv)
+            return carry
+        lax.fori_loop(first, last, inner, 0)
+
+    def self_grads():
+        def lower(i):
+            r = block(i, 64)
+            qs[r] = (dq[r] * 0.125).astype(LOW)
+            ks[r] = dk[r].astype(LOW)
+            vs[r] = dv[r].astype(LOW)
+        each(rows_all // 64, lower)
+        for i, src in ((0, qs), (1, ks), (2, vs)):
+            for n in (0, 1):
+                put(i, n, tmm(tgt[...], src[:, pl.ds(256 * n, 256)]))
+        padded = jnp.concatenate([ng[...], jnp.zeros((NORM - 8, SLAB), F32)], axis=0)
+        gs[:, :, :, :, :, pl.ds(0, NORM)] = jnp.transpose(padded).astype(LOW).reshape(4, 2, 2, 2, ROWS, NORM)
+        for r in SELF_ROUNDS:
+            go(core(r))
+
+    def self_target():
+        for n in (0, 1):
+            total = mmt(qs[...], weight_rows(0, n)) + mmt(ks[...], weight_rows(1, n))
+            cols = pl.ds(256 * n, 256)
+            target_grad[:, cols] = dpre[:, cols] + total + mmt(vs[...], weight_rows(2, n))
+
+    add_core(0)
+    memory_core()
+    add_core(1)
+    self_norm()
+    add_first(0)
+    add_core(2)
+    self_out()
+    add_second(0)
+    add_first(1)
+    add_core(3)
+    self_tiles(0, 0, 2)
+    add_second(1)
+    add_first(2)
+    self_tiles(1, 0, 4)
+    add_z(0)
+    add_second(2)
+    add_first(3)
+    self_grads()
+    add_core(4)
+    add_core(5)
+    self_target()
+    memory_end()
+    add_z(1)
+    add_second(3)
+    add_first(4)
+    add_first(5)
+    add_z(2)
+    add_second(4)
+    add_z(3)
+    add_second(5)
+    add_z(4)
+    add_z(5)
+    for copy in sent:
+        copy.wait_send()
+
+
+def scatter_all(grads, mem_grads, gathered, target, state):
+    any_space = pl.BlockSpec(memory_space=pl.ANY)
+    vmem = pl.BlockSpec(memory_space=pltpu.VMEM)
+    dma = pltpu.SemaphoreType.DMA
+    n = len(SCATTER_ROUNDS)
+    rows = mem_grads.shape[2]
+    low = lambda *s: pltpu.VMEM(s, LOW)
+    f32 = lambda *s: pltpu.VMEM(s, F32)
+    return pl.pallas_call(
+        scatter_kernel,
+        out_shape=(
+            jax.ShapeDtypeStruct((ROWS, LANES), F32),
+            jax.ShapeDtypeStruct((rows, SLAB), F32),
+            jax.ShapeDtypeStruct((rows, SLAB), F32),
+        ),
+        in_specs=[any_space] * 16,
+        out_specs=(vmem,) * 3,
+        scratch_shapes=[
+            low(4, 2, 2, ROWS, LANES),
+            low(4, 2, 2, ROWS, LANES),
+            low(4, 2, ROWS, LANES),
+            low(4, ROWS, LANES),
+            low(3, ROWS, LANES),
+            low(2, rows, SLAB),
+            low(2, rows, SLAB),
+            low(rows, SLAB),
+        ]
+        + [pltpu.VMEM(s.shape, s.dtype) for s in state_shapes(rows)]
+        + [
+            low(32, ROWS, 4 * SLAB),
+            low(rows, SLAB),
+            low(4, 2, 2, 2, ROWS, SELF_LANES),
+            f32(rows, SLAB),
+            f32(rows, SLAB),
+            f32(rows, SLAB),
+            low(rows, 2 * SLAB),
+            low(rows, SLAB),
+            dma((n,)),
+            dma(()),
+            dma((14,)),
+            dma((n,)),
+            dma((n,)),
+            dma((n, 2)),
+            dma((n, 2)),
+            dma((n, 2)),
+            dma((n, 2)),
+            dma((n, 3)),
+            dma((n, 3)),
+            dma((2,)),
+            dma((2,)),
+        ],
+        compiler_params=pltpu.CompilerParams(
+            collective_id=2, has_side_effects=True, vmem_limit_bytes=56 << 20),
+        name="scatter",
+    )(grads, mem_grads, gathered, target, *state)
 
 
 def local(target_in, memory, out_grad, *rest):
@@ -1205,10 +1326,15 @@
     norms = jnp.stack(weights[10:], axis=1)
     norms = jnp.pad(norms, ((0, 0), (0, NORM - norms.shape[1])))
     gathered, all_memory = gather_all(weights[:10], norms, memory)
-    layer_out, target_grad, grads, mem_grads = compute(*tables, target_in, out_grad, all_memory, gathered)
+    layer_out, grads, mem_grads, *state = compute(*tables, target_in, out_grad, all_memory, gathered)
     rows = target_in.shape[0]
-    out, mem_out = scatter_all(
-        grads.reshape(4, 2, 2, 2, ROWS, LANES), mem_grads.reshape(2, 2, rows, SLAB))
+    out, mem_out, target_grad = scatter_all(
+        grads.reshape(4, 2, 2, 2, ROWS, LANES),
+        mem_grads.reshape(2, 2, rows, SLAB),
+        gathered,
+        target_in,
+        state,
+    )
     part = lambda i, n=1: out[:, NORM + SLAB * i : NORM + SLAB * (i + n)]
     w2_grad = jnp.concatenate([part(12 + k) for k in range(4)], axis=0)
     return (

time: 195 us -> 172 us (0.88)
  Pallas kernels: 184 us -> 155 us
  local copies, waits for them, and re-layouts: 9.85 us -> 14.6 us
    pallas_call x1, Pallas kernels: 64.9 us -> 35.9 us  [compute(): pl.pallas_call(compute_kernel, out_shape=(jax.ShapeDtypeStruct((rows, SLA...]
    unnamed x3 -> x2, local copies, waits for them, and re-layouts: 2.55 us -> 4.52 us
where the time goes in v4:
time: 172 us; the launch traced here: 171 us
  Pallas kernels  155 us (90%)
  local copies, waits for them, and re-layouts  14.6 us (8%)
    pallas_call x1, Pallas kernels, scatter_all(): pl.pallas_call(scatter_kernel, out_shape=(jax.ShapeDtypeStruct((ROWS, LAN...  60.3 us
    pallas_call x1, Pallas kernels, gather_all(): pl.pallas_call(gather_kernel, out_shape=(jax.ShapeDtypeStruct((4, 2, 2, 2...  59.1 us
    pallas_call x1, Pallas kernels, compute(): pl.pallas_call(compute_kernel, out_shape=(jax.ShapeDtypeStruct((rows, SLA...  35.9 us
    another operation x7, local copies, waits for them, and re-layouts, local(): norms = jnp.stack(weights[10:], axis=1)  4.56 us
    unnamed x2, local copies, waits for them, and re-layouts  4.52 us

profile of v4, /device:TPU:0, one launch (start us, length us, event | category | flops | bytes accessed | tf_op | source)
XLA Modules:
  0.0 171.2 jit_solution(14907717681944653482)
XLA Ops:
  0.7 0.7 copy.47
  1.4 0.7 copy.48
  2.1 0.7 copy.49
  2.9 0.7 copy.50
  3.6 0.7 copy.51
  4.4 0.7 copy.52
  5.1 0.1 stack.27
  5.2 0.6 pad.4.refs_10_
  5.8 59.1 %gather.1 = (bf16[4,2,2,2,16,8320]{5,4,3,2,1,0:T(8,128)(2,1)}, bf16[2,2,512,512]{3,2,1,0:T(8,128)(2,1)}) custom-call(bf16[16,512]{1,0:T(8,128)(2,1)} %refs_0_.1, bf16[16,512]{1,0:T(8,128)(2,1)} %refs_1_.1, bf16[16,512]{1,0:T(8,128)(2,1)} %refs_2_.1, bf16[16,512]{1,0:T(8,128)(2,1)} %refs_3_.1, bf16[16,512]{1,0:T(8,128)(2,1)} %refs_4_.1, ...), custom_call_target="tpu_custom_call" | custom-call | tf_op jit(solution)/shard_map/gather/pallas_call | solution.py:221
  64.9 35.9 %compute.1 = (bf16[512,512]{1,0:T(8,128)(2,1)}, bf16[32,16,8320]{2,1,0:T(8,128)(2,1)}, bf16[2048,512]{1,0:T(8,128)(2,1)}, f32[512,512]{1,0:T(8,128)}, f32[512,51...) custom-call(s32[1,64]{1,0:T(1,128)} %lens_ref.1, ...), custom_call_target="tpu_custom_call" | custom-call | tf_op jit(solution)/shard_map/compute/pallas_call | solution.py:937
  100.8 60.3 %scatter.1 = (f32[16,8320]{1,0:T(8,128)}, f32[512,512]{1,0:T(8,128)}, f32[512,512]{1,0:T(8,128)}) custom-call(bf16[4,2,2,2,16,8320]{5,4,3,2,1,0:T(8,128)(2,1)} %bitcast.12, bf16[2,2,512,512]{3,2,1,0:T(8,128)(2,1)} %bitcast.13, bf16[32,16,8320]{2,1,0:T(8,128)(2,1)} %bitcast.11, bf16[512,512]{1,0:T(8,128)(2,1)} %target.3, ...), custom_call_target="tpu_custom_call" | custom-call | tf_op jit(solution)/shard_map/scatter/pallas_call | solution.py:1272
  161.1 1.7 slice_reduce_fusion
  162.8 1.6 slice.65
  164.4 1.6 fusion
  166.0 0.7 pad_maximum_fusion
  166.7 2.3 %copy.55 = f32[512,512]{1,0:T(8,128)} copy(f32[512,512]{1,0:T(8,128)} %get-tuple-element.97) | data formatting | bytes 2097152
  169.0 2.3 %copy.56 = f32[512,512]{1,0:T(8,128)} copy(f32[512,512]{1,0:T(8,128)} %get-tuple-element.98) | data formatting | bytes 2097152

commit v5 on v4

--- a/solution.py
+++ b/solution.py
@@ -60,6 +60,7 @@
     out, mem_out, local_sem, mem_local = refs[12:16]
     z_sems, first_sems, second_sems = refs[16:18], refs[18:20], refs[20:22]
     across, mems = refs[22:24], refs[24:26]
+    stage, mem_stage = refs[26:28]
     z, x, y, c = here()
     xp, yp, cp_ = device(z, 1 - x, y, c), device(z, x, 1 - y, c), device(z, x, y, 1 - c)
     own = out.at[z, x, y, c]
@@ -69,7 +70,7 @@
 
     def bring(src, start, width):
         local.append(
-            pltpu.make_async_copy(src, own.at[:, pl.ds(start, width)], local_sem.at[len(local)])
+            pltpu.make_async_copy(src, stage.at[:, pl.ds(start, width)], local_sem.at[len(local)])
         )
 
     bring(norm_ref, 0, NORM)
@@ -80,12 +81,14 @@
         bring(shards[9].at[pl.ds(ROWS * k, ROWS)], NORM + SLAB * (12 + k), SLAB)
     for one in local:
         one.start()
-    keep = pltpu.make_async_copy(memory_ref, mem_out.at[y, c], mem_local)
+    keep = pltpu.make_async_copy(memory_ref, mem_stage, mem_local.at[0])
     keep.start()
     zn = [device((z + k) % 4, x, y, c) for k in (1, 3)]
     greet([xp, yp, cp_] + zn)
     for one in local:
         one.wait()
+    own_out = pltpu.make_async_copy(stage, own, mem_local.at[1])
+    own_out.start()
 
     def column(slot):
         return z if slot == 0 else (z - slot if slot < 4 else z + (slot - 3))
@@ -111,9 +114,10 @@
     def along(slot, r, up):
         a, _, b = GATHER_ROUNDS[r]
         ref = out.at[column(slot), x, y, c, :, pl.ds(a, b - a)]
+        src = stage.at[:, pl.ds(a, b - a)] if slot == 0 else ref
         d = 0 if slot == 0 else (slot if slot < 4 else slot - 3)
         peer = device((z + (1 if up else 3)) % 4, x, y, c)
-        return remote(ref, ref, z_sems, (0 if up else 1, d, r), peer)
+        return remote(src, ref, z_sems, (0 if up else 1, d, r), peer)
 
     def arrived(slot, r):
         a, _, b = GATHER_ROUNDS[r]
@@ -129,7 +133,9 @@
             ref = out.at[zz, (1 - x) if arriving else x, y, c, :, pl.ds(a, m - a)]
         else:
             ref = out.at[zz, x, (1 - y) if arriving else y, c, :, pl.ds(m, b - m)]
-        return remote(ref, ref, first_sems, (slot, part, r), xp if part == 0 else yp)
+        lanes = pl.ds(a, m - a) if part == 0 else pl.ds(m, b - m)
+        src = stage.at[:, lanes] if slot == 0 and not arriving else ref
+        return remote(src, ref, first_sems, (slot, part, r), xp if part == 0 else yp)
 
     def second(slot, r, part, hop, arriving=False):
         a, m, b = GATHER_ROUNDS[r]
@@ -140,7 +146,9 @@
         else:
             side = (1 - y) if hop else y
             ref = out.at[zz, (1 - x) if arriving else x, side, c, :, pl.ds(m, b - m)]
-        return remote(ref, ref, second_sems, (slot, part, hop, r), yp if part == 0 else xp)
+        lanes = pl.ds(a, m - a) if part == 0 else pl.ds(m, b - m)
+        src = stage.at[:, lanes] if slot == 0 and not (arriving or hop) else ref
+        return remote(src, ref, second_sems, (slot, part, hop, r), yp if part == 0 else xp)
 
     def over(slot, r, arriving=False):
         a, _, b = GATHER_ROUNDS[r]
@@ -190,10 +198,13 @@
     pass_on((0,))
     from_z(2)
     pass_on((1, 4))
+    own_out.wait()
     hand_over((0,))
     keep.wait()
-    go(lambda: remote(mem_own, mem_own, mems, 0, yp))
-    go(lambda: remote(mem_own, mem_own, mems, 1, cp_))
+    kept = pltpu.make_async_copy(mem_stage, mem_own, mem_local.at[2])
+    kept.start()
+    go(lambda: remote(mem_stage, mem_own, mems, 0, yp))
+    go(lambda: remote(mem_stage, mem_own, mems, 1, cp_))
     from_z(3)
     pass_on((2, 5))
     hand_over((1, 4))
@@ -209,6 +220,7 @@
     for i, side in ((1, y), (2, 1 - y)):
         block = mem_out.at[side, 1 - c]
         remote(block, block, mems, i, cp_).wait_recv()
+    kept.wait()
     for cond, make in sent:
         guarded(cond, lambda make=make: make().wait_send())
 
@@ -226,8 +238,9 @@
         ),
         in_specs=[any_space] * 12,
         out_specs=(any_space, any_space),
-        scratch_shapes=[dma((14,)), dma(())]
-        + both(2, 3, n) + both(7, 2, n) + both(7, 2, 2, n) + both(7, n) + both(3),
+        scratch_shapes=[dma((14,)), dma((3,))]
+        + both(2, 3, n) + both(7, 2, n) + both(7, 2, 2, n) + both(7, n) + both(3)
+        + [pltpu.VMEM((ROWS, LANES), jnp.bfloat16), pltpu.VMEM(memory.shape, jnp.bfloat16)],
         compiler_params=pltpu.CompilerParams(collective_id=1, has_side_effects=True),
         name="gather",
     )(*shards, norms, memory)
@@ -638,7 +651,12 @@
     ng[...] = jnp.zeros_like(ng)
 
     loads["norm"].wait()
-    gb[...] = jnp.transpose(w[:, :, pl.ds(0, NORM)].reshape(SLAB, NORM).astype(F32))[:8]
+    for j in range(SLAB // TILE):
+        total = jnp.zeros((8, TILE), F32)
+        for k in range(8):
+            one = w[8 * j + k, :, pl.ds(0, NORM)].astype(F32)[:8]
+            total = total + (pltpu.roll(one, ROWS * k, 1) if k else one)
+        gb[:, pl.ds(TILE * j, TILE)] = total
     loads["x"].wait()
     for i, dst in ((0, qs), (1, ks), (2, vs)):
         loads[i].wait()
@@ -1008,11 +1026,13 @@
 
 
 def scatter_kernel(grads, mem_grads, gathered, target, *rest):
-    state, (out, mem_out, target_grad), rest = rest[:12], rest[12:15], rest[15:]
+    state, (out_ref, mem_ref, target_ref), rest = rest[:12], rest[12:15], rest[15:]
     (acc, from_core, from_first, from_second, from_z, macc, mfrom_core, mfrom_y), rest = rest[:8], rest[8:]
     held, rest = rest[:12], rest[12:]
-    (w, tgt, gs, dq, dk, dv, dnx, g_b), rest = rest[:8], rest[8:]
-    (own_sems, mown_sem, state_sems, core_s, core_r, first_s, first_r,
+    (w, tgt, gs, dq, dk, dv, dnx, g_b, out, mem_out), rest = rest[:10], rest[10:]
+    target_grad = rest[0]
+    rest = rest[1:]
+    (out_sems, own_sems, mown_sem, state_sems, core_s, core_r, first_s, first_r,
      second_s, second_r, zs_s, zs_r, mem_s, mem_r) = rest
     dpre, xh1, rs1, num_s, tot_s, qs, ks, vs, o_b, gb, ng, low_s = held
     z, x, y, c = here()
@@ -1214,8 +1234,12 @@
         for i, src in ((0, qs), (1, ks), (2, vs)):
             for n in (0, 1):
                 put(i, n, tmm(tgt[...], src[:, pl.ds(256 * n, 256)]))
-        padded = jnp.concatenate([ng[...], jnp.zeros((NORM - 8, SLAB), F32)], axis=0)
-        gs[:, :, :, :, :, pl.ds(0, NORM)] = jnp.transpose(padded).astype(LOW).reshape(4, 2, 2, 2, ROWS, NORM)
+        inside = lane_iota((8, TILE)) < ROWS
+        for d in range(DEV):
+            one = ng[:, pl.ds(TILE * (d // 8), TILE)]
+            one = pltpu.roll(one, (TILE - ROWS * (d % 8)) % TILE, 1) if d % 8 else one
+            one = jnp.concatenate([jnp.where(inside, one, 0.0), jnp.zeros((8, TILE), F32)], axis=0)
+            gs[d // 8, d // 4 % 2, d // 2 % 2, d % 2, :, pl.ds(0, NORM)] = one.astype(LOW)
         for r in SELF_ROUNDS:
             go(core(r))
 
@@ -1246,7 +1270,11 @@
     add_core(4)
     add_core(5)
     self_target()
+    to_target = pltpu.make_async_copy(target_grad, target_ref, out_sems.at[0])
+    to_target.start()
     memory_end()
+    to_memory = pltpu.make_async_copy(mem_out, mem_ref, out_sems.at[1])
+    to_memory.start()
     add_z(1)
     add_second(3)
     add_first(4)
@@ -1257,13 +1285,16 @@
     add_second(5)
     add_z(4)
     add_z(5)
+    to_rows = pltpu.make_async_copy(out, out_ref, out_sems.at[2])
+    to_rows.start()
+    for copy in (to_target, to_memory, to_rows):
+        copy.wait()
     for copy in sent:
         copy.wait_send()
 
 
 def scatter_all(grads, mem_grads, gathered, target, state):
     any_space = pl.BlockSpec(memory_space=pl.ANY)
-    vmem = pl.BlockSpec(memory_space=pltpu.VMEM)
     dma = pltpu.SemaphoreType.DMA
     n = len(SCATTER_ROUNDS)
     rows = mem_grads.shape[2]
@@ -1277,7 +1308,7 @@
             jax.ShapeDtypeStruct((rows, SLAB), F32),
         ),
         in_specs=[any_space] * 16,
-        out_specs=(vmem,) * 3,
+        out_specs=(any_space,) * 3,
         scratch_shapes=[
             low(4, 2, 2, ROWS, LANES),
             low(4, 2, 2, ROWS, LANES),
@@ -1298,6 +1329,10 @@
             f32(rows, SLAB),
             low(rows, 2 * SLAB),
             low(rows, SLAB),
+            f32(ROWS, LANES),
+            f32(rows, SLAB),
+            f32(rows, SLAB),
+            dma((3,)),
             dma((n,)),
             dma(()),
             dma((14,)),
@@ -1318,13 +1353,75 @@
     )(grads, mem_grads, gathered, target, *state)
 
 
+def finish_kernel(rows_ref, mem_ref, target_ref, *rest):
+    outs, (rows, mem, target, in_sems, out_sems) = rest[:18], rest[18:]
+    copies = []
+    loads = []
+    half = target.shape[0] // 2
+    pieces = [pl.ds(0, half), pl.ds(half, half)]
+    cuts_ = [(NORM + SLAB * i, SLAB) for i in range(8)] + [(NORM + SLAB * 8, 4 * SLAB)]
+    cuts_ += [(NORM + SLAB * (12 + k), SLAB) for k in range(4)]
+
+    def load(src, dst):
+        copy = pltpu.make_async_copy(src, dst, in_sems.at[len(loads)])
+        copy.start()
+        loads.append(copy)
+
+    def bring(src, dst):
+        copy = pltpu.make_async_copy(src, dst, out_sems.at[len(copies)])
+        copy.start()
+        copies.append(copy)
+
+    for p in pieces:
+        load(target_ref.at[p], target.at[p])
+        load(mem_ref.at[p], mem.at[p])
+    load(rows_ref, rows)
+    for i, p in enumerate(pieces):
+        loads[2 * i].wait()
+        bring(target.at[p], outs[0].at[p])
+        loads[2 * i + 1].wait()
+        bring(mem.at[p], outs[1].at[p])
+    loads[4].wait()
+    for i, (start, width) in enumerate(cuts_):
+        dst = outs[2 + i] if i < 9 else outs[11].at[pl.ds(ROWS * (i - 9), ROWS)]
+        bring(rows.at[:, pl.ds(start, width)], dst)
+    for i in range(6):
+        outs[12 + i][...] = rows[i, pl.ds(0, ROWS)]
+    for copy in copies:
+        copy.wait()
+
+
+def finish(rows, mem, target):
+    any_space = pl.BlockSpec(memory_space=pl.ANY)
+    shape = lambda *s: jax.ShapeDtypeStruct(s, F32)
+    return pl.pallas_call(
+        finish_kernel,
+        out_shape=(shape(*target.shape), shape(*mem.shape))
+        + (shape(ROWS, SLAB),) * 8
+        + (shape(ROWS, 4 * SLAB), shape(4 * ROWS, SLAB))
+        + (shape(ROWS),) * 6,
+        in_specs=[any_space] * 3,
+        out_specs=(any_space,) * 12 + (pl.BlockSpec(memory_space=pltpu.VMEM),) * 6,
+        scratch_shapes=[
+            pltpu.VMEM(rows.shape, F32),
+            pltpu.VMEM(mem.shape, F32),
+            pltpu.VMEM(target.shape, F32),
+            pltpu.SemaphoreType.DMA((5,)),
+            pltpu.SemaphoreType.DMA((17,)),
+        ],
+        name="finish",
+    )(rows, mem, target)
+
+
 def local(target_in, memory, out_grad, *rest):
     fast = two_by_two((lax.axis_size("dp"), lax.axis_size("mem")))
     if not fast:
         return plain(target_in, memory, out_grad, *rest)
     weights, tables = rest[:16], rest[16:]
-    norms = jnp.stack(weights[10:], axis=1)
-    norms = jnp.pad(norms, ((0, 0), (0, NORM - norms.shape[1])))
+    norms = sum(
+        jnp.pad(one[None, :], ((i, ROWS - 1 - i), (0, NORM - ROWS)))
+        for i, one in enumerate(weights[10:])
+    )
     gathered, all_memory = gather_all(weights[:10], norms, memory)
     layer_out, grads, mem_grads, *state = compute(*tables, target_in, out_grad, all_memory, gathered)
     rows = target_in.shape[0]
@@ -1335,14 +1432,7 @@
         target_in,
         state,
     )
-    part = lambda i, n=1: out[:, NORM + SLAB * i : NORM + SLAB * (i + n)]
-    w2_grad = jnp.concatenate([part(12 + k) for k in range(4)], axis=0)
-    return (
-        (layer_out, target_grad, mem_out)
-        + tuple(part(i) for i in range(8))
-        + (part(8, 4), w2_grad)
-        + tuple(out[:, i] for i in range(6))
-    )
+    return (layer_out,) + tuple(finish(out, mem_out, target_grad))
 
 
 def solution(mesh):

time: 172 us -> 155 us (0.901)
  local copies, waits for them, and re-layouts: 14.6 us -> 0 us
  Pallas kernels: 155 us -> 153 us
    pallas_call x1, Pallas kernels: 59.1 us -> 52.9 us  [gather_all(): pl.pallas_call(gather_kernel, out_shape=(jax.ShapeDtypeStruct((4, 2, 2, 2...]
    slice x3 -> x0, local copies, waits for them, and re-layouts: 4.9 us -> none  [the longest x2 3.2 us: local(): part = lambda i, n=1: out[:, NORM + SLAB * i:NORM + SLAB * (i + n)]]
    another operation x7 -> x0, local copies, waits for them, and re-layouts: 4.56 us -> none  [local(): norms = jnp.stack(weights[10:], axis=1)]
    unnamed x2 -> x0, local copies, waits for them, and re-layouts: 4.52 us -> none
    pallas_call x0 -> x1, Pallas kernels: none -> 3.24 us  [finish(): pl.pallas_call(finish_kernel, out_shape=(shape(*target.shape), shape(*mem...]
where the time goes in v5:
time: 155 us
  Pallas kernels  153 us (99%)
    pallas_call x1, Pallas kernels, scatter_all(): pl.pallas_call(scatter_kernel, out_shape=(jax.ShapeDtypeStruct((ROWS, LAN...  60 us
    pallas_call x1, Pallas kernels, gather_all(): pl.pallas_call(gather_kernel, out_shape=(jax.ShapeDtypeStruct((4, 2, 2, 2...  52.9 us
    pallas_call x1, Pallas kernels, compute(): pl.pallas_call(compute_kernel, out_shape=(jax.ShapeDtypeStruct((rows, SLA...  36.4 us
    pallas_call x1, Pallas kernels, finish(): pl.pallas_call(finish_kernel, out_shape=(shape(*target.shape), shape(*mem...  3.24 us

profile of v5, /device:TPU:0, one launch (start us, length us, event | category | flops | bytes accessed | tf_op | source)
XLA Modules:
  0.0 154.8 jit_solution(4150515400620234304)
XLA Ops:
  0.7 1.3 pad_add_fusion.refs_10_
  2.0 52.9 %gather.1 = (bf16[4,2,2,2,16,8320]{5,4,3,2,1,0:T(8,128)(2,1)}, bf16[2,2,512,512]{3,2,1,0:T(8,128)(2,1)}) custom-call(bf16[16,512]{1,0:T(8,128)(2,1)} %refs_0_.1, bf16[16,512]{1,0:T(8,128)(2,1)} %refs_1_.1, bf16[16,512]{1,0:T(8,128)(2,1)} %refs_2_.1, bf16[16,512]{1,0:T(8,128)(2,1)} %refs_3_.1, bf16[16,512]{1,0:T(8,128)(2,1)} %refs_4_.1, ...), custom_call_target="tpu_custom_call" | custom-call | tf_op jit(solution)/shard_map/gather/pallas_call | solution.py:233
  54.9 36.4 %compute.1 = (bf16[512,512]{1,0:T(8,128)(2,1)}, bf16[32,16,8320]{2,1,0:T(8,128)(2,1)}, bf16[2048,512]{1,0:T(8,128)(2,1)}, f32[512,512]{1,0:T(8,128)}, f32[512,51...) custom-call(s32[1,64]{1,0:T(1,128)} %lens_ref.1, ...), custom_call_target="tpu_custom_call" | custom-call | tf_op jit(solution)/shard_map/compute/pallas_call | solution.py:955
  91.4 60.0 %scatter.1 = (f32[16,8320]{1,0:T(8,128)}, f32[512,512]{1,0:T(8,128)}, f32[512,512]{1,0:T(8,128)}) custom-call(bf16[4,2,2,2,16,8320]{5,4,3,2,1,0:T(8,128)(2,1)} %bitcast.12, bf16[2,2,512,512]{3,2,1,0:T(8,128)(2,1)} %bitcast.13, bf16[32,16,8320]{2,1,0:T(8,128)(2,1)} %bitcast.11, bf16[512,512]{1,0:T(8,128)(2,1)} %target.3, ...), custom_call_target="tpu_custom_call" | custom-call | tf_op jit(solution)/shard_map/scatter/pallas_call | solution.py:1303
  151.4 3.2 %finish.1 = (f32[512,512]{1,0:T(8,128)}, f32[512,512]{1,0:T(8,128)}, f32[16,512]{1,0:T(8,128)}, f32[16,512]{1,0:T(8,128)}, f32[16,512]{1,0:T(8,128)}, /*index=5*...) custom-call(f32[16,8320]{1,0:T(8,128)} %get-tuple-element.74.rows_re, ...), custom_call_target="tpu_custom_call" | custom-call | tf_op jit(solution)/shard_map/finish/pallas_call | solution.py:1397

commit v6 on v5

--- a/solution.py
+++ b/solution.py
@@ -52,15 +52,20 @@
     return tuple(spans)
 
 
-GATHER_ROUNDS = cuts((33, 32), 0.25)
+GATHER_ROUNDS = cuts((17, 48), 0.25)
 
 
 def gather_kernel(*refs):
-    shards, norm_ref, memory_ref = refs[:10], refs[10], refs[11]
-    out, mem_out, local_sem, mem_local = refs[12:16]
-    z_sems, first_sems, second_sems = refs[16:18], refs[18:20], refs[20:22]
-    across, mems = refs[22:24], refs[24:26]
-    stage, mem_stage = refs[26:28]
+    shards, norm_ref, memory_ref, lens_ref, target = refs[:10], *refs[10:14]
+    out, mem_out = refs[14:16]
+    state_out, refs = refs[16:28], refs[28:]
+    local_sem, mem_local = refs[:2]
+    z_sems, first_sems, second_sems = refs[2:4], refs[4:6], refs[6:8]
+    across, mems = refs[8:10], refs[10:12]
+    stage, mem_stage = refs[12:14]
+    state, refs = refs[14:26], refs[26:]
+    after, a_b, xh1, rs1, num, tot, qs, ks, vs, o_b, gb, low_s = state
+    w, norms, tgt, starts, state_sems = refs
     z, x, y, c = here()
     xp, yp, cp_ = device(z, 1 - x, y, c), device(z, x, 1 - y, c), device(z, x, y, 1 - c)
     own = out.at[z, x, y, c]
@@ -162,8 +167,7 @@
         for part in (1, 0):
             go(functools.partial(second, slot, r, part, 0), cond)
 
-    def from_z(d):
-        for r in rounds:
+    def from_z(d, r):
             for slot in (d, d + 3):
                 cond = there(slot)
                 guarded(cond, lambda slot=slot, r=r: arrived(slot, r).wait_recv())
@@ -172,16 +176,14 @@
                     go(functools.partial(along, slot, r, slot < 4), both(cond, onward))
                 spread(slot, r)
 
-    def pass_on(slots):
-        for r in rounds:
+    def pass_on(slots, r):
             for slot in slots:
                 cond = there(slot)
                 for part in (1, 0):
                     guarded(cond, lambda s=slot, r=r, p=part: first(s, r, p, True).wait_recv())
                     go(functools.partial(second, slot, r, part, 1), cond)
 
-    def hand_over(slots):
-        for r in rounds:
+    def hand_over(slots, r):
             for slot in slots:
                 cond = there(slot)
                 for part in (0, 1):
@@ -194,57 +196,190 @@
         go(functools.partial(along, 0, r, False), z > 0)
         spread(0, r)
     mem_own = mem_out.at[y, c]
-    from_z(1)
-    pass_on((0,))
-    from_z(2)
-    pass_on((1, 4))
+
+    def memory_rows():
+        keep.wait()
+        kept = pltpu.make_async_copy(mem_stage, mem_own, mem_local.at[2])
+        kept.start()
+        go(lambda: remote(mem_stage, mem_own, mems, 0, yp))
+        go(lambda: remote(mem_stage, mem_own, mems, 1, cp_))
+        return kept
+
+    def memory_far():
+        far = mem_out.at[1 - y, c]
+        remote(far, far, mems, 0, yp).wait_recv()
+        go(lambda: remote(far, far, mems, 2, cp_))
+
+    everyone = (0, 1, 4, 2, 5, 3, 6)
+
+    def all_over(r):
+        for slot in everyone:
+            guarded(there(slot), lambda s=slot: over(s, r, True).wait_recv())
+
+    rows_all = tgt.shape[0]
+    n_sent = starts.shape[0]
+    loads = [pltpu.make_async_copy(target, tgt, state_sems.at[12])]
+    loads.append(pltpu.make_async_copy(out.at[:, :, :, :, :, pl.ds(NORM, 4 * SLAB)], w, state_sems.at[13]))
+    loads.append(pltpu.make_async_copy(out.at[:, :, :, :, :, pl.ds(0, NORM)], norms, state_sems.at[14]))
+    saves = [pltpu.make_async_copy(src, dst, state_sems.at[i]) for i, (src, dst) in enumerate(zip(state, state_out))]
+
+    def weight(i, n):
+        return w[:, :, :, :, :, pl.ds(SLAB * i + 256 * n, 256)].reshape(SLAB, 256)
+
+    def prepare():
+        base = lax.axis_index("mem") * n_sent
+
+        def count(j, at):
+            starts[j] = at
+            return at + lens_ref[0, base + j]
+        lax.fori_loop(0, n_sent, count, jnp.int32(0))
+        for i in range(rows_all // TILE):
+            row = i * TILE + row_iota((TILE, TILE))
+            found = jnp.zeros((TILE, TILE), jnp.int32)
+            for j in range(n_sent):
+                found = jnp.where(row >= starts[j], starts[j], found)
+            low_s[pl.ds(i * TILE, TILE)] = found
+        zero(num)
+        zero(tot)
+
+    def project():
+        for one in loads:
+            one.wait()
+        for j in range(SLAB // TILE):
+            total = jnp.zeros((8, TILE), F32)
+            for k in range(8):
+                d = 8 * j + k
+                one = norms[d // 8, d // 4 % 2, d // 2 % 2, d % 2].astype(F32)[:8]
+                total = total + (pltpu.roll(one, ROWS * k, 1) if k else one)
+            gb[:, pl.ds(TILE * j, TILE)] = total
+        for i, dst in ((0, qs), (1, ks), (2, vs)):
+            for n in (0, 1):
+                value = mm(tgt[...], weight(i, n)).astype(LOW)
+                dst[:, pl.ds(256 * n, 256)] = value * jnp.asarray(0.125, LOW) if i == 0 else value
+
+    def self_tiles(i, first_tile, last_tile):
+        def inner(kt, carry):
+            r = pl.ds(i * RT, RT)
+            key = kt * TILE + lane_iota((RT, TILE))
+            row = i * RT + row_iota((RT, TILE))
+            bias = jnp.where((key >= low_s[r]) & (key <= row), 0.0, HIDE)
+            tile_forward(r, block(kt), bias, qs, ks, vs, num, tot)
+            return carry
+        lax.fori_loop(first_tile, last_tile, inner, 0)
+
+    def project_out():
+        divide(num, tot, o_b, rows_all)
+        for n in (0, 1):
+            cols = pl.ds(256 * n, 256)
+            after[:, cols] = tgt[:, cols].astype(F32) + mm(o_b[...], weight(3, n))
+
+    def norm_rows(i):
+        r = block(i, 64)
+        xh, rs = normalize(after[r])
+        xh1[r] = xh
+        rs1[r] = jnp.broadcast_to(rs, (64, TILE))
+        value = xh * gb[0:1] + gb[1:2]
+        after[r] = value
+        a_b[r] = value.astype(LOW)
+
+    loads[0].start()
+    prepare()
+    from_z(1, 0)
+    from_z(1, 1)
+    pass_on((0,), 0)
+    from_z(2, 0)
+    pass_on((0,), 1)
+    pass_on((1, 4), 0)
+    from_z(3, 0)
+    from_z(2, 1)
+    pass_on((2, 5), 0)
     own_out.wait()
-    hand_over((0,))
-    keep.wait()
-    kept = pltpu.make_async_copy(mem_stage, mem_own, mem_local.at[2])
-    kept.start()
-    go(lambda: remote(mem_stage, mem_own, mems, 0, yp))
-    go(lambda: remote(mem_stage, mem_own, mems, 1, cp_))
-    from_z(3)
-    pass_on((2, 5))
-    hand_over((1, 4))
-    far = mem_out.at[1 - y, c]
-    remote(far, far, mems, 0, yp).wait_recv()
-    go(lambda: remote(far, far, mems, 2, cp_))
-    pass_on((3, 6))
-    hand_over((2, 5))
-    hand_over((3, 6))
-    for slot in (0, 1, 4, 2, 5, 3, 6):
-        for r in rounds:
-            guarded(there(slot), lambda s=slot, r=r: over(s, r, True).wait_recv())
+    hand_over((0,), 0)
+    pass_on((1, 4), 1)
+    pass_on((3, 6), 0)
+    kept = memory_rows()
+    hand_over((1, 4), 0)
+    hand_over((2, 5), 0)
+    from_z(3, 1)
+    hand_over((3, 6), 0)
+    all_over(0)
+    loads[1].start()
+    loads[2].start()
+    pass_on((2, 5), 1)
+    project()
+    hand_over((0,), 1)
+    self_tiles(0, 0, 2)
+    pass_on((3, 6), 1)
+    self_tiles(1, 0, 4)
+    hand_over((1, 4), 1)
+    memory_far()
+    project_out()
+    each(rows_all // 64, norm_rows)
+    hand_over((2, 5), 1)
+    hand_over((3, 6), 1)
+    for one in saves:
+        one.start()
+    all_over(1)
+    for one in saves:
+        one.wait()
     for i, side in ((1, y), (2, 1 - y)):
-        block = mem_out.at[side, 1 - c]
-        remote(block, block, mems, i, cp_).wait_recv()
+        last = mem_out.at[side, 1 - c]
+        remote(last, last, mems, i, cp_).wait_recv()
     kept.wait()
     for cond, make in sent:
         guarded(cond, lambda make=make: make().wait_send())
 
 
-def gather_all(shards, norms, memory):
+def gather_all(shards, norms, memory, lens, target):
     any_space = pl.BlockSpec(memory_space=pl.ANY)
     dma = pltpu.SemaphoreType.DMA
     n = len(GATHER_ROUNDS)
     both = lambda *s: [dma(s), dma(s)]
-    gathered, whole_memory = pl.pallas_call(
+    state = forward_shapes(target.shape[0])
+    low = lambda *s: pltpu.VMEM(s, LOW)
+    gathered, whole_memory, *saved = pl.pallas_call(
         gather_kernel,
         out_shape=(
             jax.ShapeDtypeStruct((4, 2, 2, 2, ROWS, LANES), jnp.bfloat16),
             jax.ShapeDtypeStruct((2, 2) + memory.shape, jnp.bfloat16),
-        ),
-        in_specs=[any_space] * 12,
-        out_specs=(any_space, any_space),
+        )
+        + state,
+        in_specs=[any_space] * 12 + [pl.BlockSpec(memory_space=pltpu.SMEM), any_space],
+        out_specs=(any_space,) * 14,
         scratch_shapes=[dma((14,)), dma((3,))]
         + both(2, 3, n) + both(7, 2, n) + both(7, 2, 2, n) + both(7, n) + both(3)
-        + [pltpu.VMEM((ROWS, LANES), jnp.bfloat16), pltpu.VMEM(memory.shape, jnp.bfloat16)],
-        compiler_params=pltpu.CompilerParams(collective_id=1, has_side_effects=True),
+        + [low(ROWS, LANES), low(*memory.shape)]
+        + [pltpu.VMEM(s.shape, s.dtype) for s in state]
+        + [
+            low(4, 2, 2, 2, ROWS, 4 * SLAB),
+            low(4, 2, 2, 2, ROWS, NORM),
+            low(*target.shape),
+            pltpu.SMEM((16,), jnp.int32),
+            dma((15,)),
+        ],
+        compiler_params=pltpu.CompilerParams(
+            collective_id=1, has_side_effects=True, vmem_limit_bytes=60 << 20),
         name="gather",
-    )(*shards, norms, memory)
-    return gathered.reshape(32, ROWS, LANES), whole_memory.reshape(-1, SLAB)
+    )(*shards, norms, memory, lens, target)
+    return gathered.reshape(32, ROWS, LANES), whole_memory.reshape(-1, SLAB), saved
+
+
+def forward_shapes(rows):
+    full = lambda dtype, lanes=SLAB, n=rows: jax.ShapeDtypeStruct((n, lanes), dtype)
+    return (
+        full(F32),
+        full(LOW),
+        full(F32),
+        full(F32, TILE),
+        full(F32),
+        full(F32),
+        full(LOW),
+        full(LOW),
+        full(LOW),
+        full(LOW),
+        full(F32, SLAB, 8),
+        full(jnp.int32, TILE),
+    )
 
 
 def two_by_two(mesh_axes):
@@ -565,16 +700,29 @@
     each(2, body)
 
 
-def compute_kernel(lens_ref, spans_ref, offs_ref, target, out_grad, memory, gathered,
-                   layer_out, grads, mem_grads, *rest):
-    (dpre_out, xh1_out, rs1_out, num_out, tot_out, q_out, k_out, v_out, o_out, gb_out, ng_out, low_out,
-                   w, w2, x, og, mem, qs, ks, vs, qc, kc, vc, big, act, dhid, dv,
-                   num_s, tot_s, num_c, tot_c, xh1, xh2, t1, dpre, dq, rs1, rs2, low_s, o_b, oc_b, a_b, c_b,
-                   g_b, dnx, ng, gb, lout,
-                   low_c, high_c, memc, sel, idx,
-     starts, packed, in_sem, w_sem, out_sem) = rest
+def divide(num, tot, out, rows_all):
+    def body(i):
+        r = block(i, 64)
+        o = num[r] / tot[r]
+        num[r] = o
+        out[r] = o.astype(LOW)
+    each(rows_all // 64, body)
+
+
+def normalize(y):
+    mean = jnp.mean(y, axis=1, keepdims=True)
+    centre = y - mean
+    r = lax.rsqrt(jnp.mean(centre * centre, axis=1, keepdims=True) + EPS)
+    return centre * r, r
+
+
+def compute_kernel(lens_ref, spans_ref, offs_ref, out_grad, memory, gathered, after_ref, low_ref, gains_ref,
+                   layer_out, grads, mem_grads, dpre_out, ng_out, *scratch):
+    (w, w2, og, mem, qc, kc, vc, big, act, dhid, dv, num_c, tot_c, xh2, t1, dpre, dq, rs2,
+     oc_b, a_b, c_b, g_b, dnx, ng, gb, lout, low_c, high_c, memc, sel, idx,
+     starts, packed, in_sem, w_sem, out_sem) = scratch
     n_src = mem.shape[0]
-    rows_all = x.shape[0]
+    rows_all = og.shape[0]
     n_sent = starts.shape[0] - 1
     member = lax.axis_index("mem")
     base = member * n_sent
@@ -585,20 +733,24 @@
         loads[name] = pltpu.make_async_copy(src, dst, sem)
         loads[name].start()
 
-    load("x", target, x, in_sem.at[0])
-    load("norm", gathered.at[:, :, pl.ds(0, NORM)], w.at[:, :, pl.ds(0, NORM)], w_sem.at[12])
-    for i in range(3):
-        lanes = pl.ds(NORM + SLAB * i, SLAB)
+    def load_slab(i, count=1):
+        lanes = pl.ds(NORM + SLAB * i, SLAB * count)
         load(i, gathered.at[:, :, lanes], w.at[:, :, lanes], w_sem.at[i])
+
+    load("a", low_ref, a_b, in_sem.at[0])
+    load_slab(4)
     load("mem", memory, mem, in_sem.at[1])
-    for i in (3, 5, 6, 4, 7):
-        lanes = pl.ds(NORM + SLAB * i, SLAB)
-        load(i, gathered.at[:, :, lanes], w.at[:, :, lanes], w_sem.at[i])
-    lanes = pl.ds(NORM + SLAB * 8, 4 * SLAB)
-    load("w1", gathered.at[:, :, lanes], w.at[:, :, lanes], w_sem.at[8])
-    for k in range(4):
-        load(("w2", k), gathered.at[:, :, pl.ds(CUT + SLAB * k, SLAB)], w2.at[:, k], w_sem.at[13 + k])
-    load("og", out_grad, og, in_sem.at[2])
+    load_slab(5)
+    load_slab(6)
+
+    def load_rest():
+        load("t1", after_ref, t1, in_sem.at[3])
+        load("gb", gains_ref, gb, in_sem.at[4])
+        load_slab(7)
+        load_slab(8, 4)
+        for k in range(4):
+            load(("w2", k), gathered.at[:, :, pl.ds(CUT + SLAB * k, SLAB)], w2.at[:, k], w_sem.at[13 + k])
+        load("og", out_grad, og, in_sem.at[2])
 
     outs = []
 
@@ -639,32 +791,13 @@
 
         def pick(j, found):
             here_on = row >= starts[j]
-            values = (starts[j], packed[j], packed[j + 1])
+            values = (packed[j], packed[j + 1])
             return tuple(jnp.where(here_on, v, f) for v, f in zip(values, found))
-        low_s[block(i)], low_c[block(i)], high_c[block(i)] = lax.fori_loop(
-            0, n_sent, pick, (nothing, nothing, nothing))
+        low_c[block(i)], high_c[block(i)] = lax.fori_loop(0, n_sent, pick, (nothing, nothing))
     each(rows_all // TILE, lows)
-    zero(num_s)
-    zero(tot_s)
     zero(num_c)
     zero(tot_c)
     ng[...] = jnp.zeros_like(ng)
-
-    loads["norm"].wait()
-    for j in range(SLAB // TILE):
-        total = jnp.zeros((8, TILE), F32)
-        for k in range(8):
-            one = w[8 * j + k, :, pl.ds(0, NORM)].astype(F32)[:8]
-            total = total + (pltpu.roll(one, ROWS * k, 1) if k else one)
-        gb[:, pl.ds(TILE * j, TILE)] = total
-    loads["x"].wait()
-    for i, dst in ((0, qs), (1, ks), (2, vs)):
-        loads[i].wait()
-
-        def project(n, i=i, dst=dst):
-            value = mm(x[...], weight(i, n)).astype(LOW)
-            dst[:, columns(n)] = value * jnp.asarray(0.125, LOW) if i == 0 else value
-        each(2, project)
 
     def last_at(table, row):
         def pick(j, found):
@@ -679,13 +812,6 @@
             return lax.fori_loop(first(i) // TILE, (last(i) - 1) // TILE + 1, inner, carry)
         lax.fori_loop(0, rows_all // RT, outer, 0)
 
-    def self_tiles(body):
-        def bias(i, kt):
-            key = kt * TILE + lane_iota((RT, TILE))
-            row = i * RT + row_iota((RT, TILE))
-            return jnp.where((key >= low_s[block(i, RT)]) & (key <= row), 0.0, HIDE)
-        tiles(body, bias, lambda i: last_at(lambda j: starts[j], i * RT), lambda i: (i + 1) * RT)
-
     def cross_tiles(body):
         def bias(i, kt):
             key = kt * TILE + lane_iota((RT, TILE))
@@ -694,52 +820,15 @@
         tiles(body, bias, lambda i: last_at(lambda j: packed[j], i * RT),
               lambda i: last_at(lambda j: packed[j + 1], (i + 1) * RT - 1))
 
-    self_tiles(lambda r, k, bias: tile_forward(r, k, bias, qs, ks, vs, num_s, tot_s))
-
-    def divide(num, tot, out):
-        def body(i):
-            r = block(i, 64)
-            o = num[r] / tot[r]
-            num[r] = o
-            out[r] = o.astype(LOW)
-        each(rows_all // 64, body)
-
-    divide(num_s, tot_s, o_b)
-    for src, dst in ((num_s, num_out), (tot_s, tot_out), (qs, q_out), (ks, k_out), (vs, v_out),
-                     (o_b, o_out), (gb, gb_out), (low_s, low_out)):
-        send(src, dst)
-
-    def normalize(y):
-        mean = jnp.mean(y, axis=1, keepdims=True)
-        centre = y - mean
-        r = lax.rsqrt(jnp.mean(centre * centre, axis=1, keepdims=True) + EPS)
-        return centre * r, r
-
-    loads[3].wait()
-
-    def self_out(n):
-        t1[:, columns(n)] = x[:, columns(n)].astype(F32) + mm(o_b[...], weight(3, n))
-    each(2, self_out)
-
-    def norm_self(i):
-        r = block(i, 64)
-        xh, rs = normalize(t1[r])
-        xh1[r] = xh
-        rs1[r] = jnp.broadcast_to(rs, (64, TILE))
-        after = xh * gb[0:1] + gb[1:2]
-        t1[r] = after
-        a_b[r] = after.astype(LOW)
-    each(rows_all // 64, norm_self)
-
-    send(xh1, xh1_out)
-    send(rs1, rs1_out)
-    for i in (4, 5, 6):
-        loads[i].wait()
-    loads["mem"].wait()
+    loads["a"].wait()
+    loads[4].wait()
 
     def query(n):
         qc[:, columns(n)] = mm(a_b[...], weight(4, n)).astype(LOW) * jnp.asarray(0.125, LOW)
     each(2, query)
+    load_rest()
+    for name in ("mem", 5, 6):
+        loads[name].wait()
 
     def choose(ct):
         r = block(ct, CHUNK)
@@ -768,8 +857,9 @@
     each(chunks, keys)
 
     cross_tiles(lambda r, k, bias: tile_forward(r, k, bias, qc, kc, vc, num_c, tot_c))
-    divide(num_c, tot_c, oc_b)
-    loads[7].wait()
+    divide(num_c, tot_c, oc_b, rows_all)
+    for name in (7, "t1", "gb"):
+        loads[name].wait()
 
     def cross_out(n):
         t1[:, columns(n)] += mm(oc_b[...], weight(7, n))
@@ -785,7 +875,7 @@
         c_b[r] = after.astype(LOW)
     each(rows_all // 64, norm_cross)
 
-    loads["w1"].wait()
+    loads[8].wait()
 
     def hidden(n):
         v = mm(c_b[...], weight(8, n))
@@ -943,8 +1033,8 @@
     )
 
 
-def compute(lens, spans, offs, target, out_grad, memory, gathered):
-    rows, n_src = target.shape[0], memory.shape[0]
+def compute(lens, spans, offs, out_grad, memory, gathered, after, after_low, gains):
+    rows, n_src = out_grad.shape[0], memory.shape[0]
     n_sent = 16
     n_keys = n_sent * 112
     any_space = pl.BlockSpec(memory_space=pl.ANY)
@@ -958,18 +1048,16 @@
             jax.ShapeDtypeStruct((rows, SLAB), LOW),
             jax.ShapeDtypeStruct((DEV, ROWS, LANES), LOW),
             jax.ShapeDtypeStruct((n_src, SLAB), LOW),
-        ) + state_shapes(rows),
-        in_specs=[smem] * 3 + [any_space] * 4,
-        out_specs=(any_space,) * 15,
+            jax.ShapeDtypeStruct((rows, SLAB), F32),
+            jax.ShapeDtypeStruct((8, SLAB), F32),
+        ),
+        in_specs=[smem] * 3 + [any_space] * 6,
+        out_specs=(any_space,) * 5,
         scratch_shapes=[
             low(DEV, ROWS, CUT),
             low(DEV, 4, ROWS, SLAB),
             low(rows, SLAB),
-            low(rows, SLAB),
             low(n_src, SLAB),
-            low(rows, SLAB),
-            low(rows, SLAB),
-            low(rows, SLAB),
             low(rows, SLAB),
             low(n_keys, SLAB),
             low(n_keys, SLAB),
@@ -983,13 +1071,7 @@
             f32(rows, SLAB),
             f32(rows, SLAB),
             f32(rows, SLAB),
-            f32(rows, SLAB),
-            f32(rows, SLAB),
-            f32(rows, SLAB),
             f32(rows, TILE),
-            f32(rows, TILE),
-            pltpu.VMEM((rows, TILE), jnp.int32),
-            low(rows, SLAB),
             low(rows, SLAB),
             low(rows, SLAB),
             low(rows, SLAB),
@@ -1005,13 +1087,13 @@
             pltpu.VMEM((n_keys, TILE), jnp.int32),
             pltpu.SMEM((n_sent + 1,), jnp.int32),
             pltpu.SMEM((n_sent + 1,), jnp.int32),
-            dma((4,)),
+            dma((5,)),
             dma((17,)),
             dma((32,)),
         ],
         compiler_params=pltpu.CompilerParams(vmem_limit_bytes=60 << 20),
         name="compute",
-    )(lens, spans, offs, target, out_grad, memory, gathered)
+    )(lens, spans, offs, out_grad, memory, gathered, after, after_low, gains)
 def scatter_rounds(share=0.25):
     spans = []
     for at, tiles in ((33, 6), (39, 12), (51, 14), (17, 16), (0, 11), (11, 6)):
@@ -1422,8 +1504,12 @@
         jnp.pad(one[None, :], ((i, ROWS - 1 - i), (0, NORM - ROWS)))
         for i, one in enumerate(weights[10:])
     )
-    gathered, all_memory = gather_all(weights[:10], norms, memory)
-    layer_out, grads, mem_grads, *state = compute(*tables, target_in, out_grad, all_memory, gathered)
+    gathered, all_memory, saved = gather_all(weights[:10], norms, memory, tables[0], target_in)
+    after, after_low, xh1, rs1, num, tot, q, k, v, o, gains, low_s = saved
+    layer_out, grads, mem_grads, d_after, norm_grads = compute(
+        *tables, out_grad, all_memory, gathered, after, after_low, gains
+    )
+    state = (d_after, xh1, rs1, num, tot, q, k, v, o, gains, norm_grads, low_s)
     rows = target_in.shape[0]
     out, mem_out, target_grad = scatter_all(
         grads.reshape(4, 2, 2, 2, ROWS, LANES),

time: 155 us -> 151 us (0.974)
  Pallas kernels: 153 us -> 149 us
    pallas_call x1, Pallas kernels: 36.4 us -> 30 us  [compute(): pl.pallas_call(compute_kernel, out_shape=(jax.ShapeDtypeStruct((rows, SLA...]
    pallas_call x1, Pallas kernels: 52.9 us -> 55.8 us  [gather_all(): pl.pallas_call(gather_kernel, out_shape=(jax.ShapeDtypeStruct((4, 2, 2, 2...]
where the time goes in v6:
time: 151 us
  Pallas kernels  149 us (99%)
    pallas_call x1, Pallas kernels, scatter_all(): pl.pallas_call(scatter_kernel, out_shape=(jax.ShapeDtypeStruct((ROWS, LAN...  60 us
    pallas_call x1, Pallas kernels, gather_all(): pl.pallas_call(gather_kernel, out_shape=(jax.ShapeDtypeStruct((4, 2, 2, 2...  55.8 us
    pallas_call x1, Pallas kernels, compute(): pl.pallas_call(compute_kernel, out_shape=(jax.ShapeDtypeStruct((rows, SLA...  30 us
    pallas_call x1, Pallas kernels, finish(): pl.pallas_call(finish_kernel, out_shape=(shape(*target.shape), shape(*mem...  3.24 us

profile of v6, /device:TPU:0, one launch (start us, length us, event | category | flops | bytes accessed | tf_op | source)
XLA Modules:
  0.0 151.3 jit_solution(9369981867140257992)
XLA Ops:
  0.7 1.3 pad_add_fusion.refs_10_
  2.0 55.8 %gather.1 = (bf16[4,2,2,2,16,8320]{5,4,3,2,1,0:T(8,128)(2,1)}, bf16[2,2,512,512]{3,2,1,0:T(8,128)(2,1)}, f32[512,512]{1,0:T(8,128)}, bf16[512,512]{1,0:T(8,128)(...) custom-call(bf16[16,512]{1,0:T(8,128)(2,1)} %refs_0_.1, ...), custom_call_target="tpu_custom_call" | custom-call | tf_op jit(solution)/shard_map/gather/pallas_call | solution.py:340
  57.8 30.0 %compute.1 = (bf16[512,512]{1,0:T(8,128)(2,1)}, bf16[32,16,8320]{2,1,0:T(8,128)(2,1)}, bf16[2048,512]{1,0:T(8,128)(2,1)}, f32[512,512]{1,0:T(8,128)}, f32[8,512]{1,0:T(8,128)}) custom-call(s32[1,64]{1,0:T(1,128)} %lens_ref.1, s32[1,64]{1,0:T(1,128)} %spans_ref.1, s32[1,64]{1,0:T(1,128)} %offs_ref.1, bf16[512,512]{1,0:T(8,128)(2,1)} %out_grad.1, ...), custom_call_target="tpu_custom_call" | custom-call | tf_op jit(solution)/shard_map/compute/pallas_call | solution.py:1045
  87.8 60.0 %scatter.1 = (f32[16,8320]{1,0:T(8,128)}, f32[512,512]{1,0:T(8,128)}, f32[512,512]{1,0:T(8,128)}) custom-call(bf16[4,2,2,2,16,8320]{5,4,3,2,1,0:T(8,128)(2,1)} %bitcast.12, bf16[2,2,512,512]{3,2,1,0:T(8,128)(2,1)} %bitcast.13, bf16[32,16,8320]{2,1,0:T(8,128)(2,1)} %bitcast.11, bf16[512,512]{1,0:T(8,128)(2,1)} %target.1, ...), custom_call_target="tpu_custom_call" | custom-call | tf_op jit(solution)/shard_map/scatter/pallas_call | solution.py:1385
  147.9 3.2 %finish.1 = (f32[512,512]{1,0:T(8,128)}, f32[512,512]{1,0:T(8,128)}, f32[16,512]{1,0:T(8,128)}, f32[16,512]{1,0:T(8,128)}, f32[16,512]{1,0:T(8,128)}, /*index=5*...) custom-call(f32[16,8320]{1,0:T(8,128)} %get-tuple-element.78.rows_re, ...), custom_call_target="tpu_custom_call" | custom-call | tf_op jit(solution)/shard_map/finish/pallas_call | solution.py:1479

commit v7 on v6

--- a/solution.py
+++ b/solution.py
@@ -48,11 +48,11 @@
         n = tiles * 128
         spans.append((at, at + max(1, round(tiles * share)) * 128, at + n))
         at += n
-    assert at == LANES
     return tuple(spans)
 
 
-GATHER_ROUNDS = cuts((17, 48), 0.25)
+GATHER_ROUNDS = cuts((17, 36), 0.22)
+Z_LAST = (53 * 128, 59 * 128, 65 * 128)
 
 
 def gather_kernel(*refs):
@@ -65,7 +65,8 @@
     stage, mem_stage = refs[12:14]
     state, refs = refs[14:26], refs[26:]
     after, a_b, xh1, rs1, num, tot, qs, ks, vs, o_b, gb, low_s = state
-    w, norms, tgt, starts, state_sems = refs
+    w, norms, tgt, starts, state_sems, refs = *refs[:5], refs[5:]
+    cf_sems, cs_sems, cz_sems, co_sems = refs[:2], refs[2:4], refs[4:6], refs[6:8]
     z, x, y, c = here()
     xp, yp, cp_ = device(z, 1 - x, y, c), device(z, x, 1 - y, c), device(z, x, y, 1 - c)
     own = out.at[z, x, y, c]
@@ -191,10 +192,72 @@
                         guarded(cond, lambda s=slot, r=r, p=part, h=hop: second(s, r, p, h, True).wait_recv())
                 go(functools.partial(over, slot, r), cond)
 
+    cut_c = [pl.ds(Z_LAST[p], Z_LAST[p + 1] - Z_LAST[p]) for p in (0, 1)]
+    lanes_c = pl.ds(Z_LAST[0], Z_LAST[2] - Z_LAST[0])
+
+    def first_c(part, arriving=False):
+        if part == 0:
+            ref = out.at[z, (1 - x) if arriving else x, y, c, :, cut_c[0]]
+        else:
+            ref = out.at[z, x, (1 - y) if arriving else y, c, :, cut_c[1]]
+        src = ref if arriving else stage.at[:, cut_c[part]]
+        return remote(src, ref, cf_sems, part, xp if part == 0 else yp)
+
+    def second_c(part, hop, arriving=False):
+        if part == 0:
+            ref = out.at[z, (1 - x) if hop else x, (1 - y) if arriving else y, c, :, cut_c[0]]
+        else:
+            ref = out.at[z, (1 - x) if arriving else x, (1 - y) if hop else y, c, :, cut_c[1]]
+        src = ref if arriving or hop else stage.at[:, cut_c[part]]
+        return remote(src, ref, cs_sems, (part, hop), yp if part == 0 else xp)
+
+    def along_c(slot, up):
+        ref = out.at[column(slot), :, :, c, :, lanes_c]
+        d = 0 if slot == 0 else (slot if slot < 4 else slot - 3)
+        peer = device((z + (1 if up else 3)) % 4, x, y, c)
+        return remote(ref, ref, cz_sems, (0 if up else 1, d), peer)
+
+    def arrived_c(slot):
+        ref = out.at[column(slot), :, :, c, :, lanes_c]
+        up = slot < 4
+        return remote(ref, ref, cz_sems, (0 if up else 1, (slot if up else slot - 3) - 1), xp)
+
+    def over_c(slot, arriving=False):
+        ref = out.at[column(slot), :, :, (1 - c) if arriving else c, :, lanes_c]
+        return remote(ref, ref, co_sems, slot, cp_)
+
+    def pass_on_c():
+        for part in (0, 1):
+            first_c(part, True).wait_recv()
+            go(functools.partial(second_c, part, 1))
+
+    def plane_c():
+        own_out.wait()
+        for part in (0, 1):
+            for hop in (0, 1):
+                second_c(part, hop, True).wait_recv()
+        go(functools.partial(along_c, 0, True), z < 3)
+        go(functools.partial(along_c, 0, False), z > 0)
+        go(functools.partial(over_c, 0))
+
+    def from_z_c(d):
+        for slot in (d, d + 3):
+            cond = there(slot)
+            guarded(cond, lambda slot=slot: arrived_c(slot).wait_recv())
+            if d < 3:
+                onward = z < 3 if slot < 4 else z > 0
+                go(functools.partial(along_c, slot, slot < 4), both(cond, onward))
+            go(functools.partial(over_c, slot), cond)
+
     for r in rounds:
         go(functools.partial(along, 0, r, True), z < 3)
         go(functools.partial(along, 0, r, False), z > 0)
         spread(0, r)
+        if r == 0:
+            for part in (0, 1):
+                go(functools.partial(first_c, part))
+            for part in (0, 1):
+                go(functools.partial(second_c, part, 0))
     mem_own = mem_out.at[y, c]
 
     def memory_rows():
@@ -285,27 +348,31 @@
     loads[0].start()
     prepare()
     from_z(1, 0)
+    pass_on_c()
     from_z(1, 1)
     pass_on((0,), 0)
+    plane_c()
     from_z(2, 0)
     pass_on((0,), 1)
     pass_on((1, 4), 0)
     from_z(3, 0)
     from_z(2, 1)
     pass_on((2, 5), 0)
-    own_out.wait()
     hand_over((0,), 0)
+    from_z_c(1)
     pass_on((1, 4), 1)
     pass_on((3, 6), 0)
     kept = memory_rows()
     hand_over((1, 4), 0)
     hand_over((2, 5), 0)
     from_z(3, 1)
+    from_z_c(2)
     hand_over((3, 6), 0)
     all_over(0)
     loads[1].start()
     loads[2].start()
     pass_on((2, 5), 1)
+    from_z_c(3)
     project()
     hand_over((0,), 1)
     self_tiles(0, 0, 2)
@@ -320,6 +387,8 @@
     for one in saves:
         one.start()
     all_over(1)
+    for slot in everyone:
+        guarded(there(slot), lambda s=slot: over_c(s, True).wait_recv())
     for one in saves:
         one.wait()
     for i, side in ((1, y), (2, 1 - y)):
@@ -356,7 +425,8 @@
             low(*target.shape),
             pltpu.SMEM((16,), jnp.int32),
             dma((15,)),
-        ],
+        ]
+        + both(2) + both(2, 2) + both(2, 3) + both(7),
         compiler_params=pltpu.CompilerParams(
             collective_id=1, has_side_effects=True, vmem_limit_bytes=60 << 20),
         name="gather",
@@ -1094,15 +1164,16 @@
         compiler_params=pltpu.CompilerParams(vmem_limit_bytes=60 << 20),
         name="compute",
     )(lens, spans, offs, out_grad, memory, gathered, after, after_low, gains)
-def scatter_rounds(share=0.25):
+def scatter_rounds(share=0.35):
     spans = []
-    for at, tiles in ((33, 6), (39, 12), (51, 14), (17, 16), (0, 11), (11, 6)):
+    for at, tiles in ((33, 6), (39, 8), (47, 8), (17, 16), (0, 11), (11, 6)):
         split = at + max(1, round(tiles * share))
         spans.append((at * 128, split * 128, (at + tiles) * 128))
     return tuple(spans)
 
 
 SCATTER_ROUNDS = scatter_rounds()
+Z_FIRST = (55 * 128, 60 * 128, 65 * 128)
 SELF_LANES = NORM + 4 * SLAB
 SELF_ROUNDS = (4, 5)
 
@@ -1112,10 +1183,9 @@
     (acc, from_core, from_first, from_second, from_z, macc, mfrom_core, mfrom_y), rest = rest[:8], rest[8:]
     held, rest = rest[:12], rest[12:]
     (w, tgt, gs, dq, dk, dv, dnx, g_b, out, mem_out), rest = rest[:10], rest[10:]
-    target_grad = rest[0]
-    rest = rest[1:]
+    (target_grad, from_zc, from_fc, from_sc), rest = rest[:4], rest[4:]
     (out_sems, own_sems, mown_sem, state_sems, core_s, core_r, first_s, first_r,
-     second_s, second_r, zs_s, zs_r, mem_s, mem_r) = rest
+     second_s, second_r, zs_s, zs_r, mem_s, mem_r, zc_s, zc_r, fc_s, fc_r, sc_s, sc_r) = rest
     dpre, xh1, rs1, num_s, tot_s, qs, ks, vs, o_b, gb, ng, low_s = held
     z, x, y, c = here()
     xp, yp, cp_ = device(z, 1 - x, y, c), device(z, x, 1 - y, c), device(z, x, y, 1 - c)
@@ -1130,7 +1200,7 @@
         sent.append(copy)
 
     def span(r, part=None):
-        a, m, b = SCATTER_ROUNDS[r]
+        a, m, b = Z_FIRST if r == count else SCATTER_ROUNDS[r]
         return {None: (a, b - a), 0: (a, m - a), 1: (m, b - m)}[part]
 
     def own(r):
@@ -1173,7 +1243,7 @@
     early = [r for r in range(count) if r not in SELF_ROUNDS]
     own(0).start()
     mem_own.start()
-    for r in early[1:]:
+    for r in [count] + early[1:]:
         own(r).start()
     copies = [bring(i, src, dst) for i, (src, dst) in enumerate(zip(state, held))]
     copies.append(bring(12, gathered.at[:, :, pl.ds(NORM, 4 * SLAB)], w))
@@ -1181,7 +1251,7 @@
     greet([xp, yp, cp_] + zp)
     go(core(early[0]))
     go(mem_core)
-    for r in early[1:]:
+    for r in [count] + early[1:]:
         go(core(r))
 
     def add_core(r):
@@ -1243,6 +1313,62 @@
             total = total + from_z[k, :, lanes].astype(jnp.float32)
         out[:, lanes] = total
 
+    lanes_c = pl.ds(*span(count))
+    cut_c = [pl.ds(*span(count, part)) for part in (0, 1)]
+    width_c = [span(count, part)[1] for part in (0, 1)]
+
+    def far_c(k):
+        return remote(acc.at[(z + k + 1) % 4, :, :, :, lanes_c], from_zc.at[k], (zc_s, zc_r), k, zp[k])
+
+    def first_c(part):
+        src = acc.at[z, 1 - x, :, :, cut_c[0]] if part == 0 else acc.at[z, :, 1 - y, :, cut_c[1]]
+        return remote(src, from_fc.at[part, :, :, pl.ds(0, width_c[part])], (fc_s, fc_r), part,
+                      xp if part == 0 else yp)
+
+    def second_c(part):
+        src = acc.at[z, x, 1 - y, :, cut_c[0]] if part == 0 else acc.at[z, 1 - x, y, :, cut_c[1]]
+        return remote(src, from_sc.at[part, :, pl.ds(0, width_c[part])], (sc_s, sc_r), part,
+                      yp if part == 0 else xp)
+
+    def add_core_c():
+        own(count).wait()
+        core(count).wait_recv()
+        for k in (0, 2, 1, 3):
+            zi = (z + k + 1) % 4
+            for xi in (0, 1):
+                for yi in (0, 1):
+                    acc[zi, xi, yi, :, lanes_c] = (
+                        acc[zi, xi, yi, :, lanes_c] + from_core[zi, xi, yi, :, lanes_c])
+            if k < 3:
+                go(far_c(k))
+
+    def add_far_c():
+        for k in (0, 2, 1):
+            far_c(k).wait_recv()
+        for xi in (0, 1):
+            for yi in (0, 1):
+                total = acc[z, xi, yi, :, lanes_c].astype(F32)
+                for k in range(3):
+                    total = total + from_zc[k, xi, yi].astype(F32)
+                acc[z, xi, yi, :, lanes_c] = total.astype(LOW)
+        for part in (0, 1):
+            go(first_c(part))
+
+    def add_first_c():
+        for part in (0, 1):
+            first_c(part).wait_recv()
+            for o in (0, 1):
+                xi, yi = (x, o) if part == 0 else (o, y)
+                acc[z, xi, yi, :, cut_c[part]] = (
+                    acc[z, xi, yi, :, cut_c[part]] + from_fc[part, o, :, pl.ds(0, width_c[part])])
+            go(second_c(part))
+
+    def end_c():
+        for part in (0, 1):
+            second_c(part).wait_recv()
+            out[:, cut_c[part]] = (acc[z, x, y, :, cut_c[part]].astype(F32)
+                                   + from_sc[part, :, pl.ds(0, width_c[part])].astype(F32))
+
     def memory_core():
         mem_own.wait()
         mem_core.wait_recv()
@@ -1333,6 +1459,7 @@
 
     add_core(0)
     memory_core()
+    add_core_c()
     add_core(1)
     self_norm()
     add_first(0)
@@ -1348,12 +1475,14 @@
     add_z(0)
     add_second(2)
     add_first(3)
+    add_far_c()
     self_grads()
     add_core(4)
     add_core(5)
     self_target()
     to_target = pltpu.make_async_copy(target_grad, target_ref, out_sems.at[0])
     to_target.start()
+    add_first_c()
     memory_end()
     to_memory = pltpu.make_async_copy(mem_out, mem_ref, out_sems.at[1])
     to_memory.start()
@@ -1364,6 +1493,7 @@
     add_z(2)
     add_second(4)
     add_z(3)
+    end_c()
     add_second(5)
     add_z(4)
     add_z(5)
@@ -1380,6 +1510,7 @@
     dma = pltpu.SemaphoreType.DMA
     n = len(SCATTER_ROUNDS)
     rows = mem_grads.shape[2]
+    wide = Z_FIRST[2] - Z_FIRST[0]
     low = lambda *s: pltpu.VMEM(s, LOW)
     f32 = lambda *s: pltpu.VMEM(s, F32)
     return pl.pallas_call(
@@ -1414,18 +1545,27 @@
             f32(ROWS, LANES),
             f32(rows, SLAB),
             f32(rows, SLAB),
+            low(3, 2, 2, ROWS, wide),
+            low(2, 2, ROWS, wide),
+            low(2, ROWS, wide),
             dma((3,)),
-            dma((n,)),
+            dma((n + 1,)),
             dma(()),
             dma((14,)),
-            dma((n,)),
-            dma((n,)),
+            dma((n + 1,)),
+            dma((n + 1,)),
             dma((n, 2)),
             dma((n, 2)),
             dma((n, 2)),
             dma((n, 2)),
             dma((n, 3)),
             dma((n, 3)),
+            dma((2,)),
+            dma((2,)),
+            dma((3,)),
+            dma((3,)),
+            dma((2,)),
+            dma((2,)),
             dma((2,)),
             dma((2,)),
         ],

time: 151 us -> 148 us (0.980)
  Pallas kernels: 149 us -> 146 us
    pallas_call x1, Pallas kernels: 60 us -> 58.2 us  [scatter_all(): pl.pallas_call(scatter_kernel, out_shape=(jax.ShapeDtypeStruct((ROWS, LAN...]
    pallas_call x1, Pallas kernels: 55.8 us -> 54.2 us  [gather_all(): pl.pallas_call(gather_kernel, out_shape=(jax.ShapeDtypeStruct((4, 2, 2, 2...]
where the time goes in v7:
time: 148 us
  Pallas kernels  146 us (99%)
    pallas_call x1, Pallas kernels, scatter_all(): pl.pallas_call(scatter_kernel, out_shape=(jax.ShapeDtypeStruct((ROWS, LAN...  58.2 us
    pallas_call x1, Pallas kernels, gather_all(): pl.pallas_call(gather_kernel, out_shape=(jax.ShapeDtypeStruct((4, 2, 2, 2...  54.2 us
    pallas_call x1, Pallas kernels, compute(): pl.pallas_call(compute_kernel, out_shape=(jax.ShapeDtypeStruct((rows, SLA...  30 us
    pallas_call x1, Pallas kernels, finish(): pl.pallas_call(finish_kernel, out_shape=(shape(*target.shape), shape(*mem...  3.24 us

profile of v7, /device:TPU:0, one launch (start us, length us, event | category | flops | bytes accessed | tf_op | source)
XLA Modules:
  0.0 147.8 jit_solution(2447496614971390820)
XLA Ops:
  0.7 1.3 pad_add_fusion.refs_10_
  2.0 54.2 %gather.1 = (bf16[4,2,2,2,16,8320]{5,4,3,2,1,0:T(8,128)(2,1)}, bf16[2,2,512,512]{3,2,1,0:T(8,128)(2,1)}, f32[512,512]{1,0:T(8,128)}, bf16[512,512]{1,0:T(8,128)(...) custom-call(bf16[16,512]{1,0:T(8,128)(2,1)} %refs_0_.1, ...), custom_call_target="tpu_custom_call" | custom-call | tf_op jit(solution)/shard_map/gather/pallas_call | solution.py:409
  56.2 30.0 %compute.1 = (bf16[512,512]{1,0:T(8,128)(2,1)}, bf16[32,16,8320]{2,1,0:T(8,128)(2,1)}, bf16[2048,512]{1,0:T(8,128)(2,1)}, f32[512,512]{1,0:T(8,128)}, f32[8,512]{1,0:T(8,128)}) custom-call(s32[1,64]{1,0:T(1,128)} %lens_ref.1, s32[1,64]{1,0:T(1,128)} %spans_ref.1, s32[1,64]{1,0:T(1,128)} %offs_ref.1, bf16[512,512]{1,0:T(8,128)(2,1)} %out_grad.1, ...), custom_call_target="tpu_custom_call" | custom-call | tf_op jit(solution)/shard_map/compute/pallas_call | solution.py:1115
  86.2 58.2 %scatter.1 = (f32[16,8320]{1,0:T(8,128)}, f32[512,512]{1,0:T(8,128)}, f32[512,512]{1,0:T(8,128)}) custom-call(bf16[4,2,2,2,16,8320]{5,4,3,2,1,0:T(8,128)(2,1)} %bitcast.12, bf16[2,2,512,512]{3,2,1,0:T(8,128)(2,1)} %bitcast.13, bf16[32,16,8320]{2,1,0:T(8,128)(2,1)} %bitcast.11, bf16[512,512]{1,0:T(8,128)(2,1)} %target.1, ...), custom_call_target="tpu_custom_call" | custom-call | tf_op jit(solution)/shard_map/scatter/pallas_call | solution.py:1516
  144.4 3.2 %finish.1 = (f32[512,512]{1,0:T(8,128)}, f32[512,512]{1,0:T(8,128)}, f32[16,512]{1,0:T(8,128)}, f32[16,512]{1,0:T(8,128)}, f32[16,512]{1,0:T(8,128)}, /*index=5*...) custom-call(f32[16,8320]{1,0:T(8,128)} %get-tuple-element.78.rows_re, ...), custom_call_target="tpu_custom_call" | custom-call | tf_op jit(solution)/shard_map/finish/pallas_call | solution.py:1619

commit v8 on v7

--- a/solution.py
+++ b/solution.py
@@ -56,16 +56,17 @@
 
 
 def gather_kernel(*refs):
-    shards, norm_ref, memory_ref, lens_ref, target = refs[:10], *refs[10:14]
-    out, mem_out = refs[14:16]
-    state_out, refs = refs[16:28], refs[28:]
+    shards, memory_ref, lens_ref, target = refs[:10], *refs[10:13]
+    params, refs = refs[13:19], refs[19:]
+    out, mem_out = refs[:2]
+    state_out, refs = refs[2:14], refs[14:]
     local_sem, mem_local = refs[:2]
     z_sems, first_sems, second_sems = refs[2:4], refs[4:6], refs[6:8]
     across, mems = refs[8:10], refs[10:12]
     stage, mem_stage = refs[12:14]
     state, refs = refs[14:26], refs[26:]
     after, a_b, xh1, rs1, num, tot, qs, ks, vs, o_b, gb, low_s = state
-    w, norms, tgt, starts, state_sems, refs = *refs[:5], refs[5:]
+    w, norms, tgt, starts, state_sems, rows, refs = *refs[:6], refs[6:]
     cf_sems, cs_sems, cz_sems, co_sems = refs[:2], refs[2:4], refs[4:6], refs[6:8]
     z, x, y, c = here()
     xp, yp, cp_ = device(z, 1 - x, y, c), device(z, x, 1 - y, c), device(z, x, y, 1 - c)
@@ -79,7 +80,6 @@
             pltpu.make_async_copy(src, stage.at[:, pl.ds(start, width)], local_sem.at[len(local)])
         )
 
-    bring(norm_ref, 0, NORM)
     for i in range(8):
         bring(shards[i], NORM + SLAB * i, SLAB)
     bring(shards[8], NORM + SLAB * 8, 4 * SLAB)
@@ -90,6 +90,10 @@
     keep = pltpu.make_async_copy(memory_ref, mem_stage, mem_local.at[0])
     keep.start()
     zn = [device((z + k) % 4, x, y, c) for k in (1, 3)]
+    rows[...] = jnp.zeros_like(rows)
+    for i, one in enumerate(params):
+        rows[i : i + 1, :ROWS] = one[...].astype(F32)
+    stage[:, :NORM] = rows[...].astype(LOW)
     greet([xp, yp, cp_] + zn)
     for one in local:
         one.wait()
@@ -399,7 +403,7 @@
         guarded(cond, lambda make=make: make().wait_send())
 
 
-def gather_all(shards, norms, memory, lens, target):
+def gather_all(shards, params, memory, lens, target):
     any_space = pl.BlockSpec(memory_space=pl.ANY)
     dma = pltpu.SemaphoreType.DMA
     n = len(GATHER_ROUNDS)
@@ -413,7 +417,9 @@
             jax.ShapeDtypeStruct((2, 2) + memory.shape, jnp.bfloat16),
         )
         + state,
-        in_specs=[any_space] * 12 + [pl.BlockSpec(memory_space=pltpu.SMEM), any_space],
+        in_specs=[any_space] * 11
+        + [pl.BlockSpec(memory_space=pltpu.SMEM), any_space]
+        + [pl.BlockSpec(memory_space=pltpu.VMEM)] * 6,
         out_specs=(any_space,) * 14,
         scratch_shapes=[dma((14,)), dma((3,))]
         + both(2, 3, n) + both(7, 2, n) + both(7, 2, 2, n) + both(7, n) + both(3)
@@ -425,12 +431,13 @@
             low(*target.shape),
             pltpu.SMEM((16,), jnp.int32),
             dma((15,)),
+            pltpu.VMEM((ROWS, NORM), F32),
         ]
         + both(2) + both(2, 2) + both(2, 3) + both(7),
         compiler_params=pltpu.CompilerParams(
             collective_id=1, has_side_effects=True, vmem_limit_bytes=60 << 20),
         name="gather",
-    )(*shards, norms, memory, lens, target)
+    )(*shards, memory, lens, target, *[p[None, :] for p in params])
     return gathered.reshape(32, ROWS, LANES), whole_memory.reshape(-1, SLAB), saved
 
 
@@ -626,6 +633,7 @@
 
 TILE = 128
 RT = 256
+RC = 512
 CHUNK = 256
 EPS = 1e-05
 HIDE = -1e30
@@ -877,18 +885,18 @@
     def tiles(body, bias, first, last):
         def outer(i, carry):
             def inner(kt, carry):
-                body(block(i, RT), block(kt), bias(i, kt))
+                body(block(i, RC), block(kt), bias(i, kt))
                 return carry
             return lax.fori_loop(first(i) // TILE, (last(i) - 1) // TILE + 1, inner, carry)
-        lax.fori_loop(0, rows_all // RT, outer, 0)
+        lax.fori_loop(0, rows_all // RC, outer, 0)
 
     def cross_tiles(body):
         def bias(i, kt):
-            key = kt * TILE + lane_iota((RT, TILE))
-            r = block(i, RT)
+            key = kt * TILE + lane_iota((RC, TILE))
+            r = block(i, RC)
             return jnp.where((key >= low_c[r]) & (key < high_c[r]), 0.0, HIDE)
-        tiles(body, bias, lambda i: last_at(lambda j: packed[j], i * RT),
-              lambda i: last_at(lambda j: packed[j + 1], (i + 1) * RT - 1))
+        tiles(body, bias, lambda i: last_at(lambda j: packed[j], i * RC),
+              lambda i: last_at(lambda j: packed[j + 1], (i + 1) * RC - 1))
 
     loads["a"].wait()
     loads[4].wait()
@@ -1640,11 +1648,9 @@
     if not fast:
         return plain(target_in, memory, out_grad, *rest)
     weights, tables = rest[:16], rest[16:]
-    norms = sum(
-        jnp.pad(one[None, :], ((i, ROWS - 1 - i), (0, NORM - ROWS)))
-        for i, one in enumerate(weights[10:])
+    gathered, all_memory, saved = gather_all(
+        weights[:10], weights[10:], memory, tables[0], target_in
     )
-    gathered, all_memory, saved = gather_all(weights[:10], norms, memory, tables[0], target_in)
     after, after_low, xh1, rs1, num, tot, q, k, v, o, gains, low_s = saved
     layer_out, grads, mem_grads, d_after, norm_grads = compute(
         *tables, out_grad, all_memory, gathered, after, after_low, gains

time: 148 us -> 144 us (0.973)
  Pallas kernels: 146 us -> 143 us
    pallas_call x1, Pallas kernels: 30 us -> 26.9 us  [compute(): pl.pallas_call(compute_kernel, out_shape=(jax.ShapeDtypeStruct((rows, SLA...]
where the time goes in v8:
time: 144 us
  Pallas kernels  143 us (99%)
    pallas_call x1, Pallas kernels, scatter_all(): pl.pallas_call(scatter_kernel, out_shape=(jax.ShapeDtypeStruct((ROWS, LAN...  58.2 us
    pallas_call x1, Pallas kernels, gather_all(): pl.pallas_call(gather_kernel, out_shape=(jax.ShapeDtypeStruct((4, 2, 2, 2...  54.4 us
    pallas_call x1, Pallas kernels, compute(): pl.pallas_call(compute_kernel, out_shape=(jax.ShapeDtypeStruct((rows, SLA...  26.9 us
    pallas_call x1, Pallas kernels, finish(): pl.pallas_call(finish_kernel, out_shape=(shape(*target.shape), shape(*mem...  3.24 us

profile of v8, /device:TPU:0, one launch (start us, length us, event | category | flops | bytes accessed | tf_op | source)
XLA Modules:
  0.0 143.7 jit_solution(4538132294567648769)
XLA Ops:
  0.7 54.4 %gather.1 = (bf16[4,2,2,2,16,8320]{5,4,3,2,1,0:T(8,128)(2,1)}, bf16[2,2,512,512]{3,2,1,0:T(8,128)(2,1)}, f32[512,512]{1,0:T(8,128)}, bf16[512,512]{1,0:T(8,128)(...) custom-call(bf16[16,512]{1,0:T(8,128)(2,1)} %refs_0_.1, ...), custom_call_target="tpu_custom_call" | custom-call | tf_op jit(solution)/shard_map/gather/pallas_call | solution.py:413
  55.1 26.9 %compute.1 = (bf16[512,512]{1,0:T(8,128)(2,1)}, bf16[32,16,8320]{2,1,0:T(8,128)(2,1)}, bf16[2048,512]{1,0:T(8,128)(2,1)}, f32[512,512]{1,0:T(8,128)}, f32[8,512]{1,0:T(8,128)}) custom-call(s32[1,64]{1,0:T(1,128)} %lens_ref.1, s32[1,64]{1,0:T(1,128)} %spans_ref.1, s32[1,64]{1,0:T(1,128)} %offs_ref.1, bf16[512,512]{1,0:T(8,128)(2,1)} %out_grad.1, ...), custom_call_target="tpu_custom_call" | custom-call | tf_op jit(solution)/shard_map/compute/pallas_call | solution.py:1123
  82.0 58.2 %scatter.1 = (f32[16,8320]{1,0:T(8,128)}, f32[512,512]{1,0:T(8,128)}, f32[512,512]{1,0:T(8,128)}) custom-call(bf16[4,2,2,2,16,8320]{5,4,3,2,1,0:T(8,128)(2,1)} %bitcast.12, bf16[2,2,512,512]{3,2,1,0:T(8,128)(2,1)} %bitcast.13, bf16[32,16,8320]{2,1,0:T(8,128)(2,1)} %bitcast.11, bf16[512,512]{1,0:T(8,128)(2,1)} %target.1, ...), custom_call_target="tpu_custom_call" | custom-call | tf_op jit(solution)/shard_map/scatter/pallas_call | solution.py:1524
  140.2 3.2 %finish.1 = (f32[512,512]{1,0:T(8,128)}, f32[512,512]{1,0:T(8,128)}, f32[16,512]{1,0:T(8,128)}, f32[16,512]{1,0:T(8,128)}, f32[16,512]{1,0:T(8,128)}, /*index=5*...) custom-call(f32[16,8320]{1,0:T(8,128)} %get-tuple-element.78.rows_re, ...), custom_call_target="tpu_custom_call" | custom-call | tf_op jit(solution)/shard_map/finish/pallas_call | solution.py:1627

commit v9 on v8

--- a/solution.py
+++ b/solution.py
@@ -1172,16 +1172,16 @@
         compiler_params=pltpu.CompilerParams(vmem_limit_bytes=60 << 20),
         name="compute",
     )(lens, spans, offs, out_grad, memory, gathered, after, after_low, gains)
-def scatter_rounds(share=0.35):
+def scatter_rounds(share=0.42):
     spans = []
-    for at, tiles in ((33, 6), (39, 8), (47, 8), (17, 16), (0, 11), (11, 6)):
+    for at, tiles in ((33, 6), (39, 7), (46, 7), (17, 16), (0, 11), (11, 6)):
         split = at + max(1, round(tiles * share))
         spans.append((at * 128, split * 128, (at + tiles) * 128))
     return tuple(spans)
 
 
 SCATTER_ROUNDS = scatter_rounds()
-Z_FIRST = (55 * 128, 60 * 128, 65 * 128)
+Z_FIRST = (53 * 128, 59 * 128, 65 * 128)
 SELF_LANES = NORM + 4 * SLAB
 SELF_ROUNDS = (4, 5)
 

time: 144 us -> 142 us (0.986)
  Pallas kernels: 143 us -> 141 us
    pallas_call x1, Pallas kernels: 58.2 us -> 56.7 us  [scatter_all(): pl.pallas_call(scatter_kernel, out_shape=(jax.ShapeDtypeStruct((ROWS, LAN...]
where the time goes in v9:
time: 142 us
  Pallas kernels  141 us (99%)
    pallas_call x1, Pallas kernels, scatter_all(): pl.pallas_call(scatter_kernel, out_shape=(jax.ShapeDtypeStruct((ROWS, LAN...  56.7 us
    pallas_call x1, Pallas kernels, gather_all(): pl.pallas_call(gather_kernel, out_shape=(jax.ShapeDtypeStruct((4, 2, 2, 2...  54.4 us
    pallas_call x1, Pallas kernels, compute(): pl.pallas_call(compute_kernel, out_shape=(jax.ShapeDtypeStruct((rows, SLA...  26.9 us
    pallas_call x1, Pallas kernels, finish(): pl.pallas_call(finish_kernel, out_shape=(shape(*target.shape), shape(*mem...  3.24 us

profile of v9, /device:TPU:0, one launch (start us, length us, event | category | flops | bytes accessed | tf_op | source)
XLA Modules:
  0.0 142.2 jit_solution(12546758586850372836)
XLA Ops:
  0.7 54.4 %gather.1 = (bf16[4,2,2,2,16,8320]{5,4,3,2,1,0:T(8,128)(2,1)}, bf16[2,2,512,512]{3,2,1,0:T(8,128)(2,1)}, f32[512,512]{1,0:T(8,128)}, bf16[512,512]{1,0:T(8,128)(...) custom-call(bf16[16,512]{1,0:T(8,128)(2,1)} %refs_0_.1, ...), custom_call_target="tpu_custom_call" | custom-call | tf_op jit(solution)/shard_map/gather/pallas_call | solution.py:413
  55.1 26.9 %compute.1 = (bf16[512,512]{1,0:T(8,128)(2,1)}, bf16[32,16,8320]{2,1,0:T(8,128)(2,1)}, bf16[2048,512]{1,0:T(8,128)(2,1)}, f32[512,512]{1,0:T(8,128)}, f32[8,512]{1,0:T(8,128)}) custom-call(s32[1,64]{1,0:T(1,128)} %lens_ref.1, s32[1,64]{1,0:T(1,128)} %spans_ref.1, s32[1,64]{1,0:T(1,128)} %offs_ref.1, bf16[512,512]{1,0:T(8,128)(2,1)} %out_grad.1, ...), custom_call_target="tpu_custom_call" | custom-call | tf_op jit(solution)/shard_map/compute/pallas_call | solution.py:1123
  82.0 56.7 %scatter.1 = (f32[16,8320]{1,0:T(8,128)}, f32[512,512]{1,0:T(8,128)}, f32[512,512]{1,0:T(8,128)}) custom-call(bf16[4,2,2,2,16,8320]{5,4,3,2,1,0:T(8,128)(2,1)} %bitcast.12, bf16[2,2,512,512]{3,2,1,0:T(8,128)(2,1)} %bitcast.13, bf16[32,16,8320]{2,1,0:T(8,128)(2,1)} %bitcast.11, bf16[512,512]{1,0:T(8,128)(2,1)} %target.1, ...), custom_call_target="tpu_custom_call" | custom-call | tf_op jit(solution)/shard_map/scatter/pallas_call | solution.py:1524
  138.8 3.2 %finish.1 = (f32[512,512]{1,0:T(8,128)}, f32[512,512]{1,0:T(8,128)}, f32[16,512]{1,0:T(8,128)}, f32[16,512]{1,0:T(8,128)}, f32[16,512]{1,0:T(8,128)}, /*index=5*...) custom-call(f32[16,8320]{1,0:T(8,128)} %get-tuple-element.78.rows_re, ...), custom_call_target="tpu_custom_call" | custom-call | tf_op jit(solution)/shard_map/finish/pallas_call | solution.py:1627

commit v10 on v9

--- a/solution.py
+++ b/solution.py
@@ -326,9 +326,9 @@
 
     def self_tiles(i, first_tile, last_tile):
         def inner(kt, carry):
-            r = pl.ds(i * RT, RT)
-            key = kt * TILE + lane_iota((RT, TILE))
-            row = i * RT + row_iota((RT, TILE))
+            r = pl.ds(i * RC, RC)
+            key = kt * TILE + lane_iota((RC, TILE))
+            row = i * RC + row_iota((RC, TILE))
             bias = jnp.where((key >= low_s[r]) & (key <= row), 0.0, HIDE)
             tile_forward(r, block(kt), bias, qs, ks, vs, num, tot)
             return carry
@@ -381,7 +381,7 @@
     hand_over((0,), 1)
     self_tiles(0, 0, 2)
     pass_on((3, 6), 1)
-    self_tiles(1, 0, 4)
+    self_tiles(0, 2, 4)
     hand_over((1, 4), 1)
     memory_far()
     project_out()
@@ -1432,9 +1432,9 @@
 
     def self_tiles(i, first, last):
         def inner(kt, carry):
-            r = pl.ds(i * RT, RT)
-            key = kt * TILE + lane_iota((RT, TILE))
-            row = i * RT + row_iota((RT, TILE))
+            r = pl.ds(i * RC, RC)
+            key = kt * TILE + lane_iota((RC, TILE))
+            row = i * RC + row_iota((RC, TILE))
             bias = jnp.where((key >= low_s[r]) & (key <= row), 0.0, HIDE)
             tile_backward(r, block(kt), bias, qs, ks, vs, dnx, dq, dk, dv)
             return carry
@@ -1479,7 +1479,7 @@
     self_tiles(0, 0, 2)
     add_second(1)
     add_first(2)
-    self_tiles(1, 0, 4)
+    self_tiles(0, 2, 4)
     add_z(0)
     add_second(2)
     add_first(3)

time: 142 us -> 142 us (level)
  no operation moved by 1% of the time
where the time goes in v10:
time: 142 us; the launch traced here: 141 us
  Pallas kernels  140 us (99%)
    pallas_call x1, Pallas kernels, scatter_all(): pl.pallas_call(scatter_kernel, out_shape=(jax.ShapeDtypeStruct((ROWS, LAN...  56.1 us
    pallas_call x1, Pallas kernels, gather_all(): pl.pallas_call(gather_kernel, out_shape=(jax.ShapeDtypeStruct((4, 2, 2, 2...  54.2 us
    pallas_call x1, Pallas kernels, compute(): pl.pallas_call(compute_kernel, out_shape=(jax.ShapeDtypeStruct((rows, SLA...  26.9 us
    pallas_call x1, Pallas kernels, finish(): pl.pallas_call(finish_kernel, out_shape=(shape(*target.shape), shape(*mem...  3.24 us

profile of v10, /device:TPU:0, one launch (start us, length us, event | category | flops | bytes accessed | tf_op | source)
XLA Modules:
  0.0 141.3 jit_solution(13853552133257512218)
XLA Ops:
  0.7 54.2 %gather.1 = (bf16[4,2,2,2,16,8320]{5,4,3,2,1,0:T(8,128)(2,1)}, bf16[2,2,512,512]{3,2,1,0:T(8,128)(2,1)}, f32[512,512]{1,0:T(8,128)}, bf16[512,512]{1,0:T(8,128)(...) custom-call(bf16[16,512]{1,0:T(8,128)(2,1)} %refs_0_.1, ...), custom_call_target="tpu_custom_call" | custom-call | tf_op jit(solution)/shard_map/gather/pallas_call | solution.py:413
  54.9 26.9 %compute.1 = (bf16[512,512]{1,0:T(8,128)(2,1)}, bf16[32,16,8320]{2,1,0:T(8,128)(2,1)}, bf16[2048,512]{1,0:T(8,128)(2,1)}, f32[512,512]{1,0:T(8,128)}, f32[8,512]{1,0:T(8,128)}) custom-call(s32[1,64]{1,0:T(1,128)} %lens_ref.1, s32[1,64]{1,0:T(1,128)} %spans_ref.1, s32[1,64]{1,0:T(1,128)} %offs_ref.1, bf16[512,512]{1,0:T(8,128)(2,1)} %out_grad.1, ...), custom_call_target="tpu_custom_call" | custom-call | tf_op jit(solution)/shard_map/compute/pallas_call | solution.py:1123
  81.8 56.1 %scatter.1 = (f32[16,8320]{1,0:T(8,128)}, f32[512,512]{1,0:T(8,128)}, f32[512,512]{1,0:T(8,128)}) custom-call(bf16[4,2,2,2,16,8320]{5,4,3,2,1,0:T(8,128)(2,1)} %bitcast.12, bf16[2,2,512,512]{3,2,1,0:T(8,128)(2,1)} %bitcast.13, bf16[32,16,8320]{2,1,0:T(8,128)(2,1)} %bitcast.11, bf16[512,512]{1,0:T(8,128)(2,1)} %target.1, ...), custom_call_target="tpu_custom_call" | custom-call | tf_op jit(solution)/shard_map/scatter/pallas_call | solution.py:1524
  137.9 3.2 %finish.1 = (f32[512,512]{1,0:T(8,128)}, f32[512,512]{1,0:T(8,128)}, f32[16,512]{1,0:T(8,128)}, f32[16,512]{1,0:T(8,128)}, f32[16,512]{1,0:T(8,128)}, /*index=5*...) custom-call(f32[16,8320]{1,0:T(8,128)} %get-tuple-element.78.rows_re, ...), custom_call_target="tpu_custom_call" | custom-call | tf_op jit(solution)/shard_map/finish/pallas_call | solution.py:1627
